TPU v7x, 256 devices: a whole 4x4x8 slice. The times are simulated.
256 devices in a mesh: aux: 32 (over y_hi, z, core), vir: 8 (over x, y_lo).
Axes of the slice: x: 4, y: 4 (y_hi: 2, y_lo: 2; y = y_hi * 2 + y_lo), z: 8, core: 2. Of those that a mesh axis runs over, the one named last changes fastest.
Arguments:
- b_ov: bfloat16 [128, 2048, 512], P('aux', 'vir'), may hold values from -0.00390625 to 0.00390625
- b_vv: bfloat16 [128, 2048, 2048], P('aux', 'vir'), may hold values from -0.125 to 0.125
- b_oo: bfloat16 [128, 512, 512], P('aux'), may hold values from -0.03125 to 0.03125
- rhs: float32 [2048, 512], P('vir'), may hold values from -6 to 6
- fit_pert: float32 [128], P('aux'), may hold values from -6 to 6
- eps_vir: float32 [2048], P('vir'), may hold values from 1 to 3
- eps_occ: float32 [512], replicated, may hold values from -2 to -1
Outputs:
- response: float32 [2048, 512], P('vir')
All inputs are finite; a program needn't handle non-finite values.
Results may differ from a plain program's by a relative error of at most 0.006.
Values may be sent and summed in bfloat16 or wider, within the bound.
No kernel may reach another device: no remote copies, remote signals or barrier semaphores. Data moves between devices by JAX's collectives and lax.ppermute only.
A program may use at most 64 MiB of HBM per device.

v0:
```python
import functools
import math

import jax
import jax.numpy as jnp
from jax import lax
from jax.sharding import Mesh
from jax.sharding import PartitionSpec as P

V = 2048
O = 512
ITERS = 3
VIR = ("vir_0", "vir_1")


def by_axis(value, axes):
    return functools.reduce(lax.psum, axes, value)


def whole_of(value, axes, dim):
    out = value
    for number in range(len(axes) - 1, -1, -1):
        out = lax.all_gather(out, axes[number], axis=dim, tiled=True)
    return out


def cut_along(value, dim, length):
    before, after = (value.shape[:dim], value.shape[dim + 1 :])
    return jnp.moveaxis(value.reshape(*before, length, -1, *after), dim, 0)


def summed_on_arrival(value, axis, dim):
    pieces = cut_along(value, dim, lax.axis_size(axis))
    arrived = lax.all_to_all(pieces, axis, split_axis=0, concat_axis=0, tiled=True)
    return arrived.sum(axis=0)


def laid_out(pieces, dim):
    dims = list(pieces.shape[1:])
    dims[dim] *= pieces.shape[0]
    return jnp.moveaxis(pieces, 0, dim).reshape(dims)


def sent_to_all(value, axis):
    length = lax.axis_size(axis)
    return lax.all_to_all(
        jnp.broadcast_to(value[None], (length, *value.shape)), axis, 0, 0, tiled=True
    )


def gathered_copies(value, axis, dim):
    return laid_out(sent_to_all(value, axis), dim)


def local(b_ov, b_vv, b_oo, rhs, fit_pert, eps_vir, eps_occ):
    aux_local = b_ov.shape[0]
    occ_count = b_ov.shape[2]
    aux_total = aux_local * lax.axis_size("aux")
    scale = math.sqrt(4.0 * V * O / aux_total)
    denom = eps_vir[:, None] - eps_occ[None, :]
    current = (rhs / denom).astype(jnp.bfloat16)
    result = rhs
    for step in range(ITERS):
        local_fit = jnp.einsum("qbj,bj->q", b_ov, current, preferred_element_type=jnp.float32)
        fitted = by_axis(local_fit, VIR)
        weight = scale * fit_pert - 4.0 * fitted
        mixed = jnp.einsum(
            "qab,bj->qaj", b_vv, whole_of(current, VIR, 0), preferred_element_type=jnp.float32
        )
        mixed_half = mixed.astype(jnp.bfloat16)
        partial_value = jnp.einsum(
            "qaj,qji->ai", mixed_half, b_oo, preferred_element_type=jnp.float32
        )
        partial_value = partial_value + jnp.einsum("qai,q->ai", b_ov, weight)
        share = summed_on_arrival(partial_value, "aux", 1)
        width = occ_count // lax.axis_size("aux")
        begin = lax.axis_index("aux") * width
        rhs_part = lax.dynamic_slice_in_dim(rhs, begin, width, 1)
        denom_part = lax.dynamic_slice_in_dim(denom, begin, width, 1)
        updated = (rhs_part + share) / denom_part
        if step < ITERS - 1:
            current = gathered_copies(updated.astype(jnp.bfloat16), "aux", 1)
        else:
            result = gathered_copies(updated, "aux", 1)
    return result


def solution(mesh):
    split = Mesh(mesh.devices.reshape(mesh.shape["aux"], 4, 2), ("aux", "vir_0", "vir_1"))
    placed = (
        P("aux", VIR, None),
        P("aux", VIR, None),
        P("aux", None, None),
        P(VIR, None),
        P("aux"),
        P(VIR),
        P(),
    )
    return jax.shard_map(
        local, mesh=split, in_specs=placed, out_specs=P(VIR, None), check_vma=False
    )
```

profile of v0, /device:TPU:1, one launch (start us, length us, event | category | flops | bytes accessed | tf_op | source)
XLA Modules:
  0.0 304.3 jit_solution(3499290747826682595)
XLA Ops:
  6.5 1.4 copy.15
  7.9 1.6 broadcast_subtract_fusion
  9.6 7.6 %all_gather.18 = bf16[512,512]{0,1:T(8,128)(2,1)} all-gather(bf16[256,512]{0,1:T(8,128)(2,1)S(1)} %get-tuple-element.6), channel_id=1, replica_groups=mesh['aux'=32,'vir_0'=4,'vir_1'=2] {'vir_1'}, dimensions={0}, use_global_device_ids=true | all-gather | bytes 786432 | tf_op jit(solution)/shard_map/all_gather | solution.py:23
  17.7 2.0 copy.26
  20.7 1.9 convolution_bitcast_fusion.5
  22.6 9.6 %psum.42 = f32[4]{0:T(128)S(1)} all-reduce(f32[4]{0:T(128)S(1)} %convolution_bitcast_fusion.5), channel_id=1, replica_groups=mesh['aux'=32,'vir_0'=4,'vir_1'=2] {'vir_0'}, use_global_device_ids=true, to_apply=%region_0.0 | all-reduce | flops 4 | bytes 32 | tf_op jit(solution)/shard_map/psum | solution.py:17
  32.2 3.8 %psum.43 = f32[4]{0:T(128)S(1)} all-reduce(f32[4]{0:T(128)S(1)} %psum.42), channel_id=1, replica_groups=mesh['aux'=32,'vir_0'=4,'vir_1'=2] {'vir_1'}, use_global_device_ids=true, to_apply=%region_1.0 | all-reduce | flops 4 | bytes 32 | tf_op jit(solution)/shard_map/psum | solution.py:17
  35.9 2.7 fusion.33
  38.7 16.8 %all-gather.4.cloned.1.call-done = bf16[2048,512]{0,1:T(8,128)(2,1)} async-done(((bf16[512,512]{0,1:T(8,128)(2,1)}), bf16[2048,512]{0,1:T(8,128)(2,1)}) %all-gather.4.cloned.1.call-update) | async-done | bytes 2097168 | tf_op jit(solution)/shard_map/all_gather | solution.py:23
  55.5 5.8 %fusion.24 = f32[256,512]{1,0:T(8,128)S(1)} fusion(bf16[4,512,512]{2,1,0:T(8,128)(2,1)S(1)} %copy-done, bf16[4,256,2048]{2,1,0:T(8,128)(2,1)} %param.8, bf16[2048,512]{0,1:T(8,128)(2,1)} %all-gather.4.cloned.1.call-done, f32[1,256,512]{2,0,1:T(1,128)} %fusion.33), kind=kOutput, calls=%fused_computation.15 | convolution fusion | flops 2685009920 | bytes 9437184 | tf_op jit(solution)/shard_map/qaj,qji->ai/dot_general | solution.py:71
  62.3 10.5 %all-to-all-start = ((f32[32,256,16]{1,2,0:T(8,128)}), f32[32,256,16]{1,2,0:T(8,128)S(1)}, u32[]{:S(2)}, u32[]{:S(2)}) async-start(f32[32,256,16]{1,2,0:T(8,128)} %bitcast.115), calls=%async_computation | async-start | bytes 1048576 | tf_op jit(solution)/shard_map/all_to_all | solution.py:34
  72.8 18.0 %all-to-all-done = f32[32,256,16]{1,2,0:T(8,128)S(1)} async-done(((f32[32,256,16]{1,2,0:T(8,128)}), f32[32,256,16]{1,2,0:T(8,128)S(1)}, u32[]{:S(2)}, u32[]{:S(2)}) %all-to-all-start) | async-done | bytes 524320 | tf_op jit(solution)/shard_map/all_to_all | solution.py:34
  91.6 18.1 %all_to_all.30 = bf16[32,256,16]{1,2,0:T(8,128)(2,1)S(1)} all-to-all(bf16[32,256,16]{1,2,0:T(8,128)(2,1)S(1)} %broadcast_in_dim.6), channel_id=1, replica_groups=mesh['aux'=32,'vir_0'=4,'vir_1'=2] {'aux'}, dimensions={0} | all-to-all | bytes 524288 | tf_op jit(solution)/shard_map/all_to_all | solution.py:46
  109.8 7.0 %all_gather.20 = bf16[512,512]{0,1:T(8,128)(2,1)} all-gather(bf16[256,512]{0,1:T(8,128)(2,1)S(1)} %bitcast.110), channel_id=1, replica_groups=mesh['aux'=32,'vir_0'=4,'vir_1'=2] {'vir_1'}, dimensions={0}, use_global_device_ids=true | all-gather | bytes 786432 | tf_op jit(solution)/shard_map/all_gather | solution.py:23
  117.3 3.0 convolution_bitcast_fusion.4
  120.3 6.5 %psum.44 = f32[4]{0:T(128)S(1)} all-reduce(f32[4]{0:T(128)S(1)} %convolution_bitcast_fusion.4), channel_id=1, replica_groups=mesh['aux'=32,'vir_0'=4,'vir_1'=2] {'vir_0'}, use_global_device_ids=true, to_apply=%region_3.0 | all-reduce | flops 4 | bytes 32 | tf_op jit(solution)/shard_map/psum | solution.py:17
  126.9 4.3 %psum.45 = f32[4]{0:T(128)S(1)} all-reduce(f32[4]{0:T(128)S(1)} %psum.44), channel_id=1, replica_groups=mesh['aux'=32,'vir_0'=4,'vir_1'=2] {'vir_1'}, use_global_device_ids=true, to_apply=%region_4.0 | all-reduce | flops 4 | bytes 32 | tf_op jit(solution)/shard_map/psum | solution.py:17
  131.2 1.9 fusion.34
  133.1 12.5 %all-gather.6.cloned.1.call-done = bf16[2048,512]{0,1:T(8,128)(2,1)} async-done(((bf16[512,512]{0,1:T(8,128)(2,1)}), bf16[2048,512]{0,1:T(8,128)(2,1)}) %all-gather.6.cloned.1.call-update) | async-done | bytes 2097168 | tf_op jit(solution)/shard_map/all_gather | solution.py:23
  145.7 6.5 %fusion.25 = f32[256,512]{1,0:T(8,128)} fusion(bf16[4,512,512]{2,1,0:T(8,128)(2,1)S(1)} %copy-done, bf16[4,256,2048]{2,1,0:T(8,128)(2,1)} %param.8, bf16[2048,512]{0,1:T(8,128)(2,1)} %all-gather.6.cloned.1.call-done, f32[1,256,512]{2,0,1:T(1,128)S(1)} %fusion.34), kind=kOutput, calls=%fused_computation.16 | convolution fusion | flops 2685009920 | bytes 9437184 | tf_op jit(solution)/shard_map/qaj,qji->ai/dot_general | solution.py:71
  152.2 1.2 copy.20
  153.4 28.4 %all_to_all.31 = f32[32,256,16]{1,2,0:T(8,128)} all-to-all(f32[32,256,16]{1,2,0:T(8,128)S(1)} %bitcast.116), channel_id=1, replica_groups=mesh['aux'=32,'vir_0'=4,'vir_1'=2] {'aux'}, dimensions={0} | all-to-all | bytes 1048576 | tf_op jit(solution)/shard_map/all_to_all | solution.py:34
  183.7 18.1 %all_to_all.32 = bf16[32,256,16]{1,2,0:T(8,128)(2,1)S(1)} all-to-all(bf16[32,256,16]{1,2,0:T(8,128)(2,1)S(1)} %broadcast_in_dim.7), channel_id=1, replica_groups=mesh['aux'=32,'vir_0'=4,'vir_1'=2] {'aux'}, dimensions={0} | all-to-all | bytes 524288 | tf_op jit(solution)/shard_map/all_to_all | solution.py:46
  201.8 7.0 %all_gather.22 = bf16[512,512]{0,1:T(8,128)(2,1)} all-gather(bf16[256,512]{0,1:T(8,128)(2,1)S(1)} %bitcast.112), channel_id=1, replica_groups=mesh['aux'=32,'vir_0'=4,'vir_1'=2] {'vir_1'}, dimensions={0}, use_global_device_ids=true | all-gather | bytes 786432 | tf_op jit(solution)/shard_map/all_gather | solution.py:23
  209.3 3.0 convolution_bitcast_fusion.3
  212.3 6.5 %psum.46 = f32[4]{0:T(128)S(1)} all-reduce(f32[4]{0:T(128)S(1)} %convolution_bitcast_fusion.3), channel_id=1, replica_groups=mesh['aux'=32,'vir_0'=4,'vir_1'=2] {'vir_0'}, use_global_device_ids=true, to_apply=%region_6.0 | all-reduce | flops 4 | bytes 32 | tf_op jit(solution)/shard_map/psum | solution.py:17
  218.9 4.2 %psum.47 = f32[4]{0:T(128)S(1)} all-reduce(f32[4]{0:T(128)S(1)} %psum.46), channel_id=1, replica_groups=mesh['aux'=32,'vir_0'=4,'vir_1'=2] {'vir_1'}, use_global_device_ids=true, to_apply=%region_7.0 | all-reduce | flops 4 | bytes 32 | tf_op jit(solution)/shard_map/psum | solution.py:17
  223.1 2.7 fusion.35
  225.8 12.0 %all-gather.8.cloned.1.call-done = bf16[2048,512]{0,1:T(8,128)(2,1)} async-done(((bf16[512,512]{0,1:T(8,128)(2,1)}), bf16[2048,512]{0,1:T(8,128)(2,1)}) %all-gather.8.cloned.1.call-update) | async-done | bytes 2097168 | tf_op jit(solution)/shard_map/all_gather | solution.py:23
  237.7 5.8 %fusion.26 = f32[256,512]{1,0:T(8,128)S(1)} fusion(bf16[4,512,512]{2,1,0:T(8,128)(2,1)S(1)} %copy-done, bf16[4,256,2048]{2,1,0:T(8,128)(2,1)} %param.8, bf16[2048,512]{0,1:T(8,128)(2,1)} %all-gather.8.cloned.1.call-done, f32[1,256,512]{2,0,1:T(1,128)} %fusion.35), kind=kOutput, calls=%fused_computation.17 | convolution fusion | flops 2685009920 | bytes 9437184 | tf_op jit(solution)/shard_map/qaj,qji->ai/dot_general | solution.py:71
  244.6 28.5 %all_to_all.33 = f32[32,256,16]{1,2,0:T(8,128)S(1)} all-to-all(f32[32,256,16]{1,2,0:T(8,128)} %bitcast.117), channel_id=1, replica_groups=mesh['aux'=32,'vir_0'=4,'vir_1'=2] {'aux'}, dimensions={0} | all-to-all | bytes 1048576 | tf_op jit(solution)/shard_map/all_to_all | solution.py:34
  273.9 22.9 %all_to_all.34 = f32[32,256,16]{1,2,0:T(8,128)S(1)} all-to-all(f32[32,256,16]{1,2,0:T(8,128)S(1)} %broadcast_in_dim.8), channel_id=1, replica_groups=mesh['aux'=32,'vir_0'=4,'vir_1'=2] {'aux'}, dimensions={0} | all-to-all | bytes 1048576 | tf_op jit(solution)/shard_map/all_to_all | solution.py:46
  (27 shorter events, 8.9 us)
Async XLA Ops:
  6.5 48.9 %copy-start = (bf16[4,512,512]{2,1,0:T(8,128)(2,1)S(1)}, bf16[4,512,512]{2,1,0:T(8,128)(2,1)}, u32[]{:S(2)}) copy-start(bf16[4,512,512]{2,1,0:T(8,128)(2,1)} %param.9) | copy-start | bytes 6291460
  6.5 48.9 %all-gather.4.cloned.1.call-start = ((), (), s32[]{:S(2)}) async-start(), calls=%async_computation.6 | async-start | bytes 2621440 | tf_op jit(solution)/shard_map/all_gather | solution.py:23
  19.7 1.0 copy-start.1
  20.7 15.2 %copy-start.2 = (f32[4]{0:T(128)S(1)}, f32[4]{0:T(128)}, u32[]{:S(2)}) copy-start(f32[4]{0:T(128)} %param.11) | copy-start | bytes 52
  62.3 28.6 %all-to-all-start = ((f32[32,256,16]{1,2,0:T(8,128)}), f32[32,256,16]{1,2,0:T(8,128)S(1)}, u32[]{:S(2)}, u32[]{:S(2)}) async-start(f32[32,256,16]{1,2,0:T(8,128)} %bitcast.115), calls=%async_computation | async-start | bytes 1048576 | tf_op jit(solution)/shard_map/all_to_all | solution.py:34
  72.7 72.9 %all-gather.6.cloned.1.call-start = ((), (), s32[]{:S(2)}) async-start(), calls=%async_computation.7 | async-start | bytes 2621440 | tf_op jit(solution)/shard_map/all_gather | solution.py:23
  116.8 120.9 %all-gather.8.cloned.1.call-start = ((), (), s32[]{:S(2)}) async-start(), calls=%async_computation.8 | async-start | bytes 2621440 | tf_op jit(solution)/shard_map/all_gather | solution.py:23
Sparse Core Ops, SparseCore 0:
  17.3 38.0 all-gather.3
  116.9 28.7 all-gather.5
  209.0 28.7 all-gather.7
where the time goes:
time: 305 us; the launch traced here: 304 us
  blocking collectives  173 us (57%)
  waiting for transfers between devices  59.4 us (19%)
  matrix products  33.4 us (11%)
  between operations  13.2 us (4%)
  starting transfers between devices  10.5 us (3%)
  local copies, waits for them, and re-layouts  10.1 us (3%)
  other arithmetic  5 us (2%)
    all_to_all x3, blocking collectives, sent_to_all(): lax.all_to_all(jnp.broadcast_to(value[None], (length, *value.shape)), axi...  59.1 us
    all_to_all x2, blocking collectives, summed_on_arrival(): lax.all_to_all(pieces, axis, split_axis=0, concat_axis=0, tiled=True)  56.9 us
    all_gather x3, waiting for transfers between devices, whole_of(): out = lax.all_gather(out, axes[number], axis=dim, tiled=True)  41.3 us
    psum x6, blocking collectives, by_axis(): return functools.reduce(lax.psum, axes, value)  34.9 us
    all_gather x3, blocking collectives, whole_of(): out = lax.all_gather(out, axes[number], axis=dim, tiled=True)  21.7 us
    dot_general x3, matrix products, local(): jnp.einsum('qaj,qji->ai', mixed_half, b_oo, preferred_element_type=jnp.fl...  18.1 us
    all_to_all x1, waiting for transfers between devices, summed_on_arrival(): lax.all_to_all(pieces, axis, split_axis=0, concat_axis=0, tiled=True)  18 us
    all_to_all x1, starting transfers between devices, summed_on_arrival(): lax.all_to_all(pieces, axis, split_axis=0, concat_axis=0, tiled=True)  10.5 us
  transfers between devices with their start and end apart: 4, of which 4 were waited for; matrix products, arithmetic and copies ran while one was open for 6% of the time, Pallas kernels for 0%

commit v1 on v0

v1 whole, which is shorter than its diff:
```python
import math

import jax
import jax.numpy as jnp
from jax import lax
from jax.sharding import Mesh
from jax.sharding import PartitionSpec as P

V = 2048
O = 512
NAUX = 128
ITERS = 3
AUX = ("yh", "z", "c")
VIR = ("x", "yl")
PLANE = ("x", "yl", "yh")
SCALE = math.sqrt(4.0 * V * O / NAUX)
BF, F32 = jnp.bfloat16, jnp.float32


def swap(value, axis, bit=1):
    n = lax.axis_size(axis)
    return lax.ppermute(value, axis, [(i, i ^ bit) for i in range(n)])


def sent_to_all(value, axes, n):
    wide = jnp.broadcast_to(value[None], (n, *value.shape))
    return lax.all_to_all(wide, axes, 0, 0, tiled=True)


def half(value, which, dim):
    size = value.shape[dim] // 2
    return lax.dynamic_slice_in_dim(value, which * size, size, dim)


def local(b_ov, b_vv, b_oo, rhs, fit_pert, eps_vir, eps_occ):
    c = lax.axis_index("c")
    yh = lax.axis_index("yh")
    block = lax.axis_index("x") * 2 + lax.axis_index("yl")
    rhs_part = half(half(rhs, c, 1), yh, 0)
    denom_part = half(eps_vir, yh, 0)[:, None] - half(eps_occ, c, 0)[None, :]
    vv = (b_vv, swap(b_vv, "c"))
    oo = (half(b_oo, c, 1), swap(half(b_oo, 1 - c, 1), "c"))
    ov = jnp.concatenate([half(b_ov, c, 2), swap(half(b_ov, 1 - c, 2), "c")])
    fit = jnp.concatenate([fit_pert, swap(fit_pert, "c")])
    part = rhs_part / denom_part
    for step in range(ITERS):
        full = sent_to_all(part.astype(BF), PLANE, 16).reshape(V, O // 2)
        own = lax.dynamic_slice_in_dim(full, block * 256, 256, 0)
        fitted = jnp.sum(ov.astype(F32) * own.astype(F32)[None], axis=(1, 2))
        fitted = fitted + jnp.roll(swap(fitted, "c"), 4)
        fitted = fitted + swap(fitted, "yl")
        fitted = fitted + swap(fitted, "x", 1)
        fitted = fitted + swap(fitted, "x", 2)
        weight = SCALE * fit - 4.0 * fitted
        total = jnp.zeros((rhs.shape[0], O), F32)
        for vvs, oos in zip(vv, oo, strict=True):
            mixed = jnp.einsum("qab,bj->qaj", vvs, full, preferred_element_type=F32)
            total = total + jnp.einsum(
                "qaj,qji->ai", mixed.astype(BF), oos, preferred_element_type=F32
            )
        extra = jnp.sum(ov.astype(F32) * weight[:, None, None], axis=0)
        chip = half(total, c, 1) + extra + swap(half(total, 1 - c, 1), "c")
        rows = half(chip, yh, 0) + swap(half(chip, 1 - yh, 0).astype(BF), "yh")
        share = sent_to_all(rows.astype(BF), "z", 8).astype(F32).sum(axis=0)
        part = (rhs_part + share) / denom_part
    part = part.astype(BF)
    there = swap(part, "yh")
    both = jnp.where(yh == 0, jnp.stack([part, there]), jnp.stack([there, part]))
    both = both.reshape(2 * part.shape[0], part.shape[1])
    there = swap(both, "c")
    left, right = jnp.where(c == 0, both, there), jnp.where(c == 0, there, both)
    return jnp.concatenate([left, right], axis=1).astype(F32)


def solution(mesh):
    split = Mesh(mesh.devices.reshape(2, 8, 2, 4, 2), ("yh", "z", "c", "x", "yl"))
    placed = (
        P(AUX, VIR, None),
        P(AUX, VIR, None),
        P(AUX, None, None),
        P(VIR, None),
        P(AUX),
        P(VIR),
        P(),
    )
    return jax.shard_map(
        local, mesh=split, in_specs=placed, out_specs=P(VIR, None), check_vma=False
    )
```

time: 305 us -> 236 us (0.77)
  blocking collectives: 173 us -> 87 us
  starting transfers between devices: 10.5 us -> 44.2 us
  between operations: 13.2 us -> 0.25 us
  waiting for transfers between devices: 59.4 us -> 47.7 us
  other arithmetic: 5 us -> 11.6 us
    all_gather x3 -> x0, waiting for transfers between devices: 41.3 us -> none  [whole_of(): out = lax.all_gather(out, axes[number], axis=dim, tiled=True)]
    ppermute x0 -> x24, starting transfers between devices: none -> 39.1 us  [swap(): return lax.ppermute(value, axis, [(i, i ^ bit) for i in range(n)])]
    psum x6 -> x0, blocking collectives: 34.9 us -> none  [by_axis(): return functools.reduce(lax.psum, axes, value)]
    ppermute x0 -> x24, waiting for transfers between devices: none -> 34.1 us  [swap(): return lax.ppermute(value, axis, [(i, i ^ bit) for i in range(n)])]
    all_to_all x5, blocking collectives: 116 us -> 87 us  [sent_to_all(): return lax.all_to_all(wide, axes, 0, 0, tiled=True)]
    all_gather x3 -> x0, blocking collectives: 21.7 us -> none  [whole_of(): out = lax.all_gather(out, axes[number], axis=dim, tiled=True)]
    dynamic_slice x0 -> x7, local copies, waits for them, and re-layouts: none -> 7.55 us  [half(): return lax.dynamic_slice_in_dim(value, which * size, size, dim)]
    all_to_all x1, starting transfers between devices: 10.5 us -> 5.1 us  [sent_to_all(): return lax.all_to_all(wide, axes, 0, 0, tiled=True)]
  transfers between devices with their start and end apart: 4 -> 25, of which waited for: 4 -> 15; matrix products, arithmetic and copies ran while one was open for 6% -> 19% of each run, Pallas kernels for 0% -> 0%
where the time goes in v1:
time: 236 us; the launch traced here: 235 us
  blocking collectives  87 us (37%)
  waiting for transfers between devices  47.7 us (20%)
  starting transfers between devices  44.2 us (19%)
  matrix products  33.2 us (14%)
  other arithmetic  11.6 us (5%)
  local copies, waits for them, and re-layouts  11.2 us (5%)
    all_to_all x5, blocking collectives, sent_to_all(): return lax.all_to_all(wide, axes, 0, 0, tiled=True)  87 us
    ppermute x24, starting transfers between devices, swap(): return lax.ppermute(value, axis, [(i, i ^ bit) for i in range(n)])  39.1 us
    ppermute x24, waiting for transfers between devices, swap(): return lax.ppermute(value, axis, [(i, i ^ bit) for i in range(n)])  34.1 us
    dot_general x6, matrix products, local(): jnp.einsum('qaj,qji->ai', mixed.astype(BF), oos, preferred_element_type=F32)  33.2 us
    all_to_all x1, waiting for transfers between devices, sent_to_all(): return lax.all_to_all(wide, axes, 0, 0, tiled=True)  13.6 us
    dynamic_slice x7, local copies, waits for them, and re-layouts, half(): return lax.dynamic_slice_in_dim(value, which * size, size, dim)  7.55 us
    all_to_all x1, starting transfers between devices, sent_to_all(): return lax.all_to_all(wide, axes, 0, 0, tiled=True)  5.1 us
  transfers between devices with their start and end apart: 25, of which 15 were waited for; matrix products, arithmetic and copies ran while one was open for 19% of the time, Pallas kernels for 0%

profile of v1, /device:TPU:1, one launch (start us, length us, event | category | flops | bytes accessed | tf_op | source)
XLA Modules:
  0.0 235.2 jit_solution(15016922198780390041)
XLA Ops:
  0.0 3.2 %collective-permute-start = (bf16[4,256,2048]{2,1,0:T(8,128)(2,1)}, bf16[4,256,2048]{2,1,0:T(8,128)(2,1)}, u32[]{:S(2)}, u32[]{:S(2)}) collective-permute-start(bf16[4,256,2048]{2,1,0:T(8,128)(2,1)} %param.8), channel_id=1, source_target_pairs={{0,8},{8,0},{1,9},{9,1},{2,10},{10,2},{3,11},{11,3},{4,12},{12,4},... | collective-permute-start | bytes 12582920 | tf_op jit(solution)/shard_map/ppermute | solution.py:22
  6.8 5.1 %all-to-all-start = ((bf16[16,128,256]{2,1,0:T(8,128)(2,1)}), bf16[16,128,256]{2,1,0:T(8,128)(2,1)}, u32[]{:S(2)}, u32[]{:S(2)}) async-start(bf16[16,128,256]{2,1,0:T(8,128)(2,1)} %broadcast_in_dim.12), calls=%async_computation | async-start | bytes 2097152 | tf_op jit(solution)/shard_map/all_to_all | solution.py:27
  11.9 2.1 constant_dynamic-slice_fusion.4
  16.1 13.6 %all-to-all-done = bf16[16,128,256]{2,1,0:T(8,128)(2,1)} async-done(((bf16[16,128,256]{2,1,0:T(8,128)(2,1)}), bf16[16,128,256]{2,1,0:T(8,128)(2,1)}, u32[]{:S(2)}, u32[]{:S(2)}) %all-to-all-start) | async-done | bytes 1048608 | tf_op jit(solution)/shard_map/all_to_all | solution.py:27
  31.0 1.8 collective-permute-start.4
  32.8 5.3 %convolution_bitcast_fusion.5 = f32[256,512]{1,0:T(8,128)} fusion(bf16[4,512,512]{2,1,0:T(8,128)(2,1)S(1)} %copy-done, s32[]{:T(128)S(6)} %select_n.65, bf16[2048,256,1]{1,0,2:T(8,128)(2,1)} %bitcast.1, bf16[4,256,2048]{2,1,0:T(8,128)(2,1)} %param.8), kind=kOutput, calls=%fused_computation.29 | convolution fusion | flops 1342439424 | bytes 6815748 | tf_op jit(solution)/shard_map/qaj,qji->ai/dot_general | solution.py:58
  40.9 2.4 %collective-permute-done.6 = f32[8]{0:T(128)S(1)} collective-permute-done((f32[8]{0:T(128)S(1)}, f32[8]{0:T(128)S(1)}, u32[]{:S(2)}, u32[]{:S(2)}) %collective-permute-start.6) | collective-permute-done | bytes 64 | tf_op jit(solution)/shard_map/ppermute | solution.py:22
  44.1 5.7 %fusion.12 = f32[256,512]{1,0:T(8,128)} fusion(f32[256,512]{1,0:T(8,128)} %convolution_bitcast_fusion.5, bf16[4,256,512]{2,1,0:T(8,128)(2,1)} %collective-permute-done.1, bf16[2048,256,1]{1,0,2:T(8,128)(2,1)} %bitcast.1, bf16[4,256,2048]{2,1,0:T(8,128)(2,1)} %collective-permute-done), kind=kOutput, calls=%fused_computation.30 | convolution fusion | flops 1342570496 | bytes 7340032 | tf_op jit(solution)/shard_map/qaj,qji->ai/dot_general | solution.py:58
  50.8 2.4 %collective-permute-start.8 = (f32[256,256]{1,0:T(8,128)S(1)}, f32[256,256]{1,0:T(8,128)S(1)}, u32[]{:S(2)}, u32[]{:S(2)}) collective-permute-start(f32[256,256]{1,0:T(8,128)S(1)} %constant_dynamic-slice_fusion.2), channel_id=1, source_target_pairs={{0,8},{8,0},{1,9},{9,1},{2,10},{10,2},{3,11},{11,3},{4,12},{12,4},... | collective-permute-start | bytes 786440 | tf_op jit(solution)/shard_map/ppermute | solution.py:22
  55.4 1.7 collective-permute-start.9
  57.1 3.0 %collective-permute-done.9 = bf16[128,256]{1,0:T(8,128)(2,1)S(1)} collective-permute-done((bf16[128,256]{1,0:T(8,128)(2,1)S(1)}, bf16[128,256]{1,0:T(8,128)(2,1)S(1)}, u32[]{:S(2)}, u32[]{:S(2)}) %collective-permute-start.9) | collective-permute-done | bytes 65568 | tf_op jit(solution)/shard_map/ppermute | solution.py:22
  60.2 22.9 %all_to_all.30 = bf16[8,128,256]{2,1,0:T(8,128)(2,1)S(1)} all-to-all(bf16[8,128,256]{2,1,0:T(8,128)(2,1)S(1)} %broadcast_in_dim.13), channel_id=1, replica_groups=mesh['yh'=2,'z'=8,'c'=2,'x'=4,'yl'=2] {'z'}, dimensions={0} | all-to-all | bytes 1048576 | tf_op jit(solution)/shard_map/all_to_all | solution.py:27
  84.3 18.9 %all_to_all.31 = bf16[16,128,256]{2,1,0:T(8,128)(2,1)S(1)} all-to-all(bf16[16,128,256]{2,1,0:T(8,128)(2,1)S(1)} %broadcast_in_dim.14), channel_id=1, replica_groups=mesh['yh'=2,'z'=8,'c'=2,'x'=4,'yl'=2] {'x','yl','yh'}, dimensions={0} | all-to-all | bytes 2097152 | tf_op jit(solution)/shard_map/all_to_all | solution.py:27
  104.6 5.0 %collective-permute-start.10 = (f32[8]{0:T(128)S(1)}, f32[8]{0:T(128)S(1)}, u32[]{:S(2)}, u32[]{:S(2)}) collective-permute-start(f32[8]{0:T(128)S(1)} %fusion.2), channel_id=1, source_target_pairs={{0,8},{8,0},{1,9},{9,1},{2,10},{10,2},{3,11},{11,3},{4,12},{12,4},... | collective-permute-start | bytes 104 | tf_op jit(solution)/shard_map/ppermute | solution.py:22
  109.5 5.3 %convolution_bitcast_fusion.3 = f32[256,512]{1,0:T(8,128)} fusion(bf16[4,512,512]{2,1,0:T(8,128)(2,1)S(1)} %copy-done, s32[]{:T(128)S(6)} %select_n.65, bf16[2048,256,1]{1,0,2:T(8,128)(2,1)} %bitcast.75, bf16[4,256,2048]{2,1,0:T(8,128)(2,1)} %param.8), kind=kOutput, calls=%fused_computation.27 | convolution fusion | flops 1342439424 | bytes 6815748 | tf_op jit(solution)/shard_map/qaj,qji->ai/dot_general | solution.py:58
  114.9 5.7 %fusion.13 = f32[256,512]{1,0:T(8,128)} fusion(f32[256,512]{1,0:T(8,128)} %convolution_bitcast_fusion.3, bf16[4,256,512]{2,1,0:T(8,128)(2,1)} %collective-permute-done.1, bf16[2048,256,1]{1,0,2:T(8,128)(2,1)} %bitcast.76, bf16[4,256,2048]{2,1,0:T(8,128)(2,1)} %collective-permute-done), kind=kOutput, calls=%fused_computation.31 | convolution fusion | flops 1342570496 | bytes 7340032 | tf_op jit(solution)/shard_map/qaj,qji->ai/dot_general | solution.py:58
  122.2 2.0 collective-permute-done.11
  124.3 2.4 %collective-permute-done.12 = f32[8]{0:T(128)S(1)} collective-permute-done((f32[8]{0:T(128)S(1)}, f32[8]{0:T(128)S(1)}, u32[]{:S(2)}, u32[]{:S(2)}) %collective-permute-start.12) | collective-permute-done | bytes 64 | tf_op jit(solution)/shard_map/ppermute | solution.py:22
  127.7 2.9 %collective-permute-done.13 = f32[8]{0:T(128)S(1)} collective-permute-done((f32[8]{0:T(128)S(1)}, f32[8]{0:T(128)S(1)}, u32[]{:S(2)}, u32[]{:S(2)}) %collective-permute-start.13) | collective-permute-done | bytes 64 | tf_op jit(solution)/shard_map/ppermute | solution.py:22
  133.0 3.7 %collective-permute-done.15 = bf16[128,256]{1,0:T(8,128)(2,1)S(1)} collective-permute-done((bf16[128,256]{1,0:T(8,128)(2,1)S(1)}, bf16[128,256]{1,0:T(8,128)(2,1)S(1)}, u32[]{:S(2)}, u32[]{:S(2)}) %collective-permute-start.15) | collective-permute-done | bytes 65568 | tf_op jit(solution)/shard_map/ppermute | solution.py:22
  136.8 15.4 %all_to_all.32 = bf16[8,128,256]{2,1,0:T(8,128)(2,1)S(1)} all-to-all(bf16[8,128,256]{2,1,0:T(8,128)(2,1)S(1)} %broadcast_in_dim.15), channel_id=1, replica_groups=mesh['yh'=2,'z'=8,'c'=2,'x'=4,'yl'=2] {'z'}, dimensions={0} | all-to-all | bytes 1048576 | tf_op jit(solution)/shard_map/all_to_all | solution.py:27
  153.4 15.2 %all_to_all.33 = bf16[16,128,256]{2,1,0:T(8,128)(2,1)S(1)} all-to-all(bf16[16,128,256]{2,1,0:T(8,128)(2,1)S(1)} %broadcast_in_dim.16), channel_id=1, replica_groups=mesh['yh'=2,'z'=8,'c'=2,'x'=4,'yl'=2] {'x','yl','yh'}, dimensions={0} | all-to-all | bytes 2097152 | tf_op jit(solution)/shard_map/all_to_all | solution.py:27
  170.0 7.8 %collective-permute-start.16 = (f32[8]{0:T(128)S(1)}, f32[8]{0:T(128)S(1)}, u32[]{:S(2)}, u32[]{:S(2)}) collective-permute-start(f32[8]{0:T(128)S(1)} %fusion.4), channel_id=1, source_target_pairs={{0,8},{8,0},{1,9},{9,1},{2,10},{10,2},{3,11},{11,3},{4,12},{12,4},... | collective-permute-start | bytes 104 | tf_op jit(solution)/shard_map/ppermute | solution.py:22
  177.8 5.3 %convolution_bitcast_fusion.1 = f32[256,512]{1,0:T(8,128)} fusion(bf16[4,512,512]{2,1,0:T(8,128)(2,1)S(1)} %copy-done, s32[]{:T(128)S(6)} %select_n.65, bf16[2048,256,1]{1,0,2:T(8,128)(2,1)} %bitcast.72, bf16[4,256,2048]{2,1,0:T(8,128)(2,1)} %param.8), kind=kOutput, calls=%fused_computation.25 | convolution fusion | flops 1342439424 | bytes 6815748 | tf_op jit(solution)/shard_map/qaj,qji->ai/dot_general | solution.py:58
  183.2 5.7 %fusion.14 = f32[256,512]{1,0:T(8,128)} fusion(f32[256,512]{1,0:T(8,128)} %convolution_bitcast_fusion.1, bf16[4,256,512]{2,1,0:T(8,128)(2,1)} %collective-permute-done.1, bf16[2048,256,1]{1,0,2:T(8,128)(2,1)} %bitcast.73, bf16[4,256,2048]{2,1,0:T(8,128)(2,1)} %collective-permute-done), kind=kOutput, calls=%fused_computation.32 | convolution fusion | flops 1342570496 | bytes 7340032 | tf_op jit(solution)/shard_map/qaj,qji->ai/dot_general | solution.py:58
  190.8 2.0 collective-permute-done.17
  192.8 2.4 %collective-permute-done.18 = f32[8]{0:T(128)S(1)} collective-permute-done((f32[8]{0:T(128)S(1)}, f32[8]{0:T(128)S(1)}, u32[]{:S(2)}, u32[]{:S(2)}) %collective-permute-start.18) | collective-permute-done | bytes 64 | tf_op jit(solution)/shard_map/ppermute | solution.py:22
  196.2 2.9 %collective-permute-done.19 = f32[8]{0:T(128)S(1)} collective-permute-done((f32[8]{0:T(128)S(1)}, f32[8]{0:T(128)S(1)}, u32[]{:S(2)}, u32[]{:S(2)}) %collective-permute-start.19) | collective-permute-done | bytes 64 | tf_op jit(solution)/shard_map/ppermute | solution.py:22
  201.6 3.7 %collective-permute-done.21 = bf16[128,256]{1,0:T(8,128)(2,1)S(1)} collective-permute-done((bf16[128,256]{1,0:T(8,128)(2,1)S(1)}, bf16[128,256]{1,0:T(8,128)(2,1)S(1)}, u32[]{:S(2)}, u32[]{:S(2)}) %collective-permute-start.21) | collective-permute-done | bytes 65568 | tf_op jit(solution)/shard_map/ppermute | solution.py:22
  205.3 14.6 %all_to_all.34 = bf16[8,128,256]{2,1,0:T(8,128)(2,1)S(1)} all-to-all(bf16[8,128,256]{2,1,0:T(8,128)(2,1)S(1)} %broadcast_in_dim.17), channel_id=1, replica_groups=mesh['yh'=2,'z'=8,'c'=2,'x'=4,'yl'=2] {'z'}, dimensions={0} | all-to-all | bytes 1048576 | tf_op jit(solution)/shard_map/all_to_all | solution.py:27
  222.0 3.8 %collective-permute-done.22 = bf16[128,256]{1,0:T(8,128)(2,1)S(1)} collective-permute-done((bf16[128,256]{1,0:T(8,128)(2,1)S(1)}, bf16[128,256]{1,0:T(8,128)(2,1)S(1)}, u32[]{:S(2)}, u32[]{:S(2)}) %collective-permute-start.22) | collective-permute-done | bytes 65568 | tf_op jit(solution)/shard_map/ppermute | solution.py:22
  225.8 7.5 %collective-permute-start.23 = (bf16[256,256]{1,0:T(8,128)(2,1)S(1)}, bf16[256,256]{1,0:T(8,128)(2,1)S(1)}, u32[]{:S(2)}, u32[]{:S(2)}) collective-permute-start(bf16[256,256]{1,0:T(8,128)(2,1)S(1)} %bitcast.77), channel_id=1, source_target_pairs={{0,8},{8,0},{1,9},{9,1},{2,10},{10,2},{3,11},{11,3},{4,12},{12,4},... | collective-permute-start | bytes 393224 | tf_op jit(solution)/shard_map/ppermute | solution.py:22
  (93 shorter events, 33.3 us)
Async XLA Ops:
  0.0 14.5 %copy-start = (bf16[4,512,512]{2,1,0:T(8,128)(2,1)S(1)}, bf16[4,512,512]{2,1,0:T(8,128)(2,1)}, u32[]{:S(2)}) copy-start(bf16[4,512,512]{2,1,0:T(8,128)(2,1)} %param.9) | copy-start | bytes 6291460
  0.0 14.5 %copy-start.3 = (f32[4]{0:T(128)S(1)}, f32[4]{0:T(128)}, u32[]{:S(2)}) copy-start(f32[4]{0:T(128)} %param.11) | copy-start | bytes 52
  0.0 44.1 %collective-permute-start = (bf16[4,256,2048]{2,1,0:T(8,128)(2,1)}, bf16[4,256,2048]{2,1,0:T(8,128)(2,1)}, u32[]{:S(2)}, u32[]{:S(2)}) collective-permute-start(bf16[4,256,2048]{2,1,0:T(8,128)(2,1)} %param.8), channel_id=1, source_target_pairs={{0,8},{8,0},{1,9},{9,1},{2,10},{10,2},{3,11},{11,3},{4,12},{12,4},... | collective-permute-start | bytes 12582920 | tf_op jit(solution)/shard_map/ppermute | solution.py:22
  6.8 22.9 %all-to-all-start = ((bf16[16,128,256]{2,1,0:T(8,128)(2,1)}), bf16[16,128,256]{2,1,0:T(8,128)(2,1)}, u32[]{:S(2)}, u32[]{:S(2)}) async-start(bf16[16,128,256]{2,1,0:T(8,128)(2,1)} %broadcast_in_dim.12), calls=%async_computation | async-start | bytes 2097152 | tf_op jit(solution)/shard_map/all_to_all | solution.py:27
  14.0 16.6 %collective-permute-start.2 = (bf16[4,256,256]{2,1,0:T(8,128)(2,1)}, bf16[4,256,256]{2,1,0:T(8,128)(2,1)S(1)}, u32[]{:S(2)}, u32[]{:S(2)}) collective-permute-start(bf16[4,256,256]{2,1,0:T(8,128)(2,1)} %get-tuple-element.6), channel_id=1, source_target_pairs={{0,8},{8,0},{1,9},{9,1},{2,10},{10,2},{3,11},{11,3},{4,12},{12,4},... | collective-permute-start | bytes 1572872 | tf_op jit(solution)/shard_map/ppermute | solution.py:22
  14.5 38.7 %collective-permute-start.3 = (f32[4]{0:T(128)S(1)}, f32[4]{0:T(128)S(1)}, u32[]{:S(2)}, u32[]{:S(2)}) collective-permute-start(f32[4]{0:T(128)S(1)} %copy-done.3), channel_id=1, source_target_pairs={{0,8},{8,0},{1,9},{9,1},{2,10},{10,2},{3,11},{11,3},{4,12},{12,4},... | collective-permute-start | bytes 56 | tf_op jit(solution)/shard_map/ppermute | solution.py:22
  15.6 28.5 %collective-permute-start.1 = (bf16[4,256,512]{2,1,0:T(8,128)(2,1)}, bf16[4,256,512]{2,1,0:T(8,128)(2,1)}, u32[]{:S(2)}, u32[]{:S(2)}) collective-permute-start(bf16[4,256,512]{2,1,0:T(8,128)(2,1)} %constant_dynamic-slice_fusion.5), channel_id=1, source_target_pairs={{0,8},{8,0},{1,9},{9,1},{2,10},{10,2},{3,11},{11,3},{4,12},{12,4},... | collective-permute-start | bytes 3145736 | tf_op jit(solution)/shard_map/ppermute | solution.py:22
  31.0 7.1 %collective-permute-start.4 = (f32[8]{0:T(128)S(1)}, f32[8]{0:T(128)S(1)}, u32[]{:S(2)}, u32[]{:S(2)}) collective-permute-start(f32[8]{0:T(128)S(1)} %fusion), channel_id=1, source_target_pairs={{0,8},{8,0},{1,9},{9,1},{2,10},{10,2},{3,11},{11,3},{4,12},{12,4},... | collective-permute-start | bytes 104 | tf_op jit(solution)/shard_map/ppermute | solution.py:22
  38.3 2.6 %collective-permute-start.5 = (f32[8]{0:T(128)S(1)}, f32[8]{0:T(128)S(1)}, u32[]{:S(2)}, u32[]{:S(2)}) collective-permute-start(f32[8]{0:T(128)S(1)} %maximum_add_fusion), channel_id=1, source_target_pairs={{0,1},{1,0},{2,3},{3,2},{4,5},{5,4},{6,7},{7,6},{8,9},{9,8},{10,11... | collective-permute-start | bytes 104 | tf_op jit(solution)/shard_map/ppermute | solution.py:22
  40.9 2.4 %collective-permute-start.6 = (f32[8]{0:T(128)S(1)}, f32[8]{0:T(128)S(1)}, u32[]{:S(2)}, u32[]{:S(2)}) collective-permute-start(f32[8]{0:T(128)S(1)} %add.126), channel_id=1, source_target_pairs={{0,2},{2,0},{4,6},{6,4},{1,3},{3,1},{5,7},{7,5},{8,10},{10,8},{12,... | collective-permute-start | bytes 104 | tf_op jit(solution)/shard_map/ppermute | solution.py:22
  43.3 9.9 %collective-permute-start.7 = (f32[8]{0:T(128)S(1)}, f32[8]{0:T(128)S(1)}, u32[]{:S(2)}, u32[]{:S(2)}) collective-permute-start(f32[8]{0:T(128)S(1)} %add.127), channel_id=1, source_target_pairs={{0,4},{2,6},{4,0},{6,2},{1,5},{3,7},{5,1},{7,3},{8,12},{10,14},{12... | collective-permute-start | bytes 104 | tf_op jit(solution)/shard_map/ppermute | solution.py:22
  50.8 3.6 %collective-permute-start.8 = (f32[256,256]{1,0:T(8,128)S(1)}, f32[256,256]{1,0:T(8,128)S(1)}, u32[]{:S(2)}, u32[]{:S(2)}) collective-permute-start(f32[256,256]{1,0:T(8,128)S(1)} %constant_dynamic-slice_fusion.2), channel_id=1, source_target_pairs={{0,8},{8,0},{1,9},{9,1},{2,10},{10,2},{3,11},{11,3},{4,12},{12,4},... | collective-permute-start | bytes 786440 | tf_op jit(solution)/shard_map/ppermute | solution.py:22
  55.4 4.7 %collective-permute-start.9 = (bf16[128,256]{1,0:T(8,128)(2,1)S(1)}, bf16[128,256]{1,0:T(8,128)(2,1)S(1)}, u32[]{:S(2)}, u32[]{:S(2)}) collective-permute-start(bf16[128,256]{1,0:T(8,128)(2,1)S(1)} %dynamic-slice_convert_fusion.4), channel_id=1, source_target_pairs={{0,128},{128,0},{1,129},{129,1},{2,130},{130,2},{3,131},{131,3},{4... | collective-permute-start | bytes 196616 | tf_op jit(solution)/shard_map/ppermute | solution.py:22
  103.2 1.0 copy-start.2
  104.6 17.1 %collective-permute-start.10 = (f32[8]{0:T(128)S(1)}, f32[8]{0:T(128)S(1)}, u32[]{:S(2)}, u32[]{:S(2)}) collective-permute-start(f32[8]{0:T(128)S(1)} %fusion.2), channel_id=1, source_target_pairs={{0,8},{8,0},{1,9},{9,1},{2,10},{10,2},{3,11},{11,3},{4,12},{12,4},... | collective-permute-start | bytes 104 | tf_op jit(solution)/shard_map/ppermute | solution.py:22
  121.6 9.4 %collective-permute-start.14 = (f32[256,256]{1,0:T(8,128)S(1)}, f32[256,256]{1,0:T(8,128)S(1)}, u32[]{:S(2)}, u32[]{:S(2)}) collective-permute-start(f32[256,256]{1,0:T(8,128)S(1)} %constant_dynamic-slice_fusion.1), channel_id=1, source_target_pairs={{0,8},{8,0},{1,9},{9,1},{2,10},{10,2},{3,11},{11,3},{4,12},{12,4},... | collective-permute-start | bytes 786440 | tf_op jit(solution)/shard_map/ppermute | solution.py:22
  121.8 2.4 %collective-permute-start.11 = (f32[8]{0:T(128)S(1)}, f32[8]{0:T(128)S(1)}, u32[]{:S(2)}, u32[]{:S(2)}) collective-permute-start(f32[8]{0:T(128)S(1)} %maximum_add_fusion.1), channel_id=1, source_target_pairs={{0,1},{1,0},{2,3},{3,2},{4,5},{5,4},{6,7},{7,6},{8,9},{9,8},{10,11... | collective-permute-start | bytes 104 | tf_op jit(solution)/shard_map/ppermute | solution.py:22
  124.3 2.4 %collective-permute-start.12 = (f32[8]{0:T(128)S(1)}, f32[8]{0:T(128)S(1)}, u32[]{:S(2)}, u32[]{:S(2)}) collective-permute-start(f32[8]{0:T(128)S(1)} %add.136), channel_id=1, source_target_pairs={{0,2},{2,0},{4,6},{6,4},{1,3},{3,1},{5,7},{7,5},{8,10},{10,8},{12,... | collective-permute-start | bytes 104 | tf_op jit(solution)/shard_map/ppermute | solution.py:22
  126.7 3.9 %collective-permute-start.13 = (f32[8]{0:T(128)S(1)}, f32[8]{0:T(128)S(1)}, u32[]{:S(2)}, u32[]{:S(2)}) collective-permute-start(f32[8]{0:T(128)S(1)} %add.137), channel_id=1, source_target_pairs={{0,4},{2,6},{4,0},{6,2},{1,5},{3,7},{5,1},{7,3},{8,12},{10,14},{12... | collective-permute-start | bytes 104 | tf_op jit(solution)/shard_map/ppermute | solution.py:22
  132.0 4.7 %collective-permute-start.15 = (bf16[128,256]{1,0:T(8,128)(2,1)S(1)}, bf16[128,256]{1,0:T(8,128)(2,1)S(1)}, u32[]{:S(2)}, u32[]{:S(2)}) collective-permute-start(bf16[128,256]{1,0:T(8,128)(2,1)S(1)} %dynamic-slice_convert_fusion.2), channel_id=1, source_target_pairs={{0,128},{128,0},{1,129},{129,1},{2,130},{130,2},{3,131},{131,3},{4... | collective-permute-start | bytes 196616 | tf_op jit(solution)/shard_map/ppermute | solution.py:22
  168.6 1.0 copy-start.1
  170.0 19.9 %collective-permute-start.16 = (f32[8]{0:T(128)S(1)}, f32[8]{0:T(128)S(1)}, u32[]{:S(2)}, u32[]{:S(2)}) collective-permute-start(f32[8]{0:T(128)S(1)} %fusion.4), channel_id=1, source_target_pairs={{0,8},{8,0},{1,9},{9,1},{2,10},{10,2},{3,11},{11,3},{4,12},{12,4},... | collective-permute-start | bytes 104 | tf_op jit(solution)/shard_map/ppermute | solution.py:22
  189.9 9.6 %collective-permute-start.20 = (f32[256,256]{1,0:T(8,128)S(1)}, f32[256,256]{1,0:T(8,128)S(1)}, u32[]{:S(2)}, u32[]{:S(2)}) collective-permute-start(f32[256,256]{1,0:T(8,128)S(1)} %constant_dynamic-slice_fusion), channel_id=1, source_target_pairs={{0,8},{8,0},{1,9},{9,1},{2,10},{10,2},{3,11},{11,3},{4,12},{12,4},... | collective-permute-start | bytes 786440 | tf_op jit(solution)/shard_map/ppermute | solution.py:22
  190.1 2.7 %collective-permute-start.17 = (f32[8]{0:T(128)S(1)}, f32[8]{0:T(128)S(1)}, u32[]{:S(2)}, u32[]{:S(2)}) collective-permute-start(f32[8]{0:T(128)S(1)} %maximum_add_fusion.2), channel_id=1, source_target_pairs={{0,1},{1,0},{2,3},{3,2},{4,5},{5,4},{6,7},{7,6},{8,9},{9,8},{10,11... | collective-permute-start | bytes 104 | tf_op jit(solution)/shard_map/ppermute | solution.py:22
  192.8 2.4 %collective-permute-start.18 = (f32[8]{0:T(128)S(1)}, f32[8]{0:T(128)S(1)}, u32[]{:S(2)}, u32[]{:S(2)}) collective-permute-start(f32[8]{0:T(128)S(1)} %add.145), channel_id=1, source_target_pairs={{0,2},{2,0},{4,6},{6,4},{1,3},{3,1},{5,7},{7,5},{8,10},{10,8},{12,... | collective-permute-start | bytes 104 | tf_op jit(solution)/shard_map/ppermute | solution.py:22
  195.2 3.9 %collective-permute-start.19 = (f32[8]{0:T(128)S(1)}, f32[8]{0:T(128)S(1)}, u32[]{:S(2)}, u32[]{:S(2)}) collective-permute-start(f32[8]{0:T(128)S(1)} %add.146), channel_id=1, source_target_pairs={{0,4},{2,6},{4,0},{6,2},{1,5},{3,7},{5,1},{7,3},{8,12},{10,14},{12... | collective-permute-start | bytes 104 | tf_op jit(solution)/shard_map/ppermute | solution.py:22
  200.5 4.7 %collective-permute-start.21 = (bf16[128,256]{1,0:T(8,128)(2,1)S(1)}, bf16[128,256]{1,0:T(8,128)(2,1)S(1)}, u32[]{:S(2)}, u32[]{:S(2)}) collective-permute-start(bf16[128,256]{1,0:T(8,128)(2,1)S(1)} %dynamic-slice_convert_fusion), channel_id=1, source_target_pairs={{0,128},{128,0},{1,129},{129,1},{2,130},{130,2},{3,131},{131,3},{4... | collective-permute-start | bytes 196616 | tf_op jit(solution)/shard_map/ppermute | solution.py:22
  221.0 4.8 %collective-permute-start.22 = (bf16[128,256]{1,0:T(8,128)(2,1)S(1)}, bf16[128,256]{1,0:T(8,128)(2,1)S(1)}, u32[]{:S(2)}, u32[]{:S(2)}) collective-permute-start(bf16[128,256]{1,0:T(8,128)(2,1)S(1)} %fusion.21), channel_id=1, source_target_pairs={{0,128},{128,0},{1,129},{129,1},{2,130},{130,2},{3,131},{131,3},{4... | collective-permute-start | bytes 196616 | tf_op jit(solution)/shard_map/ppermute | solution.py:22
  225.8 8.5 %collective-permute-start.23 = (bf16[256,256]{1,0:T(8,128)(2,1)S(1)}, bf16[256,256]{1,0:T(8,128)(2,1)S(1)}, u32[]{:S(2)}, u32[]{:S(2)}) collective-permute-start(bf16[256,256]{1,0:T(8,128)(2,1)S(1)} %bitcast.77), channel_id=1, source_target_pairs={{0,8},{8,0},{1,9},{9,1},{2,10},{10,2},{3,11},{11,3},{4,12},{12,4},... | collective-permute-start | bytes 393224 | tf_op jit(solution)/shard_map/ppermute | solution.py:22

commit v2 on v1

v2 whole, which is shorter than its diff:
```python
import functools
import math

import jax
import jax.numpy as jnp
from jax import lax
from jax.experimental import pallas as pl
from jax.experimental.pallas import tpu as pltpu
from jax.sharding import Mesh
from jax.sharding import PartitionSpec as P

V = 2048
O = 512
NAUX = 128
ITERS = 3
AUX = ("yh", "z", "c")
VIR = ("x", "yl")
PLANE = ("x", "yl", "yh")
SCALE = math.sqrt(4.0 * V * O / NAUX)
BF, F32 = jnp.bfloat16, jnp.float32
ROWS, COLS, GROWS = 128, 256, 16
PIECE = ROWS + GROWS


def sds(*shape, dtype=F32):
    return jax.ShapeDtypeStruct(shape, dtype)


def whole(*shape):
    return pl.BlockSpec(shape, lambda i, s: (0,) * len(shape))


def kernel(body, name, inputs, outputs, scratch=(), limit=16, flops=0):
    specs = [
        whole(*shape) if index is None else pl.BlockSpec(shape, index)
        for shape, index in inputs
    ]
    moved = sum(math.prod(o.shape) * o.dtype.itemsize for o in outputs)
    moved += sum(2 * math.prod(shape) for shape, _ in inputs)
    return pl.pallas_call(
        body,
        out_shape=list(outputs),
        grid_spec=pltpu.PrefetchScalarGridSpec(
            num_scalar_prefetch=1,
            grid=(1,),
            in_specs=specs,
            out_specs=[whole(*o.shape) for o in outputs],
            scratch_shapes=list(scratch),
        ),
        compiler_params=pltpu.CompilerParams(vmem_limit_bytes=limit << 20),
        cost_estimate=pl.CostEstimate(
            flops=flops, bytes_accessed=moved, transcendentals=0
        ),
        name=name,
    )


def at(index, size):
    return pl.ds(pl.multiple_of(index * size, size), size)


def fill(msg, body, sums, first):
    g = jnp.sum(sums, axis=1, keepdims=True)
    high = g.astype(BF)
    low = (g - high.astype(F32)).astype(BF)
    n = sums.shape[0]
    block = jnp.concatenate(
        [jnp.broadcast_to(high, (n, 128)), jnp.broadcast_to(low, (n, 128))], axis=1
    )
    for p in range(16):
        msg[p, :ROWS, :] = body
        if n == GROWS:
            msg[p, ROWS:, :] = block
        else:
            msg[p, ROWS:, :] = first(block)


def start_body(s, rhs, ev, eo, ov, msg, keep):
    c, yh = s[0], s[1]
    u = (rhs[...] / (ev[...] - eo[...])).astype(BF)
    keep[...] = u
    wide = u.astype(F32)
    rows = [
        jnp.sum(ov[q].astype(F32) * wide, axis=0, keepdims=True) for q in range(4)
    ]
    sums = jnp.concatenate([r[:, :COLS] + r[:, COLS:] for r in rows], axis=0)
    sums = jnp.concatenate([sums, jnp.zeros((4, COLS), F32)], axis=0)
    zero = jnp.zeros_like(sums)
    sums = jnp.concatenate(
        [jnp.where(yh == 0, sums, zero), jnp.where(yh == 0, zero, sums)], axis=0
    )
    fill(msg, keep[at(yh, ROWS), at(c, COLS)], sums, None)


def pack_body(s, ov, ov2, ov8, out):
    c, yh = s[0], s[1]
    for k, ref in enumerate((ov, ov2)):
        for q in range(4):
            ov8[k * 4 + q] = ref[q, :, at(c, COLS)]
            out[k * 4 + q] = ref[q, at(1 - yh, ROWS), at(c, COLS)]


def main_body(s, v1, v2, o1, o2, u, keep, send, gown, full, zs, gs):
    c, yh = s[0], s[1]
    g = jnp.zeros((GROWS, COLS), F32)
    for p in range(16):
        full[p * ROWS : (p + 1) * ROWS, :] = u[p, :ROWS, :]
        g = g + u[p, ROWS:, :].astype(F32)
    gs[...] = g[:, :128] + g[:, 128:]
    gown[...] = gs[at(yh, 8), :]
    for k, v in enumerate((v1, v2)):
        z = jnp.dot(
            v[...].reshape(4 * 256, V), full[...], preferred_element_type=F32
        ).astype(BF)
        for q in range(4):
            zs[:, (k * 4 + q) * 256 : (k * 4 + q + 1) * 256] = z[q * 256 : (q + 1) * 256]
    a = jnp.zeros((256, COLS), F32)
    b = jnp.zeros((256, COLS), F32)
    for k, o in enumerate((o1, o2)):
        for q in range(4):
            zq = zs[:, (k * 4 + q) * 256 : (k * 4 + q + 1) * 256]
            a += jnp.dot(zq, o[q, :, at(c, COLS)], preferred_element_type=F32)
            b += jnp.dot(zq, o[q, :, at(1 - c, COLS)], preferred_element_type=F32)
    keep[...] = a
    send[...] = b


def pair_body(s, keep, got, gown, gsw, fit, ov8, mine, other, tot):
    yh = s[1]
    g = gown[...] + jnp.concatenate([gsw[4:8, :], gsw[0:4, :]], axis=0)
    w = SCALE * fit[...] - 4.0 * g
    for h in range(2):
        lanes = slice(h * 128, (h + 1) * 128)
        acc = keep[:, lanes] + got[:, lanes]
        for q in range(8):
            acc += ov8[q, :, lanes].astype(F32) * w[q : q + 1, :]
        tot[:, lanes] = acc
    mine[...] = tot[at(yh, ROWS), :]
    other[...] = tot[at(1 - yh, ROWS), :].astype(BF)


def wide_body(s, mine, recv, out):
    total = (mine[...] + recv[...].astype(F32)).astype(BF)
    for p in range(8):
        out[p] = total


def updated(zm, rhs, ev, eo):
    share = zm[0].astype(F32)
    for p in range(1, 8):
        share += zm[p].astype(F32)
    return (rhs[...] + share) / (ev[...] - eo[...])


def update_body(s, zm, rhs, ev, eo, own, oth, msg, sums):
    yh = s[1]
    u = updated(zm, rhs, ev, eo).astype(BF)
    wide = u.astype(F32)
    for ref, first in ((own, yh), (oth, 1 - yh)):
        rows = [
            jnp.sum(ref[q].astype(F32) * wide, axis=0, keepdims=True) for q in range(8)
        ]
        sums[at(first, 8), :] = jnp.concatenate(rows, axis=0)
    fill(msg, u, sums[...], None)


def last_body(s, zm, rhs, ev, eo, out):
    out[...] = updated(zm, rhs, ev, eo)


def join_body(s, w, wy, wc, wyc, out):
    c, yh = s[0], s[1]
    out[at(yh, ROWS), at(c, COLS)] = w[...]
    out[at(1 - yh, ROWS), at(c, COLS)] = wy[...]
    out[at(yh, ROWS), at(1 - c, COLS)] = wc[...]
    out[at(1 - yh, ROWS), at(1 - c, COLS)] = wyc[...]


def swap(value, axis):
    return lax.ppermute(value, axis, [(0, 1), (1, 0)])


def quarter(i, s):
    return (s[1], s[0])


def local(b_ov, b_vv, b_oo, rhs, fit_pert, eps_vir, eps_occ):
    s = jnp.stack([lax.axis_index("c"), lax.axis_index("yh")]).astype(jnp.int32)
    ev, eo = eps_vir[:, None], eps_occ[None, :]
    msg = kernel(
        start_body,
        "start",
        [((256, O), None), ((256, 1), None), ((1, O), None), ((4, 256, O), None)],
        [sds(16, PIECE, COLS, dtype=BF)],
        [pltpu.VMEM((256, O), BF)],
    )(s, rhs, ev, eo, b_ov)[0]
    vv2, oo2, ov2 = swap(b_vv, "c"), swap(b_oo, "c"), swap(b_ov, "c")
    fit = jnp.concatenate([fit_pert, swap(fit_pert, "c")])
    fit = jnp.broadcast_to(fit[:, None], (8, 128))
    ov8, ov_out = kernel(
        pack_body,
        "pack",
        [((4, 256, O), None)] * 2,
        [sds(8, 256, COLS, dtype=BF), sds(8, ROWS, COLS, dtype=BF)],
    )(s, b_ov, ov2)
    ov_in = None
    denominators = [
        ((ROWS, COLS), quarter),
        ((ROWS, 1), lambda i, s: (s[1], 0)),
        ((1, COLS), lambda i, s: (0, s[0])),
    ]
    for step in range(ITERS):
        msg = lax.all_to_all(msg, PLANE, 0, 0, tiled=True)
        if ov_in is None:
            ov_in = swap(ov_out, "yh")
        half_oo = ((4, 256, O), lambda i, s: (0, s[0], 0))
        keep, send, gown = kernel(
            main_body,
            "main",
            [((4, 256, V), None)] * 2 + [half_oo] * 2 + [((16, PIECE, COLS), None)],
            [sds(256, COLS), sds(256, COLS), sds(8, 128)],
            [
                pltpu.VMEM((V, COLS), BF),
                pltpu.VMEM((256, V), BF),
                pltpu.VMEM((GROWS, 128), F32),
            ],
            limit=32,
            flops=2 * 8 * 256 * 256 * (V + O),
        )(s, b_vv, vv2, b_oo, oo2, msg)
        mine, other = kernel(
            pair_body,
            "pair",
            [((256, COLS), None)] * 2 + [((8, 128), None)] * 3 + [((8, 256, COLS), None)],
            [sds(ROWS, COLS), sds(ROWS, COLS, dtype=BF)],
            [pltpu.VMEM((256, COLS), F32)],
        )(s, keep, swap(send, "c"), gown, swap(gown, "c"), fit, ov8)
        zm = kernel(
            wide_body,
            "wide",
            [((ROWS, COLS), None)] * 2,
            [sds(8, ROWS, COLS, dtype=BF)],
        )(s, mine, swap(other, "yh"))[0]
        zm = lax.all_to_all(zm, "z", 0, 0, tiled=True)
        if step < ITERS - 1:
            msg = kernel(
                update_body,
                "update",
                [((8, ROWS, COLS), None), *denominators]
                + [((8, ROWS, COLS), lambda i, s: (0, s[1], 0)), ((8, ROWS, COLS), None)],
                [sds(16, PIECE, COLS, dtype=BF)],
                [pltpu.VMEM((GROWS, COLS), F32)],
            )(s, zm, rhs, ev, eo, ov8, ov_in)[0]
    w = kernel(
        last_body,
        "last",
        [((8, ROWS, COLS), None), *denominators],
        [sds(ROWS, COLS)],
    )(s, zm, rhs, ev, eo)[0]
    wy, wc = swap(w, "yh"), swap(w, "c")
    return kernel(
        join_body, "join", [((ROWS, COLS), None)] * 4, [sds(256, O)]
    )(s, w, wy, wc, swap(wy, "c"))[0]


def solution(mesh):
    split = Mesh(mesh.devices.reshape(2, 8, 2, 4, 2), ("yh", "z", "c", "x", "yl"))
    placed = (
        P(AUX, VIR, None),
        P(AUX, VIR, None),
        P(AUX, None, None),
        P(VIR, None),
        P(AUX),
        P(VIR),
        P(),
    )
    return jax.shard_map(
        local, mesh=split, in_specs=placed, out_specs=P(VIR, None), check_vma=False
    )
```

time: 236 us -> 208 us (0.88)
  matrix products: 33.2 us -> 0 us
  Pallas kernels: 0 us -> 31.7 us
  blocking collectives: 87 us -> 74.5 us
  other arithmetic: 11.6 us -> 0.15 us
    dot_general x6 -> x0, matrix products: 33.2 us -> none  [local(): jnp.einsum('qaj,qji->ai', mixed.astype(BF), oos, preferred_element_type=F32)]
    pallas_call x0 -> x15, Pallas kernels: none -> 31.7 us  [the longest x3 18.1 us: local(): kernel(main_body, 'main', [((4, 256, V), None)] * 2 + [half_oo] * 2 + [((...]
    all_to_all x5 -> x4, blocking collectives: 87 us -> 74.5 us  [the longest x2 37.3 us: local(): msg = lax.all_to_all(msg, PLANE, 0, 0, tiled=True)]
    all_to_all x1 -> x2, starting transfers between devices: 5.1 us -> 13.4 us  [the longest x1 8.18 us: local(): zm = lax.all_to_all(zm, 'z', 0, 0, tiled=True)]
    ppermute x24 -> x17, waiting for transfers between devices: 34.1 us -> 25.9 us  [swap(): return lax.ppermute(value, axis, [(0, 1), (1, 0)])]
    dynamic_slice x7 -> x0, local copies, waits for them, and re-layouts: 7.55 us -> none  [half(): return lax.dynamic_slice_in_dim(value, which * size, size, dim)]
    ppermute x24 -> x17, starting transfers between devices: 39.1 us -> 32 us  [swap(): return lax.ppermute(value, axis, [(0, 1), (1, 0)])]
    unnamed x8 -> x34, local copies, waits for them, and re-layouts: 2.03 us -> 8.83 us
  transfers between devices with their start and end apart: 25 -> 19, of which waited for: 15 -> 11; matrix products, arithmetic and copies ran while one was open for 19% -> 0% of each run, Pallas kernels for 0% -> 5%
where the time goes in v2:
time: 208 us
  blocking collectives  74.5 us (36%)
  waiting for transfers between devices  46 us (22%)
  starting transfers between devices  45.4 us (22%)
  Pallas kernels  31.7 us (15%)
  local copies, waits for them, and re-layouts  9.71 us (5%)
    all_to_all x2, blocking collectives, local(): msg = lax.all_to_all(msg, PLANE, 0, 0, tiled=True)  37.3 us
    all_to_all x2, blocking collectives, local(): zm = lax.all_to_all(zm, 'z', 0, 0, tiled=True)  37.2 us
    ppermute x17, starting transfers between devices, swap(): return lax.ppermute(value, axis, [(0, 1), (1, 0)])  32 us
    ppermute x17, waiting for transfers between devices, swap(): return lax.ppermute(value, axis, [(0, 1), (1, 0)])  25.9 us
    all_to_all x1, waiting for transfers between devices, local(): msg = lax.all_to_all(msg, PLANE, 0, 0, tiled=True)  18.1 us
    pallas_call x3, Pallas kernels, local(): kernel(main_body, 'main', [((4, 256, V), None)] * 2 + [half_oo] * 2 + [((...  18.1 us
    unnamed x34, local copies, waits for them, and re-layouts  8.83 us
    all_to_all x1, starting transfers between devices, local(): zm = lax.all_to_all(zm, 'z', 0, 0, tiled=True)  8.18 us
  transfers between devices with their start and end apart: 19, of which 11 were waited for; matrix products, arithmetic and copies ran while one was open for 0% of the time, Pallas kernels for 5%

profile of v2, /device:TPU:1, one launch (start us, length us, event | category | flops | bytes accessed | tf_op | source)
XLA Modules:
  0.0 207.7 jit_solution(4407304881844580423)
XLA Ops:
  0.0 3.2 %collective-permute-start = (bf16[4,256,2048]{2,1,0:T(8,128)(2,1)}, bf16[4,256,2048]{2,1,0:T(8,128)(2,1)}, u32[]{:S(2)}, u32[]{:S(2)}) collective-permute-start(bf16[4,256,2048]{2,1,0:T(8,128)(2,1)} %v1.5), channel_id=1, source_target_pairs={{0,8},{8,0},{1,9},{9,1},{2,10},{10,2},{3,11},{11,3},{4,12},{12,4},... | collective-permute-start | bytes 12582920 | tf_op jit(solution)/shard_map/ppermute | solution.py:180
  4.1 1.0 copy-done.3
  5.1 1.2 copy-done.6
  7.1 2.2 %start.1 = bf16[16,144,256]{2,1,0:T(8,128)(2,1)} custom-call(s32[2]{0:T(128)S(1)} %pad_add_fusion.s, f32[256,512]{1,0:T(8,128)S(1)} %copy-done.3, f32[256,1]{1,0:T(8,128)S(1)} %copy.8.ev, f32[1,512]{1,0:T(1,128)S(1)} %bitcast.4, bf16[4,256,512]{2,1,0:T(8,128)(2,1)S(1)} %copy-done.6), custom_call_target="tpu_custom_call" | custom-call | bytes 2491904 | tf_op jit(solution)/shard_map/start/pallas_call | solution.py:190
  9.3 5.2 %all-to-all-start = ((bf16[16,144,256]{2,1,0:T(8,128)(2,1)}), bf16[16,144,256]{2,1,0:T(8,128)(2,1)}, u32[]{:S(2)}, u32[]{:S(2)}) async-start(bf16[16,144,256]{2,1,0:T(8,128)(2,1)} %start.1), calls=%async_computation | async-start | bytes 2359296 | tf_op jit(solution)/shard_map/all_to_all | solution.py:213
  15.4 18.1 %all-to-all-done.u = bf16[16,144,256]{2,1,0:T(8,128)(2,1)} async-done(((bf16[16,144,256]{2,1,0:T(8,128)(2,1)}), bf16[16,144,256]{2,1,0:T(8,128)(2,1)}, u32[]{:S(2)}, u32[]{:S(2)}) %all-to-all-start) | async-done | bytes 1179680 | tf_op jit(solution)/shard_map/all_to_all | solution.py:213
  33.5 2.2 %copy-done = bf16[4,256,2048]{2,1,0:T(8,128)(2,1)S(1)} copy-done((bf16[4,256,2048]{2,1,0:T(8,128)(2,1)S(1)}, bf16[4,256,2048]{2,1,0:T(8,128)(2,1)}, u32[]{:S(2)}) %copy-start) | copy-done | bytes 4194328
  35.7 6.3 %main.3 = (f32[256,256]{1,0:T(8,128)S(1)}, f32[256,256]{1,0:T(8,128)S(1)}, f32[8,128]{1,0:T(8,128)S(1)}) custom-call(s32[2]{0:T(128)S(1)} %pad_add_fusion.s, bf16[4,256,2048]{2,1,0:T(8,128)(2,1)S(1)} %copy-done, bf16[4,256,2048]{2,1,0:T(8,128)(2,1)} %collective-permute-done.v2, bf16[4,512,512]{2,1,0:T(8,128)(2,1)S(1)} %copy-done.2, ...), custom_call_target="tpu_custom_call" | custom-call | flops 2684354560 | bytes 12193792 | tf_op jit(solution)/shard_map/main/pallas_call | solution.py:217
  42.0 2.7 %collective-permute-start.2 = (f32[256,256]{1,0:T(8,128)S(1)}, f32[256,256]{1,0:T(8,128)S(1)}, u32[]{:S(2)}, u32[]{:S(2)}) collective-permute-start(f32[256,256]{1,0:T(8,128)S(1)} %get-tuple-element.23), channel_id=1, source_target_pairs={{0,8},{8,0},{1,9},{9,1},{2,10},{10,2},{3,11},{11,3},{4,12},{12,4},... | collective-permute-start | bytes 786440 | tf_op jit(solution)/shard_map/ppermute | solution.py:180
  45.9 1.9 pack.1
  48.7 2.7 %collective-permute-start.6 = (bf16[128,256]{1,0:T(8,128)(2,1)S(1)}, bf16[128,256]{1,0:T(8,128)(2,1)S(1)}, u32[]{:S(2)}, u32[]{:S(2)}) collective-permute-start(bf16[128,256]{1,0:T(8,128)(2,1)S(1)} %get-tuple-element.27), channel_id=1, source_target_pairs={{0,128},{128,0},{1,129},{129,1},{2,130},{130,2},{3,131},{131,3},{4... | collective-permute-start | bytes 196616 | tf_op jit(solution)/shard_map/ppermute | solution.py:180
  51.4 2.0 collective-permute-done.6.recv
  54.8 8.2 %all-to-all-start.1 = ((bf16[8,128,256]{2,1,0:T(8,128)(2,1)}), bf16[8,128,256]{2,1,0:T(8,128)(2,1)}, u32[]{:S(2)}, u32[]{:S(2)}) async-start(bf16[8,128,256]{2,1,0:T(8,128)(2,1)} %copy-done.9), calls=%async_computation.1 | async-start | bytes 1048576 | tf_op jit(solution)/shard_map/all_to_all | solution.py:243
  63.0 2.6 %collective-permute-start.7 = (bf16[8,128,256]{2,1,0:T(8,128)(2,1)}, bf16[8,128,256]{2,1,0:T(8,128)(2,1)S(1)}, u32[]{:S(2)}, u32[]{:S(2)}) collective-permute-start(bf16[8,128,256]{2,1,0:T(8,128)(2,1)} %copy-done.15), channel_id=1, source_target_pairs={{0,128},{128,0},{1,129},{129,1},{2,130},{130,2},{3,131},{131,3},{4... | collective-permute-start | bytes 1572872 | tf_op jit(solution)/shard_map/ppermute | solution.py:180
  65.6 10.8 %collective-permute-done.7.oth = bf16[8,128,256]{2,1,0:T(8,128)(2,1)S(1)} collective-permute-done((bf16[8,128,256]{2,1,0:T(8,128)(2,1)}, bf16[8,128,256]{2,1,0:T(8,128)(2,1)S(1)}, u32[]{:S(2)}, u32[]{:S(2)}) %collective-permute-start.7) | collective-permute-done | bytes 524320 | tf_op jit(solution)/shard_map/ppermute | solution.py:180
  77.2 1.9 all-to-all-done.1.zm
  81.2 2.3 %update.2 = bf16[16,144,256]{2,1,0:T(8,128)(2,1)S(1)} custom-call(s32[2]{0:T(128)S(1)} %pad_add_fusion.s, bf16[8,128,256]{2,1,0:T(8,128)(2,1)} %all-to-all-done.1.zm, f32[256,512]{1,0:T(8,128)S(1)} %copy-done.4, f32[256,1]{1,0:T(8,128)S(1)} %copy.8.ev, f32[1,512]{1,0:T(1,128)S(1)} %bitcast.5, bf16[8,256,256]{2,1,0:T(8,128)(2,1)S(1)} %get-tuple-element.25.ov8.own, ...), custom_call_target="tpu_custom_call" | custom-call | bytes 2818816 | tf_op jit(solution)/shard_map/update/pallas_call | solution.py:245
  83.5 19.6 %all_to_all.30.u = bf16[16,144,256]{2,1,0:T(8,128)(2,1)S(1)} all-to-all(bf16[16,144,256]{2,1,0:T(8,128)(2,1)S(1)} %update.2), channel_id=1, replica_groups=mesh['yh'=2,'z'=8,'c'=2,'x'=4,'yl'=2] {'x','yl','yh'}, dimensions={0} | all-to-all | bytes 2359296 | tf_op jit(solution)/shard_map/all_to_all | solution.py:213
  103.1 5.9 %main.4 = (f32[256,256]{1,0:T(8,128)S(1)}, f32[256,256]{1,0:T(8,128)S(1)}, f32[8,128]{1,0:T(8,128)S(1)}) custom-call(s32[2]{0:T(128)S(1)} %pad_add_fusion.s, bf16[4,256,2048]{2,1,0:T(8,128)(2,1)S(1)} %copy-done.1, bf16[4,256,2048]{2,1,0:T(8,128)(2,1)} %collective-permute-done.v2, bf16[4,512,512]{2,1,0:T(8,128)(2,1)S(1)} %copy-done.2, ...), custom_call_target="tpu_custom_call" | custom-call | flops 2684354560 | bytes 12193792 | tf_op jit(solution)/shard_map/main/pallas_call | solution.py:217
  109.0 4.0 %collective-permute-start.8 = (f32[256,256]{1,0:T(8,128)S(1)}, f32[256,256]{1,0:T(8,128)S(1)}, u32[]{:S(2)}, u32[]{:S(2)}) collective-permute-start(f32[256,256]{1,0:T(8,128)S(1)} %get-tuple-element.30), channel_id=1, source_target_pairs={{0,8},{8,0},{1,9},{9,1},{2,10},{10,2},{3,11},{11,3},{4,12},{12,4},... | collective-permute-start | bytes 786440 | tf_op jit(solution)/shard_map/ppermute | solution.py:180
  113.1 1.1 collective-permute-done.9.gsw
  115.8 4.2 %collective-permute-done.10.recv = bf16[128,256]{1,0:T(8,128)(2,1)S(1)} collective-permute-done((bf16[128,256]{1,0:T(8,128)(2,1)S(1)}, bf16[128,256]{1,0:T(8,128)(2,1)S(1)}, u32[]{:S(2)}, u32[]{:S(2)}) %collective-permute-start.10) | collective-permute-done | bytes 65568 | tf_op jit(solution)/shard_map/ppermute | solution.py:180
  120.5 19.1 %all_to_all.31.zm = bf16[8,128,256]{2,1,0:T(8,128)(2,1)S(1)} all-to-all(bf16[8,128,256]{2,1,0:T(8,128)(2,1)S(1)} %wide.4), channel_id=1, replica_groups=mesh['yh'=2,'z'=8,'c'=2,'x'=4,'yl'=2] {'z'}, dimensions={0} | all-to-all | bytes 1048576 | tf_op jit(solution)/shard_map/all_to_all | solution.py:243
  140.7 17.7 %all_to_all.32.u = bf16[16,144,256]{2,1,0:T(8,128)(2,1)S(1)} all-to-all(bf16[16,144,256]{2,1,0:T(8,128)(2,1)S(1)} %update.3), channel_id=1, replica_groups=mesh['yh'=2,'z'=8,'c'=2,'x'=4,'yl'=2] {'x','yl','yh'}, dimensions={0} | all-to-all | bytes 2359296 | tf_op jit(solution)/shard_map/all_to_all | solution.py:213
  158.4 5.9 %main.5 = (f32[256,256]{1,0:T(8,128)S(1)}, f32[256,256]{1,0:T(8,128)S(1)}, f32[8,128]{1,0:T(8,128)S(1)}) custom-call(s32[2]{0:T(128)S(1)} %pad_add_fusion.s, bf16[4,256,2048]{2,1,0:T(8,128)(2,1)S(1)} %copy-done.1, bf16[4,256,2048]{2,1,0:T(8,128)(2,1)} %collective-permute-done.v2, bf16[4,512,512]{2,1,0:T(8,128)(2,1)S(1)} %copy-done.2, ...), custom_call_target="tpu_custom_call" | custom-call | flops 2684354560 | bytes 12193792 | tf_op jit(solution)/shard_map/main/pallas_call | solution.py:217
  164.3 4.9 %collective-permute-start.11 = (f32[256,256]{1,0:T(8,128)S(1)}, f32[256,256]{1,0:T(8,128)S(1)}, u32[]{:S(2)}, u32[]{:S(2)}) collective-permute-start(f32[256,256]{1,0:T(8,128)S(1)} %get-tuple-element.35), channel_id=1, source_target_pairs={{0,8},{8,0},{1,9},{9,1},{2,10},{10,2},{3,11},{11,3},{4,12},{12,4},... | collective-permute-start | bytes 786440 | tf_op jit(solution)/shard_map/ppermute | solution.py:180
  169.3 1.1 collective-permute-done.12.gsw
  171.7 4.2 %collective-permute-done.13.recv = bf16[128,256]{1,0:T(8,128)(2,1)S(1)} collective-permute-done((bf16[128,256]{1,0:T(8,128)(2,1)S(1)}, bf16[128,256]{1,0:T(8,128)(2,1)S(1)}, u32[]{:S(2)}, u32[]{:S(2)}) %collective-permute-start.13) | collective-permute-done | bytes 65568 | tf_op jit(solution)/shard_map/ppermute | solution.py:180
  176.5 18.1 %all_to_all.33.zm = bf16[8,128,256]{2,1,0:T(8,128)(2,1)S(1)} all-to-all(bf16[8,128,256]{2,1,0:T(8,128)(2,1)S(1)} %wide.5), channel_id=1, replica_groups=mesh['yh'=2,'z'=8,'c'=2,'x'=4,'yl'=2] {'z'}, dimensions={0} | all-to-all | bytes 1048576 | tf_op jit(solution)/shard_map/all_to_all | solution.py:243
  195.7 3.8 %collective-permute-start.15 = (f32[128,256]{1,0:T(8,128)S(1)}, f32[128,256]{1,0:T(8,128)S(1)}, u32[]{:S(2)}, u32[]{:S(2)}) collective-permute-start(f32[128,256]{1,0:T(8,128)S(1)} %last.1.w), channel_id=1, source_target_pairs={{0,8},{8,0},{1,9},{9,1},{2,10},{10,2},{3,11},{11,3},{4,12},{12,4},... | collective-permute-start | bytes 393224 | tf_op jit(solution)/shard_map/ppermute | solution.py:180
  200.6 4.7 %collective-permute-start.16 = (f32[128,256]{1,0:T(8,128)S(1)}, f32[128,256]{1,0:T(8,128)S(1)}, u32[]{:S(2)}, u32[]{:S(2)}) collective-permute-start(f32[128,256]{1,0:T(8,128)S(1)} %collective-permute-done.14.wy), channel_id=1, source_target_pairs={{0,8},{8,0},{1,9},{9,1},{2,10},{10,2},{3,11},{11,3},{4,12},{12,4},... | collective-permute-start | bytes 393224 | tf_op jit(solution)/shard_map/ppermute | solution.py:180
  206.3 1.4 join.1
  (63 shorter events, 17.3 us)
Async XLA Ops:
  0.0 33.5 %collective-permute-start = (bf16[4,256,2048]{2,1,0:T(8,128)(2,1)}, bf16[4,256,2048]{2,1,0:T(8,128)(2,1)}, u32[]{:S(2)}, u32[]{:S(2)}) collective-permute-start(bf16[4,256,2048]{2,1,0:T(8,128)(2,1)} %v1.5), channel_id=1, source_target_pairs={{0,8},{8,0},{1,9},{9,1},{2,10},{10,2},{3,11},{11,3},{4,12},{12,4},... | collective-permute-start | bytes 12582920 | tf_op jit(solution)/shard_map/ppermute | solution.py:180
  3.2 30.3 %collective-permute-start.1 = (bf16[4,512,512]{2,1,0:T(8,128)(2,1)}, bf16[4,512,512]{2,1,0:T(8,128)(2,1)}, u32[]{:S(2)}, u32[]{:S(2)}) collective-permute-start(bf16[4,512,512]{2,1,0:T(8,128)(2,1)} %o1.5), channel_id=1, source_target_pairs={{0,8},{8,0},{1,9},{9,1},{2,10},{10,2},{3,11},{11,3},{4,12},{12,4},... | collective-permute-start | bytes 6291464 | tf_op jit(solution)/shard_map/ppermute | solution.py:180
  4.1 1.0 copy-start.3
  5.1 1.2 copy-start.6
  7.0 7.4 %copy-start.7 = (bf16[4,256,512]{2,1,0:T(8,128)(2,1)S(1)}, bf16[4,256,512]{2,1,0:T(8,128)(2,1)}, u32[]{:S(2)}) copy-start(bf16[4,256,512]{2,1,0:T(8,128)(2,1)} %ov.3) | copy-start | bytes 3145732
  9.3 24.2 %copy-start.2 = (bf16[4,512,512]{2,1,0:T(8,128)(2,1)S(1)}, bf16[4,512,512]{2,1,0:T(8,128)(2,1)}, u32[]{:S(2)}) copy-start(bf16[4,512,512]{2,1,0:T(8,128)(2,1)} %o1.5) | copy-start | bytes 6291460
  9.3 35.4 %copy-start.16 = (f32[4]{0:T(128)S(1)}, f32[4]{0:T(128)}, u32[]{:S(2)}) copy-start(f32[4]{0:T(128)} %param.11) | copy-start | bytes 52
  9.3 24.2 %all-to-all-start = ((bf16[16,144,256]{2,1,0:T(8,128)(2,1)}), bf16[16,144,256]{2,1,0:T(8,128)(2,1)}, u32[]{:S(2)}, u32[]{:S(2)}) async-start(bf16[16,144,256]{2,1,0:T(8,128)(2,1)} %start.1), calls=%async_computation | async-start | bytes 2359296 | tf_op jit(solution)/shard_map/all_to_all | solution.py:213
  14.5 31.4 %collective-permute-start.5 = (bf16[4,256,512]{2,1,0:T(8,128)(2,1)S(1)}, bf16[4,256,512]{2,1,0:T(8,128)(2,1)}, u32[]{:S(2)}, u32[]{:S(2)}) collective-permute-start(bf16[4,256,512]{2,1,0:T(8,128)(2,1)S(1)} %copy-done.7), channel_id=1, source_target_pairs={{0,8},{8,0},{1,9},{9,1},{2,10},{10,2},{3,11},{11,3},{4,12},{12,4},... | collective-permute-start | bytes 3145736 | tf_op jit(solution)/shard_map/ppermute | solution.py:180
  33.5 2.2 %copy-start = (bf16[4,256,2048]{2,1,0:T(8,128)(2,1)S(1)}, bf16[4,256,2048]{2,1,0:T(8,128)(2,1)}, u32[]{:S(2)}) copy-start(bf16[4,256,2048]{2,1,0:T(8,128)(2,1)} %v1.5) | copy-start | bytes 12582916
  35.7 10.2 %copy-start.8 = (bf16[4,256,512]{2,1,0:T(8,128)(2,1)S(1)}, bf16[4,256,512]{2,1,0:T(8,128)(2,1)}, u32[]{:S(2)}) copy-start(bf16[4,256,512]{2,1,0:T(8,128)(2,1)} %ov.3) | copy-start | bytes 3145732
  42.0 5.8 %collective-permute-start.2 = (f32[256,256]{1,0:T(8,128)S(1)}, f32[256,256]{1,0:T(8,128)S(1)}, u32[]{:S(2)}, u32[]{:S(2)}) collective-permute-start(f32[256,256]{1,0:T(8,128)S(1)} %get-tuple-element.23), channel_id=1, source_target_pairs={{0,8},{8,0},{1,9},{9,1},{2,10},{10,2},{3,11},{11,3},{4,12},{12,4},... | collective-permute-start | bytes 786440 | tf_op jit(solution)/shard_map/ppermute | solution.py:180
  44.7 1.2 collective-permute-start.4
  44.8 3.0 %collective-permute-start.3 = (f32[8,128]{1,0:T(8,128)S(1)}, f32[8,128]{1,0:T(8,128)S(1)}, u32[]{:S(2)}, u32[]{:S(2)}) collective-permute-start(f32[8,128]{1,0:T(8,128)S(1)} %get-tuple-element.24.gown), channel_id=1, source_target_pairs={{0,8},{8,0},{1,9},{9,1},{2,10},{10,2},{3,11},{11,3},{4,12},{12,4},... | collective-permute-start | bytes 12296 | tf_op jit(solution)/shard_map/ppermute | solution.py:180
  47.8 5.6 %copy-start.15 = (bf16[8,128,256]{2,1,0:T(8,128)(2,1)}, bf16[8,128,256]{2,1,0:T(8,128)(2,1)S(1)}, u32[]{:S(2)}) copy-start(bf16[8,128,256]{2,1,0:T(8,128)(2,1)S(1)} %get-tuple-element.28) | copy-start | bytes 1572868
  48.7 30.4 %copy-start.14 = (f32[512]{0:T(512)S(1)}, f32[512]{0:T(512)}, u32[]{:S(2)}) copy-start(f32[512]{0:T(512)} %param.13) | copy-start | bytes 6148
  48.7 4.7 %collective-permute-start.6 = (bf16[128,256]{1,0:T(8,128)(2,1)S(1)}, bf16[128,256]{1,0:T(8,128)(2,1)S(1)}, u32[]{:S(2)}, u32[]{:S(2)}) collective-permute-start(bf16[128,256]{1,0:T(8,128)(2,1)S(1)} %get-tuple-element.27), channel_id=1, source_target_pairs={{0,128},{128,0},{1,129},{129,1},{2,130},{130,2},{3,131},{131,3},{4... | collective-permute-start | bytes 196616 | tf_op jit(solution)/shard_map/ppermute | solution.py:180
  54.8 24.3 %all-to-all-start.1 = ((bf16[8,128,256]{2,1,0:T(8,128)(2,1)}), bf16[8,128,256]{2,1,0:T(8,128)(2,1)}, u32[]{:S(2)}, u32[]{:S(2)}) async-start(bf16[8,128,256]{2,1,0:T(8,128)(2,1)} %copy-done.9), calls=%async_computation.1 | async-start | bytes 1048576 | tf_op jit(solution)/shard_map/all_to_all | solution.py:243
  63.0 13.4 %collective-permute-start.7 = (bf16[8,128,256]{2,1,0:T(8,128)(2,1)}, bf16[8,128,256]{2,1,0:T(8,128)(2,1)S(1)}, u32[]{:S(2)}, u32[]{:S(2)}) collective-permute-start(bf16[8,128,256]{2,1,0:T(8,128)(2,1)} %copy-done.15), channel_id=1, source_target_pairs={{0,128},{128,0},{1,129},{129,1},{2,130},{130,2},{3,131},{131,3},{4... | collective-permute-start | bytes 1572872 | tf_op jit(solution)/shard_map/ppermute | solution.py:180
  79.1 1.0 copy-start.4
  81.2 21.9 %copy-start.1 = (bf16[4,256,2048]{2,1,0:T(8,128)(2,1)S(1)}, bf16[4,256,2048]{2,1,0:T(8,128)(2,1)}, u32[]{:S(2)}) copy-start(bf16[4,256,2048]{2,1,0:T(8,128)(2,1)} %v1.5) | copy-start | bytes 12582916
  109.0 5.2 %collective-permute-start.8 = (f32[256,256]{1,0:T(8,128)S(1)}, f32[256,256]{1,0:T(8,128)S(1)}, u32[]{:S(2)}, u32[]{:S(2)}) collective-permute-start(f32[256,256]{1,0:T(8,128)S(1)} %get-tuple-element.30), channel_id=1, source_target_pairs={{0,8},{8,0},{1,9},{9,1},{2,10},{10,2},{3,11},{11,3},{4,12},{12,4},... | collective-permute-start | bytes 786440 | tf_op jit(solution)/shard_map/ppermute | solution.py:180
  113.0 1.2 collective-permute-start.9
  115.0 24.6 %copy-start.5 = (f32[256,512]{1,0:T(8,128)S(1)}, f32[256,512]{1,0:T(8,128)}, u32[]{:S(2)}) copy-start(f32[256,512]{1,0:T(8,128)} %rhs.7) | copy-start | bytes 1572868
  115.0 24.6 %copy-start.12 = (bf16[8,128,256]{2,1,0:T(8,128)(2,1)S(1)}, bf16[8,128,256]{2,1,0:T(8,128)(2,1)}, u32[]{:S(2)}) copy-start(bf16[8,128,256]{2,1,0:T(8,128)(2,1)} %copy-done.10) | copy-start | bytes 1572868
  115.0 4.9 %collective-permute-start.10 = (bf16[128,256]{1,0:T(8,128)(2,1)S(1)}, bf16[128,256]{1,0:T(8,128)(2,1)S(1)}, u32[]{:S(2)}, u32[]{:S(2)}) collective-permute-start(bf16[128,256]{1,0:T(8,128)(2,1)S(1)} %get-tuple-element.33), channel_id=1, source_target_pairs={{0,128},{128,0},{1,129},{129,1},{2,130},{130,2},{3,131},{131,3},{4... | collective-permute-start | bytes 196616 | tf_op jit(solution)/shard_map/ppermute | solution.py:180
  164.3 6.1 %collective-permute-start.11 = (f32[256,256]{1,0:T(8,128)S(1)}, f32[256,256]{1,0:T(8,128)S(1)}, u32[]{:S(2)}, u32[]{:S(2)}) collective-permute-start(f32[256,256]{1,0:T(8,128)S(1)} %get-tuple-element.35), channel_id=1, source_target_pairs={{0,8},{8,0},{1,9},{9,1},{2,10},{10,2},{3,11},{11,3},{4,12},{12,4},... | collective-permute-start | bytes 786440 | tf_op jit(solution)/shard_map/ppermute | solution.py:180
  169.2 1.2 collective-permute-start.12
  171.2 4.7 %collective-permute-start.13 = (bf16[128,256]{1,0:T(8,128)(2,1)S(1)}, bf16[128,256]{1,0:T(8,128)(2,1)S(1)}, u32[]{:S(2)}, u32[]{:S(2)}) collective-permute-start(bf16[128,256]{1,0:T(8,128)(2,1)S(1)} %get-tuple-element.38), channel_id=1, source_target_pairs={{0,128},{128,0},{1,129},{129,1},{2,130},{130,2},{3,131},{131,3},{4... | collective-permute-start | bytes 196616 | tf_op jit(solution)/shard_map/ppermute | solution.py:180
  195.2 5.4 %collective-permute-start.14 = (f32[128,256]{1,0:T(8,128)S(1)}, f32[128,256]{1,0:T(8,128)S(1)}, u32[]{:S(2)}, u32[]{:S(2)}) collective-permute-start(f32[128,256]{1,0:T(8,128)S(1)} %last.1.w), channel_id=1, source_target_pairs={{0,128},{128,0},{1,129},{129,1},{2,130},{130,2},{3,131},{131,3},{4... | collective-permute-start | bytes 393224 | tf_op jit(solution)/shard_map/ppermute | solution.py:180
  195.7 9.6 %collective-permute-start.15 = (f32[128,256]{1,0:T(8,128)S(1)}, f32[128,256]{1,0:T(8,128)S(1)}, u32[]{:S(2)}, u32[]{:S(2)}) collective-permute-start(f32[128,256]{1,0:T(8,128)S(1)} %last.1.w), channel_id=1, source_target_pairs={{0,8},{8,0},{1,9},{9,1},{2,10},{10,2},{3,11},{11,3},{4,12},{12,4},... | collective-permute-start | bytes 393224 | tf_op jit(solution)/shard_map/ppermute | solution.py:180
  200.6 5.7 %collective-permute-start.16 = (f32[128,256]{1,0:T(8,128)S(1)}, f32[128,256]{1,0:T(8,128)S(1)}, u32[]{:S(2)}, u32[]{:S(2)}) collective-permute-start(f32[128,256]{1,0:T(8,128)S(1)} %collective-permute-done.14.wy), channel_id=1, source_target_pairs={{0,8},{8,0},{1,9},{9,1},{2,10},{10,2},{3,11},{11,3},{4,12},{12,4},... | collective-permute-start | bytes 393224 | tf_op jit(solution)/shard_map/ppermute | solution.py:180
  (4 other events, 3.3 us)

commit v3 on v1

v3 whole, which is shorter than its diff:
```python
import math

import jax
import jax.numpy as jnp
from jax import lax
from jax.experimental import pallas as pl
from jax.experimental.pallas import tpu as pltpu
from jax.sharding import Mesh
from jax.sharding import PartitionSpec as P

V = 2048
O = 512
NAUX = 128
ITERS = 3
AUX = ("yh", "z", "c")
VIR = ("x", "yl")
PLANE = ("x", "yl", "yh")
SCALE = math.sqrt(4.0 * V * O / NAUX)
BF, F32 = jnp.bfloat16, jnp.float32
ROWS, COLS, GROWS = 128, 256, 8
PIECE = ROWS + GROWS


def sds(*shape, dtype=F32):
    return jax.ShapeDtypeStruct(shape, dtype)


def kernel(body, name, outputs, scratch=(), limit=8, flops=0, scalars=1):
    def call(*args):
        moved = sum(math.prod(a.shape) * a.dtype.itemsize for a in (*args, *outputs))
        return pl.pallas_call(
            body,
            out_shape=list(outputs),
            in_specs=[
                pl.BlockSpec(memory_space=pltpu.SMEM if k < scalars else pltpu.VMEM)
                for k in range(len(args))
            ],
            out_specs=[pl.BlockSpec(memory_space=pltpu.VMEM) for _ in outputs],
            scratch_shapes=list(scratch),
            compiler_params=pltpu.CompilerParams(vmem_limit_bytes=limit << 20),
            cost_estimate=pl.CostEstimate(
                flops=flops, bytes_accessed=moved, transcendentals=0
            ),
            name=name,
        )(*args)

    return call


def at(index, size):
    return pl.ds(pl.multiple_of(index * size, size), size)


def spread(sums):
    g = jnp.sum(sums, axis=1, keepdims=True)
    high = g.astype(BF)
    low = (g - high.astype(F32)).astype(BF)
    lane = lax.broadcasted_iota(jnp.int32, (GROWS, 128), 1)
    wide = (GROWS, 128)
    return jnp.where(
        lane % 2 == 0,
        jnp.broadcast_to(high.astype(F32), wide),
        jnp.broadcast_to(low.astype(F32), wide),
    )


def send_all(msg, body, left, right):
    block = jnp.concatenate([left, right], axis=1).astype(BF)
    for p in range(16):
        msg[p, :ROWS, :] = body
        msg[p, ROWS:, :] = block


def lane_sums(refs, wide):
    return jnp.concatenate(
        [jnp.sum(v.astype(F32) * wide, axis=0, keepdims=True) for v in refs], axis=0
    )


def start_body(s, rhs, ev, eo, ov, msg, ovs, rq, dq, keep, den):
    c, yh = s[0], s[1]
    column = jnp.broadcast_to(ev[...], (128, 256)).T
    for h in range(4):
        lanes = slice(h * 128, (h + 1) * 128)
        den[:, lanes] = column - eo[:, lanes]
    u = (rhs[...] / den[...]).astype(BF)
    keep[...] = u
    rq[...] = rhs[at(yh, ROWS), at(c, COLS)]
    dq[...] = den[at(yh, ROWS), at(c, COLS)]
    sums = lane_sums([ov[q] for q in range(4)], u.astype(F32))
    sums = sums[:, :COLS] + sums[:, COLS:]
    sums = jnp.concatenate([sums, jnp.zeros((4, COLS), F32)], axis=0)
    g = spread(sums)
    zero = jnp.zeros_like(g)
    send_all(
        msg,
        keep[at(yh, ROWS), at(c, COLS)],
        jnp.where(yh == 0, g, zero),
        jnp.where(yh == 0, zero, g),
    )
    for q in range(4):
        ovs[q] = ov[q, at(1 - yh, ROWS), :]


def main_body(s, fit, v1, v2, o1, o2, u, keep, send, part, full, zs, gs):
    c, yh = s[0], s[1]
    g = jnp.zeros((GROWS, COLS), F32)
    for p in range(16):
        full[p * ROWS : (p + 1) * ROWS, :] = u[p, :ROWS, :]
        g = g + u[p, ROWS:, :].astype(F32)
    gs[...] = g
    g = gs[:, at(yh, 128)]
    g = g + pltpu.roll(g, 1, 1)
    own = [jnp.full((1, 128), SCALE * fit[q], F32) for q in range(4)]
    part[...] = jnp.concatenate([*own, jnp.zeros((4, 128), F32)], axis=0) - 4.0 * g
    for k, v in enumerate((v1, v2)):
        z = jnp.dot(
            v[...].reshape(4 * 256, V), full[...], preferred_element_type=F32
        ).astype(BF)
        for q in range(4):
            zs[:, (k * 4 + q) * 256 : (k * 4 + q + 1) * 256] = z[q * 256 : (q + 1) * 256]
    a = jnp.zeros((256, COLS), F32)
    b = jnp.zeros((256, COLS), F32)
    for k, o in enumerate((o1, o2)):
        for q in range(4):
            zq = zs[:, (k * 4 + q) * 256 : (k * 4 + q + 1) * 256]
            a += jnp.dot(zq, o[q, at(c, 256), at(c, COLS)], preferred_element_type=F32)
            b += jnp.dot(
                zq, o[q, at(c, 256), at(1 - c, COLS)], preferred_element_type=F32
            )
    keep[...] = a
    send[...] = b


def pair_body(s, keep, got, part, partsw, ov, ov2, mine, other, tot):
    c, yh = s[0], s[1]
    w = part[...] + jnp.concatenate([partsw[4:8, :], partsw[0:4, :]], axis=0)
    for h in range(2):
        lanes = slice(h * 128, (h + 1) * 128)
        acc = keep[:, lanes] + got[:, lanes]
        for q in range(8):
            ref = (ov, ov2)[q // 4]
            acc += ref[q % 4, :, at(c * 2 + h, 128)].astype(F32) * w[q : q + 1, :]
        tot[:, lanes] = acc
    mine[...] = tot[at(yh, ROWS), :]
    other[...] = tot[at(1 - yh, ROWS), :].astype(BF)


def rows_body(mine, recv, total, out):
    t = mine[...] + recv[...].astype(F32)
    total[...] = t
    out[...] = t.astype(BF)


def near_body(total, before, after, three, three_half, two_half):
    two = total[...] + after[...].astype(F32)
    t = two + before[...].astype(F32)
    three[...] = t
    three_half[...] = t.astype(BF)
    two_half[...] = two.astype(BF)


def wide_body(mine, recv, out):
    total = (mine[...] + recv[...].astype(F32)).astype(BF)
    for p in range(8):
        out[p] = total


def update_body(s, three, before, after, rq, dq, ov, ov2, oth, oth2, msg):
    c, yh = s[0], s[1]
    share = three[...] + before[...].astype(F32) + after[...].astype(F32)
    u = ((rq[...] + share) / dq[...]).astype(BF)
    wide = u.astype(F32)
    rows, cols = at(yh, ROWS), at(c, COLS)
    own = spread(lane_sums([r[q, rows, cols] for r in (ov, ov2) for q in range(4)], wide))
    far = spread(lane_sums([r[q, :, cols] for r in (oth, oth2) for q in range(4)], wide))
    send_all(
        msg, u, jnp.where(yh == 0, own, far), jnp.where(yh == 0, far, own)
    )


def last_body(zm, rq, dq, out):
    share = zm[0].astype(F32)
    for p in range(1, 8):
        share += zm[p].astype(F32)
    out[...] = (rq[...] + share) / dq[...]


def join_body(s, w, wy, wc, wyc, out):
    c, yh = s[0], s[1]
    out[at(yh, ROWS), at(c, COLS)] = w[...]
    out[at(1 - yh, ROWS), at(c, COLS)] = wy[...]
    out[at(yh, ROWS), at(1 - c, COLS)] = wc[...]
    out[at(1 - yh, ROWS), at(1 - c, COLS)] = wyc[...]


def swap(value, axis):
    return lax.ppermute(value, axis, [(0, 1), (1, 0)])


def along_z(value, shift):
    n = lax.axis_size("z")
    return lax.ppermute(value, "z", [(i, (i + shift) % n) for i in range(n)])


def local(b_ov, b_vv, b_oo, rhs, fit_pert, eps_vir, eps_occ):
    s = jnp.stack([lax.axis_index("c"), lax.axis_index("yh")]).astype(jnp.int32)
    tile = sds(ROWS, COLS)
    half = sds(ROWS, COLS, dtype=BF)
    message = sds(16, PIECE, COLS, dtype=BF)
    msg, ovs, rq, dq = kernel(
        start_body,
        "start",
        [message, sds(4, ROWS, O, dtype=BF), tile, tile],
        [pltpu.VMEM((256, O), BF), pltpu.VMEM((256, O), F32)],
    )(s, rhs, eps_vir[None, :], eps_occ[None, :], b_ov)
    vv2, oo2, ov2 = swap(b_vv, "c"), swap(b_oo, "c"), swap(b_ov, "c")
    oth = oth2 = None
    for step in range(ITERS):
        msg = lax.all_to_all(msg, PLANE, 0, 0, tiled=True)
        keep, send, part = kernel(
            main_body,
            "main",
            [sds(256, COLS), sds(256, COLS), sds(8, 128)],
            [
                pltpu.VMEM((V, COLS), BF),
                pltpu.VMEM((256, V), BF),
                pltpu.VMEM((GROWS, COLS), F32),
            ],
            limit=12,
            flops=2 * 8 * 256 * 256 * (V + O),
            scalars=2,
        )(s, fit_pert, b_vv, vv2, b_oo, oo2, msg)
        mine, other = kernel(
            pair_body, "pair", [tile, half], [pltpu.VMEM((256, COLS), F32)]
        )(s, keep, swap(send, "c"), part, swap(part, "c"), b_ov, ov2)
        recv = swap(other, "yh")
        if step == ITERS - 1:
            break
        if oth is None:
            oth = swap(ovs, "yh")
            oth2 = swap(oth, "c")
        total, out = kernel(rows_body, "rows", [tile, half], scalars=0)(mine, recv)
        three, three_half, two_half = kernel(
            near_body, "near", [tile, half, half], scalars=0
        )(total, along_z(out, 1), along_z(out, -1))
        (msg,) = kernel(update_body, "update", [message])(
            s,
            three,
            along_z(two_half, 3),
            along_z(three_half, -3),
            rq,
            dq,
            b_ov,
            ov2,
            oth,
            oth2,
        )
    (zm,) = kernel(wide_body, "wide", [sds(8, ROWS, COLS, dtype=BF)], scalars=0)(
        mine, recv
    )
    zm = lax.all_to_all(zm, "z", 0, 0, tiled=True)
    (w,) = kernel(last_body, "last", [tile], scalars=0)(zm, rq, dq)
    wy, wc = swap(w, "yh"), swap(w, "c")
    return kernel(join_body, "join", [sds(256, O)])(s, w, wy, wc, swap(wy, "c"))[0]


def solution(mesh):
    split = Mesh(mesh.devices.reshape(2, 8, 2, 4, 2), ("yh", "z", "c", "x", "yl"))
    placed = (
        P(AUX, VIR, None),
        P(AUX, VIR, None),
        P(AUX, None, None),
        P(VIR, None),
        P(AUX),
        P(VIR),
        P(),
    )
    return jax.shard_map(
        local, mesh=split, in_specs=placed, out_specs=P(VIR, None), check_vma=False
    )
```

time: 236 us -> 200 us (0.85)
  matrix products: 33.2 us -> 0 us
  blocking collectives: 87 us -> 55.1 us
  Pallas kernels: 0 us -> 25.9 us
  other arithmetic: 11.6 us -> 0.07 us
  starting transfers between devices: 44.2 us -> 53.9 us
  waiting for transfers between devices: 47.7 us -> 54.7 us
    dot_general x6 -> x0, matrix products: 33.2 us -> none  [local(): jnp.einsum('qaj,qji->ai', mixed.astype(BF), oos, preferred_element_type=F32)]
    all_to_all x5 -> x3, blocking collectives: 87 us -> 55.1 us  [the longest x2 34.8 us: local(): msg = lax.all_to_all(msg, PLANE, 0, 0, tiled=True)]
    pallas_call x0 -> x16, Pallas kernels: none -> 25.9 us  [call(): pl.pallas_call(body, out_shape=list(outputs), in_specs=[pl.BlockSpec(memo...]
    ppermute x24 -> x25, waiting for transfers between devices: 34.1 us -> 54.7 us  [the longest x17 42 us: swap(): return lax.ppermute(value, axis, [(0, 1), (1, 0)])]
    all_to_all x1, waiting for transfers between devices: 13.6 us -> 0.01 us  [local(): msg = lax.all_to_all(msg, PLANE, 0, 0, tiled=True)]
    ppermute x24 -> x25, starting transfers between devices: 39.1 us -> 48.8 us  [the longest x17 32 us: swap(): return lax.ppermute(value, axis, [(0, 1), (1, 0)])]
    dynamic_slice x7 -> x0, local copies, waits for them, and re-layouts: 7.55 us -> none  [half(): return lax.dynamic_slice_in_dim(value, which * size, size, dim)]
    unnamed x8 -> x22, local copies, waits for them, and re-layouts: 2.03 us -> 9.2 us
  transfers between devices with their start and end apart: 25 -> 26, of which waited for: 15 -> 16; matrix products, arithmetic and copies ran while one was open for 19% -> 0% of each run, Pallas kernels for 0% -> 4%
where the time goes in v3:
time: 200 us; the launch traced here: 199 us
  blocking collectives  55.1 us (28%)
  waiting for transfers between devices  54.7 us (27%)
  starting transfers between devices  53.9 us (27%)
  Pallas kernels  25.9 us (13%)
  local copies, waits for them, and re-layouts  9.2 us (5%)
    ppermute x17, waiting for transfers between devices, swap(): return lax.ppermute(value, axis, [(0, 1), (1, 0)])  42 us
    all_to_all x2, blocking collectives, local(): msg = lax.all_to_all(msg, PLANE, 0, 0, tiled=True)  34.8 us
    ppermute x17, starting transfers between devices, swap(): return lax.ppermute(value, axis, [(0, 1), (1, 0)])  32 us
    pallas_call x16, Pallas kernels, call(): pl.pallas_call(body, out_shape=list(outputs), in_specs=[pl.BlockSpec(memo...  25.9 us
    all_to_all x1, blocking collectives, local(): zm = lax.all_to_all(zm, 'z', 0, 0, tiled=True)  20.3 us
    ppermute x8, starting transfers between devices, along_z(): return lax.ppermute(value, 'z', [(i, (i + shift) % n) for i in range(n)])  16.8 us
    ppermute x8, waiting for transfers between devices, along_z(): return lax.ppermute(value, 'z', [(i, (i + shift) % n) for i in range(n)])  12.7 us
    unnamed x22, local copies, waits for them, and re-layouts  9.2 us
  transfers between devices with their start and end apart: 26, of which 16 were waited for; matrix products, arithmetic and copies ran while one was open for 0% of the time, Pallas kernels for 4%

profile of v3, /device:TPU:1, one launch (start us, length us, event | category | flops | bytes accessed | tf_op | source)
XLA Modules:
  0.0 199.1 jit_solution(10511526583618687382)
XLA Ops:
  0.0 3.2 %collective-permute-start = (bf16[4,256,2048]{2,1,0:T(8,128)(2,1)}, bf16[4,256,2048]{2,1,0:T(8,128)(2,1)}, u32[]{:S(2)}, u32[]{:S(2)}) collective-permute-start(bf16[4,256,2048]{2,1,0:T(8,128)(2,1)} %v1.5), channel_id=1, source_target_pairs={{0,8},{8,0},{1,9},{9,1},{2,10},{10,2},{3,11},{11,3},{4,12},{12,4},... | collective-permute-start | bytes 12582920 | tf_op jit(solution)/shard_map/ppermute | solution.py:198
  9.8 5.2 %all-to-all-start = ((bf16[16,136,256]{2,1,0:T(8,128)(2,1)}), bf16[16,136,256]{2,1,0:T(8,128)(2,1)S(1)}, u32[]{:S(2)}, u32[]{:S(2)}) async-start(bf16[16,136,256]{2,1,0:T(8,128)(2,1)} %copy-done.5), calls=%async_computation | async-start | bytes 2228224 | tf_op jit(solution)/shard_map/all_to_all | solution.py:220
  15.9 3.1 %collective-permute-start.10 = (bf16[4,128,512]{2,1,0:T(8,128)(2,1)}, bf16[4,128,512]{2,1,0:T(8,128)(2,1)}, u32[]{:S(2)}, u32[]{:S(2)}) collective-permute-start(bf16[4,128,512]{2,1,0:T(8,128)(2,1)} %copy-done.10), channel_id=1, source_target_pairs={{0,128},{128,0},{1,129},{129,1},{2,130},{130,2},{3,131},{131,3},{4... | collective-permute-start | bytes 1572872 | tf_op jit(solution)/shard_map/ppermute | solution.py:198
  19.1 24.7 %collective-permute-done.10.oth = bf16[4,128,512]{2,1,0:T(8,128)(2,1)} collective-permute-done((bf16[4,128,512]{2,1,0:T(8,128)(2,1)}, bf16[4,128,512]{2,1,0:T(8,128)(2,1)}, u32[]{:S(2)}, u32[]{:S(2)}) %collective-permute-start.10) | collective-permute-done | bytes 524320 | tf_op jit(solution)/shard_map/ppermute | solution.py:198
  43.7 1.6 collective-permute-start.11
  45.4 2.2 %copy-done.2 = bf16[4,256,2048]{2,1,0:T(8,128)(2,1)S(1)} copy-done((bf16[4,256,2048]{2,1,0:T(8,128)(2,1)S(1)}, bf16[4,256,2048]{2,1,0:T(8,128)(2,1)}, u32[]{:S(2)}) %copy-start.2) | copy-done | bytes 4194328
  47.6 1.6 copy-done.4
  49.2 5.8 %main.3 = (f32[256,256]{1,0:T(8,128)S(1)}, f32[256,256]{1,0:T(8,128)S(1)}, f32[8,128]{1,0:T(8,128)S(1)}) custom-call(s32[2]{0:T(128)S(1)} %pad_add_fusion.s, f32[4]{0:T(128)S(1)} %copy-done.7, bf16[4,256,2048]{2,1,0:T(8,128)(2,1)S(1)} %copy-done.2, bf16[4,256,2048]{2,1,0:T(8,128)(2,1)} %collective-permute-done.v2, bf16[4,512,512]{2,1,0:T(8,128)(2,1)S(1)} %copy-done.4, ...), custom_call_target="tpu_custom_call" | custom-call | flops 2684354560 | bytes 14225432 | tf_op jit(solution)/shard_map/main/pallas_call | solution.py:31
  58.3 4.3 %collective-permute-done.5.recv = bf16[128,256]{1,0:T(8,128)(2,1)S(1)} collective-permute-done((bf16[128,256]{1,0:T(8,128)(2,1)S(1)}, bf16[128,256]{1,0:T(8,128)(2,1)S(1)}, u32[]{:S(2)}, u32[]{:S(2)}) %collective-permute-start.5) | collective-permute-done | bytes 65568 | tf_op jit(solution)/shard_map/ppermute | solution.py:198
  62.6 5.6 %collective-permute-start.7 = (bf16[128,256]{1,0:T(8,128)(2,1)S(1)}, bf16[128,256]{1,0:T(8,128)(2,1)S(1)}, u32[]{:S(2)}, u32[]{:S(2)}) collective-permute-start(bf16[128,256]{1,0:T(8,128)(2,1)S(1)} %get-tuple-element.41), channel_id=1, source_target_pairs={{0,112},{16,0},{32,16},{48,32},{64,48},{80,64},{96,80},{112,96},{1... | collective-permute-start | bytes 196616 | tf_op jit(solution)/shard_map/ppermute | solution.py:203
  69.6 3.0 %collective-permute-done.6.before = bf16[128,256]{1,0:T(8,128)(2,1)S(1)} collective-permute-done((bf16[128,256]{1,0:T(8,128)(2,1)S(1)}, bf16[128,256]{1,0:T(8,128)(2,1)S(1)}, u32[]{:S(2)}, u32[]{:S(2)}) %collective-permute-start.6) | collective-permute-done | bytes 65568 | tf_op jit(solution)/shard_map/ppermute | solution.py:203
  72.7 4.5 %collective-permute-start.9 = (bf16[128,256]{1,0:T(8,128)(2,1)S(1)}, bf16[128,256]{1,0:T(8,128)(2,1)S(1)}, u32[]{:S(2)}, u32[]{:S(2)}) collective-permute-start(bf16[128,256]{1,0:T(8,128)(2,1)S(1)} %get-tuple-element.44), channel_id=1, source_target_pairs={{0,80},{16,96},{32,112},{48,0},{64,16},{80,32},{96,48},{112,64},{1... | collective-permute-start | bytes 196616 | tf_op jit(solution)/shard_map/ppermute | solution.py:203
  77.2 2.0 collective-permute-done.8.before
  79.2 1.7 update.2
  80.9 18.9 %all_to_all.20.u = bf16[16,136,256]{2,1,0:T(8,128)(2,1)S(1)} all-to-all(bf16[16,136,256]{2,1,0:T(8,128)(2,1)S(1)} %update.2), channel_id=1, replica_groups=mesh['yh'=2,'z'=8,'c'=2,'x'=4,'yl'=2] {'x','yl','yh'}, dimensions={0} | all-to-all | bytes 2228224 | tf_op jit(solution)/shard_map/all_to_all | solution.py:220
  99.7 5.7 %main.4 = (f32[256,256]{1,0:T(8,128)S(1)}, f32[256,256]{1,0:T(8,128)S(1)}, f32[8,128]{1,0:T(8,128)S(1)}) custom-call(s32[2]{0:T(128)S(1)} %pad_add_fusion.s, f32[4]{0:T(128)S(1)} %copy-done.7, bf16[4,256,2048]{2,1,0:T(8,128)(2,1)S(1)} %copy-done.3, bf16[4,256,2048]{2,1,0:T(8,128)(2,1)} %collective-permute-done.v2, bf16[4,512,512]{2,1,0:T(8,128)(2,1)S(1)} %copy-done.4, ...), custom_call_target="tpu_custom_call" | custom-call | flops 2684354560 | bytes 14225432 | tf_op jit(solution)/shard_map/main/pallas_call | solution.py:31
  105.5 5.0 %collective-permute-start.12 = (f32[256,256]{1,0:T(8,128)S(1)}, f32[256,256]{1,0:T(8,128)S(1)}, u32[]{:S(2)}, u32[]{:S(2)}) collective-permute-start(f32[256,256]{1,0:T(8,128)S(1)} %get-tuple-element.49), channel_id=1, source_target_pairs={{0,8},{8,0},{1,9},{9,1},{2,10},{10,2},{3,11},{11,3},{4,12},{12,4},... | collective-permute-start | bytes 786440 | tf_op jit(solution)/shard_map/ppermute | solution.py:198
  113.3 4.0 %collective-permute-done.14.recv = bf16[128,256]{1,0:T(8,128)(2,1)S(1)} collective-permute-done((bf16[128,256]{1,0:T(8,128)(2,1)S(1)}, bf16[128,256]{1,0:T(8,128)(2,1)S(1)}, u32[]{:S(2)}, u32[]{:S(2)}) %collective-permute-start.14) | collective-permute-done | bytes 65568 | tf_op jit(solution)/shard_map/ppermute | solution.py:198
  117.4 1.9 collective-permute-start.15
  119.3 1.6 collective-permute-done.16.after
  122.1 2.4 %collective-permute-start.17 = (bf16[128,256]{1,0:T(8,128)(2,1)S(1)}, bf16[128,256]{1,0:T(8,128)(2,1)S(1)}, u32[]{:S(2)}, u32[]{:S(2)}) collective-permute-start(bf16[128,256]{1,0:T(8,128)(2,1)S(1)} %get-tuple-element.56), channel_id=1, source_target_pairs={{0,48},{16,64},{32,80},{48,96},{64,112},{80,0},{96,16},{112,32},{1... | collective-permute-start | bytes 196616 | tf_op jit(solution)/shard_map/ppermute | solution.py:203
  124.5 2.1 %collective-permute-start.18 = (bf16[128,256]{1,0:T(8,128)(2,1)S(1)}, bf16[128,256]{1,0:T(8,128)(2,1)S(1)}, u32[]{:S(2)}, u32[]{:S(2)}) collective-permute-start(bf16[128,256]{1,0:T(8,128)(2,1)S(1)} %get-tuple-element.57), channel_id=1, source_target_pairs={{0,80},{16,96},{32,112},{48,0},{64,16},{80,32},{96,48},{112,64},{1... | collective-permute-start | bytes 196616 | tf_op jit(solution)/shard_map/ppermute | solution.py:203
  126.6 2.3 %collective-permute-done.17.before = bf16[128,256]{1,0:T(8,128)(2,1)S(1)} collective-permute-done((bf16[128,256]{1,0:T(8,128)(2,1)S(1)}, bf16[128,256]{1,0:T(8,128)(2,1)S(1)}, u32[]{:S(2)}, u32[]{:S(2)}) %collective-permute-start.17) | collective-permute-done | bytes 65568 | tf_op jit(solution)/shard_map/ppermute | solution.py:203
  129.0 1.4 collective-permute-done.18.after
  130.4 1.6 update.3
  131.9 16.0 %all_to_all.21.u = bf16[16,136,256]{2,1,0:T(8,128)(2,1)S(1)} all-to-all(bf16[16,136,256]{2,1,0:T(8,128)(2,1)S(1)} %update.3), channel_id=1, replica_groups=mesh['yh'=2,'z'=8,'c'=2,'x'=4,'yl'=2] {'x','yl','yh'}, dimensions={0} | all-to-all | bytes 2228224 | tf_op jit(solution)/shard_map/all_to_all | solution.py:220
  147.9 5.7 %main.5 = (f32[256,256]{1,0:T(8,128)S(1)}, f32[256,256]{1,0:T(8,128)S(1)}, f32[8,128]{1,0:T(8,128)S(1)}) custom-call(s32[2]{0:T(128)S(1)} %pad_add_fusion.s, f32[4]{0:T(128)S(1)} %copy-done.7, bf16[4,256,2048]{2,1,0:T(8,128)(2,1)S(1)} %copy-done.3, bf16[4,256,2048]{2,1,0:T(8,128)(2,1)} %collective-permute-done.v2, bf16[4,512,512]{2,1,0:T(8,128)(2,1)S(1)} %copy-done.4, ...), custom_call_target="tpu_custom_call" | custom-call | flops 2684354560 | bytes 14225432 | tf_op jit(solution)/shard_map/main/pallas_call | solution.py:31
  153.7 5.9 %collective-permute-start.19 = (f32[256,256]{1,0:T(8,128)S(1)}, f32[256,256]{1,0:T(8,128)S(1)}, u32[]{:S(2)}, u32[]{:S(2)}) collective-permute-start(f32[256,256]{1,0:T(8,128)S(1)} %get-tuple-element.59), channel_id=1, source_target_pairs={{0,8},{8,0},{1,9},{9,1},{2,10},{10,2},{3,11},{11,3},{4,12},{12,4},... | collective-permute-start | bytes 786440 | tf_op jit(solution)/shard_map/ppermute | solution.py:198
  162.4 4.0 %collective-permute-done.21.recv = bf16[128,256]{1,0:T(8,128)(2,1)S(1)} collective-permute-done((bf16[128,256]{1,0:T(8,128)(2,1)S(1)}, bf16[128,256]{1,0:T(8,128)(2,1)S(1)}, u32[]{:S(2)}, u32[]{:S(2)}) %collective-permute-start.21) | collective-permute-done | bytes 65568 | tf_op jit(solution)/shard_map/ppermute | solution.py:198
  166.3 20.3 %all_to_all.22.zm = bf16[8,128,256]{2,1,0:T(8,128)(2,1)S(1)} all-to-all(bf16[8,128,256]{2,1,0:T(8,128)(2,1)S(1)} %wide.1), channel_id=1, replica_groups=mesh['yh'=2,'z'=8,'c'=2,'x'=4,'yl'=2] {'z'}, dimensions={0} | all-to-all | bytes 1048576 | tf_op jit(solution)/shard_map/all_to_all | solution.py:262
  187.5 3.7 %collective-permute-start.23 = (f32[128,256]{1,0:T(8,128)S(1)}, f32[128,256]{1,0:T(8,128)S(1)}, u32[]{:S(2)}, u32[]{:S(2)}) collective-permute-start(f32[128,256]{1,0:T(8,128)S(1)} %last.1.w), channel_id=1, source_target_pairs={{0,8},{8,0},{1,9},{9,1},{2,10},{10,2},{3,11},{11,3},{4,12},{12,4},... | collective-permute-start | bytes 393224 | tf_op jit(solution)/shard_map/ppermute | solution.py:198
  192.2 4.6 %collective-permute-start.24 = (f32[128,256]{1,0:T(8,128)S(1)}, f32[128,256]{1,0:T(8,128)S(1)}, u32[]{:S(2)}, u32[]{:S(2)}) collective-permute-start(f32[128,256]{1,0:T(8,128)S(1)} %collective-permute-done.22.wy), channel_id=1, source_target_pairs={{0,8},{8,0},{1,9},{9,1},{2,10},{10,2},{3,11},{11,3},{4,12},{12,4},... | collective-permute-start | bytes 393224 | tf_op jit(solution)/shard_map/ppermute | solution.py:198
  (62 shorter events, 23.3 us)
Async XLA Ops:
  0.0 45.4 %collective-permute-start = (bf16[4,256,2048]{2,1,0:T(8,128)(2,1)}, bf16[4,256,2048]{2,1,0:T(8,128)(2,1)}, u32[]{:S(2)}, u32[]{:S(2)}) collective-permute-start(bf16[4,256,2048]{2,1,0:T(8,128)(2,1)} %v1.5), channel_id=1, source_target_pairs={{0,8},{8,0},{1,9},{9,1},{2,10},{10,2},{3,11},{11,3},{4,12},{12,4},... | collective-permute-start | bytes 12582920 | tf_op jit(solution)/shard_map/ppermute | solution.py:198
  3.2 42.2 %collective-permute-start.1 = (bf16[4,512,512]{2,1,0:T(8,128)(2,1)}, bf16[4,512,512]{2,1,0:T(8,128)(2,1)}, u32[]{:S(2)}, u32[]{:S(2)}) collective-permute-start(bf16[4,512,512]{2,1,0:T(8,128)(2,1)} %o1.5), channel_id=1, source_target_pairs={{0,8},{8,0},{1,9},{9,1},{2,10},{10,2},{3,11},{11,3},{4,12},{12,4},... | collective-permute-start | bytes 6291464 | tf_op jit(solution)/shard_map/ppermute | solution.py:198
  3.3 1.2 copy-start
  9.8 5.2 %copy-start.1 = (bf16[4,256,512]{2,1,0:T(8,128)(2,1)S(1)}, bf16[4,256,512]{2,1,0:T(8,128)(2,1)}, u32[]{:S(2)}) copy-start(bf16[4,256,512]{2,1,0:T(8,128)(2,1)} %ov.11) | copy-start | bytes 3145732
  9.8 35.6 %copy-start.7 = (f32[4]{0:T(128)S(1)}, f32[4]{0:T(128)}, u32[]{:S(2)}) copy-start(f32[4]{0:T(128)} %fit.5) | copy-start | bytes 52
  9.8 35.5 %all-to-all-start = ((bf16[16,136,256]{2,1,0:T(8,128)(2,1)}), bf16[16,136,256]{2,1,0:T(8,128)(2,1)S(1)}, u32[]{:S(2)}, u32[]{:S(2)}) async-start(bf16[16,136,256]{2,1,0:T(8,128)(2,1)} %copy-done.5), calls=%async_computation | async-start | bytes 2228224 | tf_op jit(solution)/shard_map/all_to_all | solution.py:220
  15.0 40.5 %collective-permute-start.4 = (bf16[4,256,512]{2,1,0:T(8,128)(2,1)S(1)}, bf16[4,256,512]{2,1,0:T(8,128)(2,1)S(1)}, u32[]{:S(2)}, u32[]{:S(2)}) collective-permute-start(bf16[4,256,512]{2,1,0:T(8,128)(2,1)S(1)} %copy-done.1), channel_id=1, source_target_pairs={{0,8},{8,0},{1,9},{9,1},{2,10},{10,2},{3,11},{11,3},{4,12},{12,4},... | collective-permute-start | bytes 3145736 | tf_op jit(solution)/shard_map/ppermute | solution.py:198
  15.9 27.8 %collective-permute-start.10 = (bf16[4,128,512]{2,1,0:T(8,128)(2,1)}, bf16[4,128,512]{2,1,0:T(8,128)(2,1)}, u32[]{:S(2)}, u32[]{:S(2)}) collective-permute-start(bf16[4,128,512]{2,1,0:T(8,128)(2,1)} %copy-done.10), channel_id=1, source_target_pairs={{0,128},{128,0},{1,129},{129,1},{2,130},{130,2},{3,131},{131,3},{4... | collective-permute-start | bytes 1572872 | tf_op jit(solution)/shard_map/ppermute | solution.py:198
  43.7 33.4 %collective-permute-start.11 = (bf16[4,128,512]{2,1,0:T(8,128)(2,1)}, bf16[4,128,512]{2,1,0:T(8,128)(2,1)}, u32[]{:S(2)}, u32[]{:S(2)}) collective-permute-start(bf16[4,128,512]{2,1,0:T(8,128)(2,1)} %collective-permute-done.10.oth), channel_id=1, source_target_pairs={{0,8},{8,0},{1,9},{9,1},{2,10},{10,2},{3,11},{11,3},{4,12},{12,4},... | collective-permute-start | bytes 1572872 | tf_op jit(solution)/shard_map/ppermute | solution.py:198
  45.4 2.2 %copy-start.2 = (bf16[4,256,2048]{2,1,0:T(8,128)(2,1)S(1)}, bf16[4,256,2048]{2,1,0:T(8,128)(2,1)}, u32[]{:S(2)}) copy-start(bf16[4,256,2048]{2,1,0:T(8,128)(2,1)} %v1.5) | copy-start | bytes 12582916
  47.6 1.6 copy-start.4
  55.0 1.6 collective-permute-start.2
  55.1 1.5 collective-permute-start.3
  57.5 5.1 %collective-permute-start.5 = (bf16[128,256]{1,0:T(8,128)(2,1)S(1)}, bf16[128,256]{1,0:T(8,128)(2,1)S(1)}, u32[]{:S(2)}, u32[]{:S(2)}) collective-permute-start(bf16[128,256]{1,0:T(8,128)(2,1)S(1)} %get-tuple-element.39), channel_id=1, source_target_pairs={{0,128},{128,0},{1,129},{129,1},{2,130},{130,2},{3,131},{131,3},{4... | collective-permute-start | bytes 196616 | tf_op jit(solution)/shard_map/ppermute | solution.py:198
  62.6 7.0 %collective-permute-start.7 = (bf16[128,256]{1,0:T(8,128)(2,1)S(1)}, bf16[128,256]{1,0:T(8,128)(2,1)S(1)}, u32[]{:S(2)}, u32[]{:S(2)}) collective-permute-start(bf16[128,256]{1,0:T(8,128)(2,1)S(1)} %get-tuple-element.41), channel_id=1, source_target_pairs={{0,112},{16,0},{32,16},{48,32},{64,48},{80,64},{96,80},{112,96},{1... | collective-permute-start | bytes 196616 | tf_op jit(solution)/shard_map/ppermute | solution.py:203
  68.3 4.3 %collective-permute-start.6 = (bf16[128,256]{1,0:T(8,128)(2,1)S(1)}, bf16[128,256]{1,0:T(8,128)(2,1)S(1)}, u32[]{:S(2)}, u32[]{:S(2)}) collective-permute-start(bf16[128,256]{1,0:T(8,128)(2,1)S(1)} %get-tuple-element.41), channel_id=1, source_target_pairs={{0,16},{16,32},{32,48},{48,64},{64,80},{80,96},{96,112},{112,0},{1... | collective-permute-start | bytes 196616 | tf_op jit(solution)/shard_map/ppermute | solution.py:203
  72.6 6.5 %collective-permute-start.8 = (bf16[128,256]{1,0:T(8,128)(2,1)S(1)}, bf16[128,256]{1,0:T(8,128)(2,1)S(1)}, u32[]{:S(2)}, u32[]{:S(2)}) collective-permute-start(bf16[128,256]{1,0:T(8,128)(2,1)S(1)} %get-tuple-element.43), channel_id=1, source_target_pairs={{0,48},{16,64},{32,80},{48,96},{64,112},{80,0},{96,16},{112,32},{1... | collective-permute-start | bytes 196616 | tf_op jit(solution)/shard_map/ppermute | solution.py:203
  72.7 6.4 %collective-permute-start.9 = (bf16[128,256]{1,0:T(8,128)(2,1)S(1)}, bf16[128,256]{1,0:T(8,128)(2,1)S(1)}, u32[]{:S(2)}, u32[]{:S(2)}) collective-permute-start(bf16[128,256]{1,0:T(8,128)(2,1)S(1)} %get-tuple-element.44), channel_id=1, source_target_pairs={{0,80},{16,96},{32,112},{48,0},{64,16},{80,32},{96,48},{112,64},{1... | collective-permute-start | bytes 196616 | tf_op jit(solution)/shard_map/ppermute | solution.py:203
  79.2 20.6 %copy-start.3 = (bf16[4,256,2048]{2,1,0:T(8,128)(2,1)S(1)}, bf16[4,256,2048]{2,1,0:T(8,128)(2,1)}, u32[]{:S(2)}) copy-start(bf16[4,256,2048]{2,1,0:T(8,128)(2,1)} %v1.5) | copy-start | bytes 12582916
  105.5 6.2 %collective-permute-start.12 = (f32[256,256]{1,0:T(8,128)S(1)}, f32[256,256]{1,0:T(8,128)S(1)}, u32[]{:S(2)}, u32[]{:S(2)}) collective-permute-start(f32[256,256]{1,0:T(8,128)S(1)} %get-tuple-element.49), channel_id=1, source_target_pairs={{0,8},{8,0},{1,9},{9,1},{2,10},{10,2},{3,11},{11,3},{4,12},{12,4},... | collective-permute-start | bytes 786440 | tf_op jit(solution)/shard_map/ppermute | solution.py:198
  110.5 1.2 collective-permute-start.13
  112.6 4.7 %collective-permute-start.14 = (bf16[128,256]{1,0:T(8,128)(2,1)S(1)}, bf16[128,256]{1,0:T(8,128)(2,1)S(1)}, u32[]{:S(2)}, u32[]{:S(2)}) collective-permute-start(bf16[128,256]{1,0:T(8,128)(2,1)S(1)} %get-tuple-element.52), channel_id=1, source_target_pairs={{0,128},{128,0},{1,129},{129,1},{2,130},{130,2},{3,131},{131,3},{4... | collective-permute-start | bytes 196616 | tf_op jit(solution)/shard_map/ppermute | solution.py:198
  117.3 3.6 %collective-permute-start.16 = (bf16[128,256]{1,0:T(8,128)(2,1)S(1)}, bf16[128,256]{1,0:T(8,128)(2,1)S(1)}, u32[]{:S(2)}, u32[]{:S(2)}) collective-permute-start(bf16[128,256]{1,0:T(8,128)(2,1)S(1)} %get-tuple-element.54), channel_id=1, source_target_pairs={{0,112},{16,0},{32,16},{48,32},{64,48},{80,64},{96,80},{112,96},{1... | collective-permute-start | bytes 196616 | tf_op jit(solution)/shard_map/ppermute | solution.py:203
  117.4 4.7 %collective-permute-start.15 = (bf16[128,256]{1,0:T(8,128)(2,1)S(1)}, bf16[128,256]{1,0:T(8,128)(2,1)S(1)}, u32[]{:S(2)}, u32[]{:S(2)}) collective-permute-start(bf16[128,256]{1,0:T(8,128)(2,1)S(1)} %get-tuple-element.54), channel_id=1, source_target_pairs={{0,16},{16,32},{32,48},{48,64},{64,80},{80,96},{96,112},{112,0},{1... | collective-permute-start | bytes 196616 | tf_op jit(solution)/shard_map/ppermute | solution.py:203
  122.1 6.9 %collective-permute-start.17 = (bf16[128,256]{1,0:T(8,128)(2,1)S(1)}, bf16[128,256]{1,0:T(8,128)(2,1)S(1)}, u32[]{:S(2)}, u32[]{:S(2)}) collective-permute-start(bf16[128,256]{1,0:T(8,128)(2,1)S(1)} %get-tuple-element.56), channel_id=1, source_target_pairs={{0,48},{16,64},{32,80},{48,96},{64,112},{80,0},{96,16},{112,32},{1... | collective-permute-start | bytes 196616 | tf_op jit(solution)/shard_map/ppermute | solution.py:203
  124.5 5.8 %collective-permute-start.18 = (bf16[128,256]{1,0:T(8,128)(2,1)S(1)}, bf16[128,256]{1,0:T(8,128)(2,1)S(1)}, u32[]{:S(2)}, u32[]{:S(2)}) collective-permute-start(bf16[128,256]{1,0:T(8,128)(2,1)S(1)} %get-tuple-element.57), channel_id=1, source_target_pairs={{0,80},{16,96},{32,112},{48,0},{64,16},{80,32},{96,48},{112,64},{1... | collective-permute-start | bytes 196616 | tf_op jit(solution)/shard_map/ppermute | solution.py:203
  153.7 7.1 %collective-permute-start.19 = (f32[256,256]{1,0:T(8,128)S(1)}, f32[256,256]{1,0:T(8,128)S(1)}, u32[]{:S(2)}, u32[]{:S(2)}) collective-permute-start(f32[256,256]{1,0:T(8,128)S(1)} %get-tuple-element.59), channel_id=1, source_target_pairs={{0,8},{8,0},{1,9},{9,1},{2,10},{10,2},{3,11},{11,3},{4,12},{12,4},... | collective-permute-start | bytes 786440 | tf_op jit(solution)/shard_map/ppermute | solution.py:198
  159.6 1.2 collective-permute-start.20
  161.6 4.7 %collective-permute-start.21 = (bf16[128,256]{1,0:T(8,128)(2,1)S(1)}, bf16[128,256]{1,0:T(8,128)(2,1)S(1)}, u32[]{:S(2)}, u32[]{:S(2)}) collective-permute-start(bf16[128,256]{1,0:T(8,128)(2,1)S(1)} %get-tuple-element.62), channel_id=1, source_target_pairs={{0,128},{128,0},{1,129},{129,1},{2,130},{130,2},{3,131},{131,3},{4... | collective-permute-start | bytes 196616 | tf_op jit(solution)/shard_map/ppermute | solution.py:198
  186.7 5.4 %collective-permute-start.22 = (f32[128,256]{1,0:T(8,128)S(1)}, f32[128,256]{1,0:T(8,128)S(1)}, u32[]{:S(2)}, u32[]{:S(2)}) collective-permute-start(f32[128,256]{1,0:T(8,128)S(1)} %last.1.w), channel_id=1, source_target_pairs={{0,128},{128,0},{1,129},{129,1},{2,130},{130,2},{3,131},{131,3},{4... | collective-permute-start | bytes 393224 | tf_op jit(solution)/shard_map/ppermute | solution.py:198
  187.5 9.2 %collective-permute-start.23 = (f32[128,256]{1,0:T(8,128)S(1)}, f32[128,256]{1,0:T(8,128)S(1)}, u32[]{:S(2)}, u32[]{:S(2)}) collective-permute-start(f32[128,256]{1,0:T(8,128)S(1)} %last.1.w), channel_id=1, source_target_pairs={{0,8},{8,0},{1,9},{9,1},{2,10},{10,2},{3,11},{11,3},{4,12},{12,4},... | collective-permute-start | bytes 393224 | tf_op jit(solution)/shard_map/ppermute | solution.py:198
  192.2 5.6 %collective-permute-start.24 = (f32[128,256]{1,0:T(8,128)S(1)}, f32[128,256]{1,0:T(8,128)S(1)}, u32[]{:S(2)}, u32[]{:S(2)}) collective-permute-start(f32[128,256]{1,0:T(8,128)S(1)} %collective-permute-done.22.wy), channel_id=1, source_target_pairs={{0,8},{8,0},{1,9},{9,1},{2,10},{10,2},{3,11},{11,3},{4,12},{12,4},... | collective-permute-start | bytes 393224 | tf_op jit(solution)/shard_map/ppermute | solution.py:198
  (5 other events, 4.2 us)

commit v4 on v3

--- a/solution.py
+++ b/solution.py
@@ -25,17 +25,26 @@
     return jax.ShapeDtypeStruct(shape, dtype)
 
 
-def kernel(body, name, outputs, scratch=(), limit=8, flops=0, scalars=1):
+def kernel(body, name, outputs, scratch=(), limit=8, flops=0, scalars=1, far=(), out=()):
     def call(*args):
         moved = sum(math.prod(a.shape) * a.dtype.itemsize for a in (*args, *outputs))
         return pl.pallas_call(
             body,
             out_shape=list(outputs),
             in_specs=[
-                pl.BlockSpec(memory_space=pltpu.SMEM if k < scalars else pltpu.VMEM)
+                pl.BlockSpec(
+                    memory_space=pltpu.SMEM
+                    if k < scalars
+                    else pltpu.HBM
+                    if k in far
+                    else pltpu.VMEM
+                )
                 for k in range(len(args))
             ],
-            out_specs=[pl.BlockSpec(memory_space=pltpu.VMEM) for _ in outputs],
+            out_specs=[
+                pl.BlockSpec(memory_space=pltpu.HBM if k in out else pltpu.VMEM)
+                for k in range(len(outputs))
+            ],
             scratch_shapes=list(scratch),
             compiler_params=pltpu.CompilerParams(vmem_limit_bytes=limit << 20),
             cost_estimate=pl.CostEstimate(
@@ -77,16 +86,30 @@
     )
 
 
-def start_body(s, rhs, ev, eo, ov, msg, ovs, rq, dq, keep, den):
-    c, yh = s[0], s[1]
+def start_body(
+    s, rhs_h, ev_h, eo_h, ov_h, msg_h, rq, dq, rhs, ev, eo, ov, msg, keep, den, sems
+):
+    c, yh = s[0], s[1]
+    copies = [
+        pltpu.make_async_copy(src, dst, sems.at[k])
+        for k, (src, dst) in enumerate(
+            ((ev_h, ev), (eo_h, eo), (rhs_h, rhs), (ov_h, ov))
+        )
+    ]
+    for copy in copies:
+        copy.start()
+    copies[0].wait()
+    copies[1].wait()
     column = jnp.broadcast_to(ev[...], (128, 256)).T
     for h in range(4):
         lanes = slice(h * 128, (h + 1) * 128)
         den[:, lanes] = column - eo[:, lanes]
+    copies[2].wait()
     u = (rhs[...] / den[...]).astype(BF)
     keep[...] = u
     rq[...] = rhs[at(yh, ROWS), at(c, COLS)]
     dq[...] = den[at(yh, ROWS), at(c, COLS)]
+    copies[3].wait()
     sums = lane_sums([ov[q] for q in range(4)], u.astype(F32))
     sums = sums[:, :COLS] + sums[:, COLS:]
     sums = jnp.concatenate([sums, jnp.zeros((4, COLS), F32)], axis=0)
@@ -98,12 +121,30 @@
         jnp.where(yh == 0, g, zero),
         jnp.where(yh == 0, zero, g),
     )
-    for q in range(4):
-        ovs[q] = ov[q, at(1 - yh, ROWS), :]
-
-
-def main_body(s, fit, v1, v2, o1, o2, u, keep, send, part, full, zs, gs):
-    c, yh = s[0], s[1]
+    out = pltpu.make_async_copy(msg, msg_h, sems.at[4])
+    out.start()
+    out.wait()
+
+
+def main_body(
+    s, fit, v1_h, v2_h, o1_h, o2_h, u, keep, send, part, v, o, full, zs, gs, sems
+):
+    c, yh = s[0], s[1]
+    pieces = ((v1_h, 0, 1), (v1_h, 1, 4), (v2_h, 0, 4))
+    copies = []
+    for k, (src, low, high) in enumerate(pieces):
+        dst = v.at[pl.ds(low + (4 if src is v2_h else 0), high - low)]
+        copies.append(
+            pltpu.make_async_copy(src.at[pl.ds(low, high - low)], dst, sems.at[k])
+        )
+    for k, src in enumerate((o1_h, o2_h)):
+        copies.append(
+            pltpu.make_async_copy(
+                src.at[:, at(c, 256), :], o.at[pl.ds(4 * k, 4)], sems.at[3 + k]
+            )
+        )
+    for copy in copies:
+        copy.start()
     g = jnp.zeros((GROWS, COLS), F32)
     for p in range(16):
         full[p * ROWS : (p + 1) * ROWS, :] = u[p, :ROWS, :]
@@ -113,21 +154,23 @@
     g = g + pltpu.roll(g, 1, 1)
     own = [jnp.full((1, 128), SCALE * fit[q], F32) for q in range(4)]
     part[...] = jnp.concatenate([*own, jnp.zeros((4, 128), F32)], axis=0) - 4.0 * g
-    for k, v in enumerate((v1, v2)):
+    for k, (low, high) in enumerate(((0, 1), (1, 4), (4, 8))):
+        copies[k].wait()
         z = jnp.dot(
-            v[...].reshape(4 * 256, V), full[...], preferred_element_type=F32
+            v[low:high].reshape((high - low) * 256, V),
+            full[...],
+            preferred_element_type=F32,
         ).astype(BF)
-        for q in range(4):
-            zs[:, (k * 4 + q) * 256 : (k * 4 + q + 1) * 256] = z[q * 256 : (q + 1) * 256]
+        for q in range(low, high):
+            zs[:, q * 256 : (q + 1) * 256] = z[(q - low) * 256 : (q - low + 1) * 256]
+    copies[3].wait()
+    copies[4].wait()
     a = jnp.zeros((256, COLS), F32)
     b = jnp.zeros((256, COLS), F32)
-    for k, o in enumerate((o1, o2)):
-        for q in range(4):
-            zq = zs[:, (k * 4 + q) * 256 : (k * 4 + q + 1) * 256]
-            a += jnp.dot(zq, o[q, at(c, 256), at(c, COLS)], preferred_element_type=F32)
-            b += jnp.dot(
-                zq, o[q, at(c, 256), at(1 - c, COLS)], preferred_element_type=F32
-            )
+    for q in range(8):
+        zq = zs[:, q * 256 : (q + 1) * 256]
+        a += jnp.dot(zq, o[q, :, at(c, COLS)], preferred_element_type=F32)
+        b += jnp.dot(zq, o[q, :, at(1 - c, COLS)], preferred_element_type=F32)
     keep[...] = a
     send[...] = b
 
@@ -152,6 +195,13 @@
     out[...] = t.astype(BF)
 
 
+def first_rows_body(s, mine, recv, ov, ov2, total, out, ovs):
+    c, yh = s[0], s[1]
+    rows_body(mine, recv, total, out)
+    for q in range(8):
+        ovs[q] = (ov, ov2)[q // 4][q % 4, at(1 - yh, ROWS), at(c, COLS)]
+
+
 def near_body(total, before, after, three, three_half, two_half):
     two = total[...] + after[...].astype(F32)
     t = two + before[...].astype(F32)
@@ -166,14 +216,14 @@
         out[p] = total
 
 
-def update_body(s, three, before, after, rq, dq, ov, ov2, oth, oth2, msg):
+def update_body(s, three, before, after, rq, dq, ov, ov2, oth, msg):
     c, yh = s[0], s[1]
     share = three[...] + before[...].astype(F32) + after[...].astype(F32)
     u = ((rq[...] + share) / dq[...]).astype(BF)
     wide = u.astype(F32)
     rows, cols = at(yh, ROWS), at(c, COLS)
     own = spread(lane_sums([r[q, rows, cols] for r in (ov, ov2) for q in range(4)], wide))
-    far = spread(lane_sums([r[q, :, cols] for r in (oth, oth2) for q in range(4)], wide))
+    far = spread(lane_sums([oth[q] for q in range(8)], wide))
     send_all(
         msg, u, jnp.where(yh == 0, own, far), jnp.where(yh == 0, far, own)
     )
@@ -208,14 +258,26 @@
     tile = sds(ROWS, COLS)
     half = sds(ROWS, COLS, dtype=BF)
     message = sds(16, PIECE, COLS, dtype=BF)
-    msg, ovs, rq, dq = kernel(
+    msg, rq, dq = kernel(
         start_body,
         "start",
-        [message, sds(4, ROWS, O, dtype=BF), tile, tile],
-        [pltpu.VMEM((256, O), BF), pltpu.VMEM((256, O), F32)],
+        [message, tile, tile],
+        [
+            pltpu.VMEM((256, O), F32),
+            pltpu.VMEM((1, 256), F32),
+            pltpu.VMEM((1, O), F32),
+            pltpu.VMEM((4, 256, O), BF),
+            pltpu.VMEM((16, PIECE, COLS), BF),
+            pltpu.VMEM((256, O), BF),
+            pltpu.VMEM((256, O), F32),
+            pltpu.SemaphoreType.DMA((5,)),
+        ],
+        limit=60,
+        far=range(1, 5),
+        out=(0,),
     )(s, rhs, eps_vir[None, :], eps_occ[None, :], b_ov)
     vv2, oo2, ov2 = swap(b_vv, "c"), swap(b_oo, "c"), swap(b_ov, "c")
-    oth = oth2 = None
+    oth = None
     for step in range(ITERS):
         msg = lax.all_to_all(msg, PLANE, 0, 0, tiled=True)
         keep, send, part = kernel(
@@ -223,11 +285,15 @@
             "main",
             [sds(256, COLS), sds(256, COLS), sds(8, 128)],
             [
+                pltpu.VMEM((8, 256, V), BF),
+                pltpu.VMEM((8, 256, O), BF),
                 pltpu.VMEM((V, COLS), BF),
                 pltpu.VMEM((256, V), BF),
                 pltpu.VMEM((GROWS, COLS), F32),
+                pltpu.SemaphoreType.DMA((5,)),
             ],
-            limit=12,
+            limit=52,
+            far=range(2, 6),
             flops=2 * 8 * 256 * 256 * (V + O),
             scalars=2,
         )(s, fit_pert, b_vv, vv2, b_oo, oo2, msg)
@@ -238,9 +304,14 @@
         if step == ITERS - 1:
             break
         if oth is None:
+            total, out, ovs = kernel(
+                first_rows_body,
+                "first_rows",
+                [tile, half, sds(8, ROWS, COLS, dtype=BF)],
+            )(s, mine, recv, b_ov, ov2)
             oth = swap(ovs, "yh")
-            oth2 = swap(oth, "c")
-        total, out = kernel(rows_body, "rows", [tile, half], scalars=0)(mine, recv)
+        else:
+            total, out = kernel(rows_body, "rows", [tile, half], scalars=0)(mine, recv)
         three, three_half, two_half = kernel(
             near_body, "near", [tile, half, half], scalars=0
         )(total, along_z(out, 1), along_z(out, -1))
@@ -254,7 +325,6 @@
             b_ov,
             ov2,
             oth,
-            oth2,
         )
     (zm,) = kernel(wide_body, "wide", [sds(8, ROWS, COLS, dtype=BF)], scalars=0)(
         mine, recv

time: 200 us -> 190 us (0.950)
  waiting for transfers between devices: 54.7 us -> 44.2 us
  local copies, waits for them, and re-layouts: 9.2 us -> 0.02 us
  Pallas kernels: 25.9 us -> 35 us
  starting transfers between devices: 53.9 us -> 58.1 us
  blocking collectives: 55.1 us -> 51.7 us
    ppermute x17 -> x16, waiting for transfers between devices: 42 us -> 14.6 us  [swap(): return lax.ppermute(value, axis, [(0, 1), (1, 0)])]
    all_to_all x1, waiting for transfers between devices: 0.01 us -> 17.2 us  [local(): msg = lax.all_to_all(msg, PLANE, 0, 0, tiled=True)]
    unnamed x22 -> x10, local copies, waits for them, and re-layouts: 9.2 us -> 0.02 us
    pallas_call x16, Pallas kernels: 25.9 us -> 35 us  [call(): pl.pallas_call(body, out_shape=list(outputs), in_specs=[pl.BlockSpec(memo...]
    ppermute x17 -> x16, starting transfers between devices: 32 us -> 35.9 us  [swap(): return lax.ppermute(value, axis, [(0, 1), (1, 0)])]
    all_to_all x2, blocking collectives: 34.8 us -> 31.4 us  [local(): msg = lax.all_to_all(msg, PLANE, 0, 0, tiled=True)]
  transfers between devices with their start and end apart: 26 -> 25, of which waited for: 16 -> 16; matrix products, arithmetic and copies ran while one was open for 0% -> 0% of each run, Pallas kernels for 4% -> 6%
where the time goes in v4:
time: 190 us
  starting transfers between devices  58.1 us (31%)
  blocking collectives  51.7 us (27%)
  waiting for transfers between devices  44.2 us (23%)
  Pallas kernels  35 us (18%)
    ppermute x16, starting transfers between devices, swap(): return lax.ppermute(value, axis, [(0, 1), (1, 0)])  35.9 us
    pallas_call x16, Pallas kernels, call(): pl.pallas_call(body, out_shape=list(outputs), in_specs=[pl.BlockSpec(memo...  35 us
    all_to_all x2, blocking collectives, local(): msg = lax.all_to_all(msg, PLANE, 0, 0, tiled=True)  31.4 us
    all_to_all x1, blocking collectives, local(): zm = lax.all_to_all(zm, 'z', 0, 0, tiled=True)  20.3 us
    all_to_all x1, waiting for transfers between devices, local(): msg = lax.all_to_all(msg, PLANE, 0, 0, tiled=True)  17.2 us
    ppermute x8, starting transfers between devices, along_z(): return lax.ppermute(value, 'z', [(i, (i + shift) % n) for i in range(n)])  17.1 us
    ppermute x16, waiting for transfers between devices, swap(): return lax.ppermute(value, axis, [(0, 1), (1, 0)])  14.6 us
    ppermute x8, waiting for transfers between devices, along_z(): return lax.ppermute(value, 'z', [(i, (i + shift) % n) for i in range(n)])  12.4 us
  transfers between devices with their start and end apart: 25, of which 16 were waited for; matrix products, arithmetic and copies ran while one was open for 0% of the time, Pallas kernels for 6%

profile of v4, /device:TPU:1, one launch (start us, length us, event | category | flops | bytes accessed | tf_op | source)
XLA Modules:
  0.0 189.8 jit_solution(12022601256970651041)
XLA Ops:
  0.0 3.2 %collective-permute-start = (bf16[4,256,2048]{2,1,0:T(8,128)(2,1)}, bf16[4,256,2048]{2,1,0:T(8,128)(2,1)}, u32[]{:S(2)}, u32[]{:S(2)}) collective-permute-start(bf16[4,256,2048]{2,1,0:T(8,128)(2,1)} %v1_h.5), channel_id=1, source_target_pairs={{0,8},{8,0},{1,9},{9,1},{2,10},{10,2},{3,11},{11,3},{4,12},{12,4},... | collective-permute-start | bytes 12582920 | tf_op jit(solution)/shard_map/ppermute | solution.py:248
  3.8 4.2 %start.1 = (bf16[16,136,256]{2,1,0:T(8,128)(2,1)}, f32[128,256]{1,0:T(8,128)}, f32[128,256]{1,0:T(8,128)}) custom-call(s32[2]{0:T(128)} %pad_add_fusion.s, f32[256,512]{1,0:T(8,128)} %rhs_h.1, f32[1,256]{1,0:T(1,128)} %bitcast.5, f32[1,512]{1,0:T(1,128)} %bitcast.4, bf16[4,256,512]{2,1,0:T(8,128)(2,1)} %ov.11), custom_call_target="tpu_custom_call" | custom-call | bytes 2952200 | tf_op jit(solution)/shard_map/start/pallas_call | solution.py:31
  8.0 5.2 %all-to-all-start = ((bf16[16,136,256]{2,1,0:T(8,128)(2,1)}), bf16[16,136,256]{2,1,0:T(8,128)(2,1)S(1)}, u32[]{:S(2)}, u32[]{:S(2)}) async-start(bf16[16,136,256]{2,1,0:T(8,128)(2,1)} %get-tuple-element.34), calls=%async_computation | async-start | bytes 2228224 | tf_op jit(solution)/shard_map/all_to_all | solution.py:282
  14.1 17.2 %all-to-all-done.u = bf16[16,136,256]{2,1,0:T(8,128)(2,1)S(1)} async-done(((bf16[16,136,256]{2,1,0:T(8,128)(2,1)}), bf16[16,136,256]{2,1,0:T(8,128)(2,1)S(1)}, u32[]{:S(2)}, u32[]{:S(2)}) %all-to-all-start) | async-done | bytes 1114144 | tf_op jit(solution)/shard_map/all_to_all | solution.py:282
  31.3 8.1 %main.3 = (f32[256,256]{1,0:T(8,128)S(1)}, f32[256,256]{1,0:T(8,128)S(1)}, f32[8,128]{1,0:T(8,128)S(1)}) custom-call(s32[2]{0:T(128)S(1)} %copy-done.3, f32[4]{0:T(128)S(1)} %copy-done.4, bf16[4,256,2048]{2,1,0:T(8,128)(2,1)} %v1_h.5, bf16[4,256,2048]{2,1,0:T(8,128)(2,1)} %collective-permute-done.v2_h, bf16[4,512,512]{2,1,0:T(8,128)(2,1)} %o1_h.5, ...), custom_call_target="tpu_custom_call" | custom-call | flops 2684354560 | bytes 14225432 | tf_op jit(solution)/shard_map/main/pallas_call | solution.py:31
  39.4 2.6 %collective-permute-start.2 = (f32[256,256]{1,0:T(8,128)S(1)}, f32[256,256]{1,0:T(8,128)S(1)}, u32[]{:S(2)}, u32[]{:S(2)}) collective-permute-start(f32[256,256]{1,0:T(8,128)S(1)} %get-tuple-element.36), channel_id=1, source_target_pairs={{0,8},{8,0},{1,9},{9,1},{2,10},{10,2},{3,11},{11,3},{4,12},{12,4},... | collective-permute-start | bytes 786440 | tf_op jit(solution)/shard_map/ppermute | solution.py:248
  44.0 2.7 %collective-permute-start.5 = (bf16[128,256]{1,0:T(8,128)(2,1)S(1)}, bf16[128,256]{1,0:T(8,128)(2,1)S(1)}, u32[]{:S(2)}, u32[]{:S(2)}) collective-permute-start(bf16[128,256]{1,0:T(8,128)(2,1)S(1)} %get-tuple-element.39), channel_id=1, source_target_pairs={{0,128},{128,0},{1,129},{129,1},{2,130},{130,2},{3,131},{131,3},{4... | collective-permute-start | bytes 196616 | tf_op jit(solution)/shard_map/ppermute | solution.py:248
  46.7 2.0 %collective-permute-done.5.recv = bf16[128,256]{1,0:T(8,128)(2,1)S(1)} collective-permute-done((bf16[128,256]{1,0:T(8,128)(2,1)S(1)}, bf16[128,256]{1,0:T(8,128)(2,1)S(1)}, u32[]{:S(2)}, u32[]{:S(2)}) %collective-permute-start.5) | collective-permute-done | bytes 65568 | tf_op jit(solution)/shard_map/ppermute | solution.py:248
  49.3 2.7 %collective-permute-start.10 = (bf16[8,128,256]{2,1,0:T(8,128)(2,1)S(1)}, bf16[8,128,256]{2,1,0:T(8,128)(2,1)S(1)}, u32[]{:S(2)}, u32[]{:S(2)}) collective-permute-start(bf16[8,128,256]{2,1,0:T(8,128)(2,1)S(1)} %get-tuple-element.47), channel_id=1, source_target_pairs={{0,128},{128,0},{1,129},{129,1},{2,130},{130,2},{3,131},{131,3},{4... | collective-permute-start | bytes 1572872 | tf_op jit(solution)/shard_map/ppermute | solution.py:248
  52.0 5.6 %collective-permute-start.7 = (bf16[128,256]{1,0:T(8,128)(2,1)S(1)}, bf16[128,256]{1,0:T(8,128)(2,1)S(1)}, u32[]{:S(2)}, u32[]{:S(2)}) collective-permute-start(bf16[128,256]{1,0:T(8,128)(2,1)S(1)} %get-tuple-element.41), channel_id=1, source_target_pairs={{0,112},{16,0},{32,16},{48,32},{64,48},{80,64},{96,80},{112,96},{1... | collective-permute-start | bytes 196616 | tf_op jit(solution)/shard_map/ppermute | solution.py:253
  57.6 1.3 collective-permute-done.7.after
  58.9 3.3 %collective-permute-done.6.before = bf16[128,256]{1,0:T(8,128)(2,1)S(1)} collective-permute-done((bf16[128,256]{1,0:T(8,128)(2,1)S(1)}, bf16[128,256]{1,0:T(8,128)(2,1)S(1)}, u32[]{:S(2)}, u32[]{:S(2)}) %collective-permute-start.6) | collective-permute-done | bytes 65568 | tf_op jit(solution)/shard_map/ppermute | solution.py:253
  62.4 4.5 %collective-permute-start.9 = (bf16[128,256]{1,0:T(8,128)(2,1)S(1)}, bf16[128,256]{1,0:T(8,128)(2,1)S(1)}, u32[]{:S(2)}, u32[]{:S(2)}) collective-permute-start(bf16[128,256]{1,0:T(8,128)(2,1)S(1)} %get-tuple-element.44), channel_id=1, source_target_pairs={{0,80},{16,96},{32,112},{48,0},{64,16},{80,32},{96,48},{112,64},{1... | collective-permute-start | bytes 196616 | tf_op jit(solution)/shard_map/ppermute | solution.py:253
  66.8 1.9 collective-permute-done.8.before
  69.7 16.1 %all_to_all.20.u = bf16[16,136,256]{2,1,0:T(8,128)(2,1)S(1)} all-to-all(bf16[16,136,256]{2,1,0:T(8,128)(2,1)S(1)} %update.2), channel_id=1, replica_groups=mesh['yh'=2,'z'=8,'c'=2,'x'=4,'yl'=2] {'x','yl','yh'}, dimensions={0} | all-to-all | bytes 2228224 | tf_op jit(solution)/shard_map/all_to_all | solution.py:282
  85.7 8.1 %main.4 = (f32[256,256]{1,0:T(8,128)S(1)}, f32[256,256]{1,0:T(8,128)S(1)}, f32[8,128]{1,0:T(8,128)S(1)}) custom-call(s32[2]{0:T(128)S(1)} %copy-done.3, f32[4]{0:T(128)S(1)} %copy-done.4, bf16[4,256,2048]{2,1,0:T(8,128)(2,1)} %v1_h.5, bf16[4,256,2048]{2,1,0:T(8,128)(2,1)} %collective-permute-done.v2_h, bf16[4,512,512]{2,1,0:T(8,128)(2,1)} %o1_h.5, ...), custom_call_target="tpu_custom_call" | custom-call | flops 2684354560 | bytes 14225432 | tf_op jit(solution)/shard_map/main/pallas_call | solution.py:31
  93.8 5.8 %collective-permute-start.11 = (f32[256,256]{1,0:T(8,128)S(1)}, f32[256,256]{1,0:T(8,128)S(1)}, u32[]{:S(2)}, u32[]{:S(2)}) collective-permute-start(f32[256,256]{1,0:T(8,128)S(1)} %get-tuple-element.49), channel_id=1, source_target_pairs={{0,8},{8,0},{1,9},{9,1},{2,10},{10,2},{3,11},{11,3},{4,12},{12,4},... | collective-permute-start | bytes 786440 | tf_op jit(solution)/shard_map/ppermute | solution.py:248
  102.4 3.9 %collective-permute-done.13.recv = bf16[128,256]{1,0:T(8,128)(2,1)S(1)} collective-permute-done((bf16[128,256]{1,0:T(8,128)(2,1)S(1)}, bf16[128,256]{1,0:T(8,128)(2,1)S(1)}, u32[]{:S(2)}, u32[]{:S(2)}) %collective-permute-start.13) | collective-permute-done | bytes 65568 | tf_op jit(solution)/shard_map/ppermute | solution.py:248
  107.2 1.6 collective-permute-start.14
  108.7 1.6 collective-permute-done.15.after
  110.3 1.2 collective-permute-done.14.before
  111.5 2.1 %collective-permute-start.16 = (bf16[128,256]{1,0:T(8,128)(2,1)S(1)}, bf16[128,256]{1,0:T(8,128)(2,1)S(1)}, u32[]{:S(2)}, u32[]{:S(2)}) collective-permute-start(bf16[128,256]{1,0:T(8,128)(2,1)S(1)} %get-tuple-element.56), channel_id=1, source_target_pairs={{0,48},{16,64},{32,80},{48,96},{64,112},{80,0},{96,16},{112,32},{1... | collective-permute-start | bytes 196616 | tf_op jit(solution)/shard_map/ppermute | solution.py:253
  113.6 2.5 %collective-permute-start.17 = (bf16[128,256]{1,0:T(8,128)(2,1)S(1)}, bf16[128,256]{1,0:T(8,128)(2,1)S(1)}, u32[]{:S(2)}, u32[]{:S(2)}) collective-permute-start(bf16[128,256]{1,0:T(8,128)(2,1)S(1)} %get-tuple-element.57), channel_id=1, source_target_pairs={{0,80},{16,96},{32,112},{48,0},{64,16},{80,32},{96,48},{112,64},{1... | collective-permute-start | bytes 196616 | tf_op jit(solution)/shard_map/ppermute | solution.py:253
  116.1 1.9 %collective-permute-done.16.before = bf16[128,256]{1,0:T(8,128)(2,1)S(1)} collective-permute-done((bf16[128,256]{1,0:T(8,128)(2,1)S(1)}, bf16[128,256]{1,0:T(8,128)(2,1)S(1)}, u32[]{:S(2)}, u32[]{:S(2)}) %collective-permute-start.16) | collective-permute-done | bytes 65568 | tf_op jit(solution)/shard_map/ppermute | solution.py:253
  120.1 15.4 %all_to_all.21.u = bf16[16,136,256]{2,1,0:T(8,128)(2,1)S(1)} all-to-all(bf16[16,136,256]{2,1,0:T(8,128)(2,1)S(1)} %update.3), channel_id=1, replica_groups=mesh['yh'=2,'z'=8,'c'=2,'x'=4,'yl'=2] {'x','yl','yh'}, dimensions={0} | all-to-all | bytes 2228224 | tf_op jit(solution)/shard_map/all_to_all | solution.py:282
  135.5 8.1 %main.5 = (f32[256,256]{1,0:T(8,128)S(1)}, f32[256,256]{1,0:T(8,128)S(1)}, f32[8,128]{1,0:T(8,128)S(1)}) custom-call(s32[2]{0:T(128)S(1)} %copy-done.3, f32[4]{0:T(128)S(1)} %copy-done.4, bf16[4,256,2048]{2,1,0:T(8,128)(2,1)} %v1_h.5, bf16[4,256,2048]{2,1,0:T(8,128)(2,1)} %collective-permute-done.v2_h, bf16[4,512,512]{2,1,0:T(8,128)(2,1)} %o1_h.5, ...), custom_call_target="tpu_custom_call" | custom-call | flops 2684354560 | bytes 14225432 | tf_op jit(solution)/shard_map/main/pallas_call | solution.py:31
  143.6 6.4 %collective-permute-start.18 = (f32[256,256]{1,0:T(8,128)S(1)}, f32[256,256]{1,0:T(8,128)S(1)}, u32[]{:S(2)}, u32[]{:S(2)}) collective-permute-start(f32[256,256]{1,0:T(8,128)S(1)} %get-tuple-element.59), channel_id=1, source_target_pairs={{0,8},{8,0},{1,9},{9,1},{2,10},{10,2},{3,11},{11,3},{4,12},{12,4},... | collective-permute-start | bytes 786440 | tf_op jit(solution)/shard_map/ppermute | solution.py:248
  152.8 3.9 %collective-permute-done.20.recv = bf16[128,256]{1,0:T(8,128)(2,1)S(1)} collective-permute-done((bf16[128,256]{1,0:T(8,128)(2,1)S(1)}, bf16[128,256]{1,0:T(8,128)(2,1)S(1)}, u32[]{:S(2)}, u32[]{:S(2)}) %collective-permute-start.20) | collective-permute-done | bytes 65568 | tf_op jit(solution)/shard_map/ppermute | solution.py:248
  156.8 20.3 %all_to_all.22.zm = bf16[8,128,256]{2,1,0:T(8,128)(2,1)S(1)} all-to-all(bf16[8,128,256]{2,1,0:T(8,128)(2,1)S(1)} %wide.1), channel_id=1, replica_groups=mesh['yh'=2,'z'=8,'c'=2,'x'=4,'yl'=2] {'z'}, dimensions={0} | all-to-all | bytes 1048576 | tf_op jit(solution)/shard_map/all_to_all | solution.py:332
  177.9 3.9 %collective-permute-start.22 = (f32[128,256]{1,0:T(8,128)S(1)}, f32[128,256]{1,0:T(8,128)S(1)}, u32[]{:S(2)}, u32[]{:S(2)}) collective-permute-start(f32[128,256]{1,0:T(8,128)S(1)} %last.1.w), channel_id=1, source_target_pairs={{0,8},{8,0},{1,9},{9,1},{2,10},{10,2},{3,11},{11,3},{4,12},{12,4},... | collective-permute-start | bytes 393224 | tf_op jit(solution)/shard_map/ppermute | solution.py:248
  182.6 4.8 %collective-permute-start.23 = (f32[128,256]{1,0:T(8,128)S(1)}, f32[128,256]{1,0:T(8,128)S(1)}, u32[]{:S(2)}, u32[]{:S(2)}) collective-permute-start(f32[128,256]{1,0:T(8,128)S(1)} %collective-permute-done.21.wy), channel_id=1, source_target_pairs={{0,8},{8,0},{1,9},{9,1},{2,10},{10,2},{3,11},{11,3},{4,12},{12,4},... | collective-permute-start | bytes 393224 | tf_op jit(solution)/shard_map/ppermute | solution.py:248
  188.4 1.4 join.1
  (48 shorter events, 16.2 us)
Async XLA Ops:
  0.0 31.3 %collective-permute-start = (bf16[4,256,2048]{2,1,0:T(8,128)(2,1)}, bf16[4,256,2048]{2,1,0:T(8,128)(2,1)}, u32[]{:S(2)}, u32[]{:S(2)}) collective-permute-start(bf16[4,256,2048]{2,1,0:T(8,128)(2,1)} %v1_h.5), channel_id=1, source_target_pairs={{0,8},{8,0},{1,9},{9,1},{2,10},{10,2},{3,11},{11,3},{4,12},{12,4},... | collective-permute-start | bytes 12582920 | tf_op jit(solution)/shard_map/ppermute | solution.py:248
  3.2 28.1 %collective-permute-start.1 = (bf16[4,512,512]{2,1,0:T(8,128)(2,1)}, bf16[4,512,512]{2,1,0:T(8,128)(2,1)}, u32[]{:S(2)}, u32[]{:S(2)}) collective-permute-start(bf16[4,512,512]{2,1,0:T(8,128)(2,1)} %o1_h.5), channel_id=1, source_target_pairs={{0,8},{8,0},{1,9},{9,1},{2,10},{10,2},{3,11},{11,3},{4,12},{12,4},... | collective-permute-start | bytes 6291464 | tf_op jit(solution)/shard_map/ppermute | solution.py:248
  8.0 5.2 %copy-start = (bf16[4,256,512]{2,1,0:T(8,128)(2,1)S(1)}, bf16[4,256,512]{2,1,0:T(8,128)(2,1)}, u32[]{:S(2)}) copy-start(bf16[4,256,512]{2,1,0:T(8,128)(2,1)} %ov.11) | copy-start | bytes 3145732
  8.0 23.3 %copy-start.3 = (s32[2]{0:T(128)S(1)}, s32[2]{0:T(128)}, u32[]{:S(2)}) copy-start(s32[2]{0:T(128)} %pad_add_fusion.s) | copy-start | bytes 28
  8.0 23.3 %copy-start.4 = (f32[4]{0:T(128)S(1)}, f32[4]{0:T(128)}, u32[]{:S(2)}) copy-start(f32[4]{0:T(128)} %fit.5) | copy-start | bytes 52
  8.0 23.2 %all-to-all-start = ((bf16[16,136,256]{2,1,0:T(8,128)(2,1)}), bf16[16,136,256]{2,1,0:T(8,128)(2,1)S(1)}, u32[]{:S(2)}, u32[]{:S(2)}) async-start(bf16[16,136,256]{2,1,0:T(8,128)(2,1)} %get-tuple-element.34), calls=%async_computation | async-start | bytes 2228224 | tf_op jit(solution)/shard_map/all_to_all | solution.py:282
  13.2 28.9 %collective-permute-start.4 = (bf16[4,256,512]{2,1,0:T(8,128)(2,1)S(1)}, bf16[4,256,512]{2,1,0:T(8,128)(2,1)S(1)}, u32[]{:S(2)}, u32[]{:S(2)}) collective-permute-start(bf16[4,256,512]{2,1,0:T(8,128)(2,1)S(1)} %copy-done), channel_id=1, source_target_pairs={{0,8},{8,0},{1,9},{9,1},{2,10},{10,2},{3,11},{11,3},{4,12},{12,4},... | collective-permute-start | bytes 3145736 | tf_op jit(solution)/shard_map/ppermute | solution.py:248
  39.4 3.7 %collective-permute-start.2 = (f32[256,256]{1,0:T(8,128)S(1)}, f32[256,256]{1,0:T(8,128)S(1)}, u32[]{:S(2)}, u32[]{:S(2)}) collective-permute-start(f32[256,256]{1,0:T(8,128)S(1)} %get-tuple-element.36), channel_id=1, source_target_pairs={{0,8},{8,0},{1,9},{9,1},{2,10},{10,2},{3,11},{11,3},{4,12},{12,4},... | collective-permute-start | bytes 786440 | tf_op jit(solution)/shard_map/ppermute | solution.py:248
  42.0 1.2 collective-permute-start.3
  44.0 4.7 %collective-permute-start.5 = (bf16[128,256]{1,0:T(8,128)(2,1)S(1)}, bf16[128,256]{1,0:T(8,128)(2,1)S(1)}, u32[]{:S(2)}, u32[]{:S(2)}) collective-permute-start(bf16[128,256]{1,0:T(8,128)(2,1)S(1)} %get-tuple-element.39), channel_id=1, source_target_pairs={{0,128},{128,0},{1,129},{129,1},{2,130},{130,2},{3,131},{131,3},{4... | collective-permute-start | bytes 196616 | tf_op jit(solution)/shard_map/ppermute | solution.py:248
  48.7 20.0 %copy-start.1 = (f32[128,256]{1,0:T(8,128)S(1)}, f32[128,256]{1,0:T(8,128)}, u32[]{:S(2)}) copy-start(f32[128,256]{1,0:T(8,128)} %get-tuple-element.45.rq) | copy-start | bytes 393220
  48.7 20.0 %copy-start.2 = (f32[128,256]{1,0:T(8,128)S(1)}, f32[128,256]{1,0:T(8,128)}, u32[]{:S(2)}) copy-start(f32[128,256]{1,0:T(8,128)} %get-tuple-element.46.dq) | copy-start | bytes 393220
  49.3 19.4 %collective-permute-start.10 = (bf16[8,128,256]{2,1,0:T(8,128)(2,1)S(1)}, bf16[8,128,256]{2,1,0:T(8,128)(2,1)S(1)}, u32[]{:S(2)}, u32[]{:S(2)}) collective-permute-start(bf16[8,128,256]{2,1,0:T(8,128)(2,1)S(1)} %get-tuple-element.47), channel_id=1, source_target_pairs={{0,128},{128,0},{1,129},{129,1},{2,130},{130,2},{3,131},{131,3},{4... | collective-permute-start | bytes 1572872 | tf_op jit(solution)/shard_map/ppermute | solution.py:248
  52.0 6.9 %collective-permute-start.7 = (bf16[128,256]{1,0:T(8,128)(2,1)S(1)}, bf16[128,256]{1,0:T(8,128)(2,1)S(1)}, u32[]{:S(2)}, u32[]{:S(2)}) collective-permute-start(bf16[128,256]{1,0:T(8,128)(2,1)S(1)} %get-tuple-element.41), channel_id=1, source_target_pairs={{0,112},{16,0},{32,16},{48,32},{64,48},{80,64},{96,80},{112,96},{1... | collective-permute-start | bytes 196616 | tf_op jit(solution)/shard_map/ppermute | solution.py:253
  57.6 4.6 %collective-permute-start.6 = (bf16[128,256]{1,0:T(8,128)(2,1)S(1)}, bf16[128,256]{1,0:T(8,128)(2,1)S(1)}, u32[]{:S(2)}, u32[]{:S(2)}) collective-permute-start(bf16[128,256]{1,0:T(8,128)(2,1)S(1)} %get-tuple-element.41), channel_id=1, source_target_pairs={{0,16},{16,32},{32,48},{48,64},{64,80},{80,96},{96,112},{112,0},{1... | collective-permute-start | bytes 196616 | tf_op jit(solution)/shard_map/ppermute | solution.py:253
  62.3 6.4 %collective-permute-start.8 = (bf16[128,256]{1,0:T(8,128)(2,1)S(1)}, bf16[128,256]{1,0:T(8,128)(2,1)S(1)}, u32[]{:S(2)}, u32[]{:S(2)}) collective-permute-start(bf16[128,256]{1,0:T(8,128)(2,1)S(1)} %get-tuple-element.43), channel_id=1, source_target_pairs={{0,48},{16,64},{32,80},{48,96},{64,112},{80,0},{96,16},{112,32},{1... | collective-permute-start | bytes 196616 | tf_op jit(solution)/shard_map/ppermute | solution.py:253
  62.4 6.4 %collective-permute-start.9 = (bf16[128,256]{1,0:T(8,128)(2,1)S(1)}, bf16[128,256]{1,0:T(8,128)(2,1)S(1)}, u32[]{:S(2)}, u32[]{:S(2)}) collective-permute-start(bf16[128,256]{1,0:T(8,128)(2,1)S(1)} %get-tuple-element.44), channel_id=1, source_target_pairs={{0,80},{16,96},{32,112},{48,0},{64,16},{80,32},{96,48},{112,64},{1... | collective-permute-start | bytes 196616 | tf_op jit(solution)/shard_map/ppermute | solution.py:253
  93.8 6.9 %collective-permute-start.11 = (f32[256,256]{1,0:T(8,128)S(1)}, f32[256,256]{1,0:T(8,128)S(1)}, u32[]{:S(2)}, u32[]{:S(2)}) collective-permute-start(f32[256,256]{1,0:T(8,128)S(1)} %get-tuple-element.49), channel_id=1, source_target_pairs={{0,8},{8,0},{1,9},{9,1},{2,10},{10,2},{3,11},{11,3},{4,12},{12,4},... | collective-permute-start | bytes 786440 | tf_op jit(solution)/shard_map/ppermute | solution.py:248
  99.6 1.2 collective-permute-start.12
  101.6 4.7 %collective-permute-start.13 = (bf16[128,256]{1,0:T(8,128)(2,1)S(1)}, bf16[128,256]{1,0:T(8,128)(2,1)S(1)}, u32[]{:S(2)}, u32[]{:S(2)}) collective-permute-start(bf16[128,256]{1,0:T(8,128)(2,1)S(1)} %get-tuple-element.52), channel_id=1, source_target_pairs={{0,128},{128,0},{1,129},{129,1},{2,130},{130,2},{3,131},{131,3},{4... | collective-permute-start | bytes 196616 | tf_op jit(solution)/shard_map/ppermute | solution.py:248
  106.3 3.9 %collective-permute-start.15 = (bf16[128,256]{1,0:T(8,128)(2,1)S(1)}, bf16[128,256]{1,0:T(8,128)(2,1)S(1)}, u32[]{:S(2)}, u32[]{:S(2)}) collective-permute-start(bf16[128,256]{1,0:T(8,128)(2,1)S(1)} %get-tuple-element.54), channel_id=1, source_target_pairs={{0,112},{16,0},{32,16},{48,32},{64,48},{80,64},{96,80},{112,96},{1... | collective-permute-start | bytes 196616 | tf_op jit(solution)/shard_map/ppermute | solution.py:253
  107.2 4.3 %collective-permute-start.14 = (bf16[128,256]{1,0:T(8,128)(2,1)S(1)}, bf16[128,256]{1,0:T(8,128)(2,1)S(1)}, u32[]{:S(2)}, u32[]{:S(2)}) collective-permute-start(bf16[128,256]{1,0:T(8,128)(2,1)S(1)} %get-tuple-element.54), channel_id=1, source_target_pairs={{0,16},{16,32},{32,48},{48,64},{64,80},{80,96},{96,112},{112,0},{1... | collective-permute-start | bytes 196616 | tf_op jit(solution)/shard_map/ppermute | solution.py:253
  111.5 6.5 %collective-permute-start.16 = (bf16[128,256]{1,0:T(8,128)(2,1)S(1)}, bf16[128,256]{1,0:T(8,128)(2,1)S(1)}, u32[]{:S(2)}, u32[]{:S(2)}) collective-permute-start(bf16[128,256]{1,0:T(8,128)(2,1)S(1)} %get-tuple-element.56), channel_id=1, source_target_pairs={{0,48},{16,64},{32,80},{48,96},{64,112},{80,0},{96,16},{112,32},{1... | collective-permute-start | bytes 196616 | tf_op jit(solution)/shard_map/ppermute | solution.py:253
  113.6 5.6 %collective-permute-start.17 = (bf16[128,256]{1,0:T(8,128)(2,1)S(1)}, bf16[128,256]{1,0:T(8,128)(2,1)S(1)}, u32[]{:S(2)}, u32[]{:S(2)}) collective-permute-start(bf16[128,256]{1,0:T(8,128)(2,1)S(1)} %get-tuple-element.57), channel_id=1, source_target_pairs={{0,80},{16,96},{32,112},{48,0},{64,16},{80,32},{96,48},{112,64},{1... | collective-permute-start | bytes 196616 | tf_op jit(solution)/shard_map/ppermute | solution.py:253
  143.6 7.6 %collective-permute-start.18 = (f32[256,256]{1,0:T(8,128)S(1)}, f32[256,256]{1,0:T(8,128)S(1)}, u32[]{:S(2)}, u32[]{:S(2)}) collective-permute-start(f32[256,256]{1,0:T(8,128)S(1)} %get-tuple-element.59), channel_id=1, source_target_pairs={{0,8},{8,0},{1,9},{9,1},{2,10},{10,2},{3,11},{11,3},{4,12},{12,4},... | collective-permute-start | bytes 786440 | tf_op jit(solution)/shard_map/ppermute | solution.py:248
  150.1 1.2 collective-permute-start.19
  152.1 4.7 %collective-permute-start.20 = (bf16[128,256]{1,0:T(8,128)(2,1)S(1)}, bf16[128,256]{1,0:T(8,128)(2,1)S(1)}, u32[]{:S(2)}, u32[]{:S(2)}) collective-permute-start(bf16[128,256]{1,0:T(8,128)(2,1)S(1)} %get-tuple-element.62), channel_id=1, source_target_pairs={{0,128},{128,0},{1,129},{129,1},{2,130},{130,2},{3,131},{131,3},{4... | collective-permute-start | bytes 196616 | tf_op jit(solution)/shard_map/ppermute | solution.py:248
  177.2 5.4 %collective-permute-start.21 = (f32[128,256]{1,0:T(8,128)S(1)}, f32[128,256]{1,0:T(8,128)S(1)}, u32[]{:S(2)}, u32[]{:S(2)}) collective-permute-start(f32[128,256]{1,0:T(8,128)S(1)} %last.1.w), channel_id=1, source_target_pairs={{0,128},{128,0},{1,129},{129,1},{2,130},{130,2},{3,131},{131,3},{4... | collective-permute-start | bytes 393224 | tf_op jit(solution)/shard_map/ppermute | solution.py:248
  177.9 9.5 %collective-permute-start.22 = (f32[128,256]{1,0:T(8,128)S(1)}, f32[128,256]{1,0:T(8,128)S(1)}, u32[]{:S(2)}, u32[]{:S(2)}) collective-permute-start(f32[128,256]{1,0:T(8,128)S(1)} %last.1.w), channel_id=1, source_target_pairs={{0,8},{8,0},{1,9},{9,1},{2,10},{10,2},{3,11},{11,3},{4,12},{12,4},... | collective-permute-start | bytes 393224 | tf_op jit(solution)/shard_map/ppermute | solution.py:248
  182.6 5.8 %collective-permute-start.23 = (f32[128,256]{1,0:T(8,128)S(1)}, f32[128,256]{1,0:T(8,128)S(1)}, u32[]{:S(2)}, u32[]{:S(2)}) collective-permute-start(f32[128,256]{1,0:T(8,128)S(1)} %collective-permute-done.21.wy), channel_id=1, source_target_pairs={{0,8},{8,0},{1,9},{9,1},{2,10},{10,2},{3,11},{11,3},{4,12},{12,4},... | collective-permute-start | bytes 393224 | tf_op jit(solution)/shard_map/ppermute | solution.py:248

commit v5 on v4

--- a/solution.py
+++ b/solution.py
@@ -27,7 +27,7 @@
 
 def kernel(body, name, outputs, scratch=(), limit=8, flops=0, scalars=1, far=(), out=()):
     def call(*args):
-        moved = sum(math.prod(a.shape) * a.dtype.itemsize for a in (*args, *outputs))
+        moved = sum(math.prod(a.shape) * jnp.dtype(a.dtype).itemsize for a in (*args, *outputs))
         return pl.pallas_call(
             body,
             out_shape=list(outputs),
@@ -87,7 +87,7 @@
 
 
 def start_body(
-    s, rhs_h, ev_h, eo_h, ov_h, msg_h, rq, dq, rhs, ev, eo, ov, msg, keep, den, sems
+    s, rhs_h, ev_h, eo_h, ov_h, msg, rq, dq, rhs, ev, eo, ov, keep, den, sems
 ):
     c, yh = s[0], s[1]
     copies = [
@@ -121,30 +121,22 @@
         jnp.where(yh == 0, g, zero),
         jnp.where(yh == 0, zero, g),
     )
-    out = pltpu.make_async_copy(msg, msg_h, sems.at[4])
-    out.start()
-    out.wait()
-
-
-def main_body(
-    s, fit, v1_h, v2_h, o1_h, o2_h, u, keep, send, part, v, o, full, zs, gs, sems
-):
-    c, yh = s[0], s[1]
-    pieces = ((v1_h, 0, 1), (v1_h, 1, 4), (v2_h, 0, 4))
-    copies = []
-    for k, (src, low, high) in enumerate(pieces):
-        dst = v.at[pl.ds(low + (4 if src is v2_h else 0), high - low)]
-        copies.append(
-            pltpu.make_async_copy(src.at[pl.ds(low, high - low)], dst, sems.at[k])
-        )
-    for k, src in enumerate((o1_h, o2_h)):
-        copies.append(
-            pltpu.make_async_copy(
-                src.at[:, at(c, 256), :], o.at[pl.ds(4 * k, 4)], sems.at[3 + k]
-            )
-        )
+
+
+def load_body(s, v1, v2, after, v, sems):
+    copies = [
+        pltpu.make_async_copy(src.at[q], v.at[4 * k + q], sems.at[4 * k + q])
+        for k, src in enumerate((v1, v2))
+        for q in range(4)
+    ]
     for copy in copies:
         copy.start()
+    for copy in copies:
+        copy.wait()
+
+
+def main_body(s, fit, v, o1, o2, u, keep, send, part, full, zs, gs, ac):
+    c, yh = s[0], s[1]
     g = jnp.zeros((GROWS, COLS), F32)
     for p in range(16):
         full[p * ROWS : (p + 1) * ROWS, :] = u[p, :ROWS, :]
@@ -154,25 +146,18 @@
     g = g + pltpu.roll(g, 1, 1)
     own = [jnp.full((1, 128), SCALE * fit[q], F32) for q in range(4)]
     part[...] = jnp.concatenate([*own, jnp.zeros((4, 128), F32)], axis=0) - 4.0 * g
-    for k, (low, high) in enumerate(((0, 1), (1, 4), (4, 8))):
-        copies[k].wait()
+    for k in range(2):
         z = jnp.dot(
-            v[low:high].reshape((high - low) * 256, V),
+            v[4 * k : 4 * k + 4].reshape(4 * 256, V),
             full[...],
             preferred_element_type=F32,
         ).astype(BF)
-        for q in range(low, high):
-            zs[:, q * 256 : (q + 1) * 256] = z[(q - low) * 256 : (q - low + 1) * 256]
-    copies[3].wait()
-    copies[4].wait()
-    a = jnp.zeros((256, COLS), F32)
-    b = jnp.zeros((256, COLS), F32)
-    for q in range(8):
-        zq = zs[:, q * 256 : (q + 1) * 256]
-        a += jnp.dot(zq, o[q, :, at(c, COLS)], preferred_element_type=F32)
-        b += jnp.dot(zq, o[q, :, at(1 - c, COLS)], preferred_element_type=F32)
-    keep[...] = a
-    send[...] = b
+        for q in range(4):
+            zs[:, (k * 4 + q) * 256 : (k * 4 + q + 1) * 256] = z[q * 256 : (q + 1) * 256]
+    o = jnp.concatenate([r[q, at(c, 256), :] for r in (o1, o2) for q in range(4)], axis=0)
+    ac[...] = jnp.dot(zs[...], o, preferred_element_type=F32)
+    keep[...] = ac[:, at(c, COLS)]
+    send[...] = ac[:, at(1 - c, COLS)]
 
 
 def pair_body(s, keep, got, part, partsw, ov, ov2, mine, other, tot):
@@ -267,36 +252,54 @@
             pltpu.VMEM((1, 256), F32),
             pltpu.VMEM((1, O), F32),
             pltpu.VMEM((4, 256, O), BF),
-            pltpu.VMEM((16, PIECE, COLS), BF),
             pltpu.VMEM((256, O), BF),
             pltpu.VMEM((256, O), F32),
             pltpu.SemaphoreType.DMA((5,)),
         ],
-        limit=60,
+        limit=12,
         far=range(1, 5),
-        out=(0,),
-    )(s, rhs, eps_vir[None, :], eps_occ[None, :], b_ov)
-    vv2, oo2, ov2 = swap(b_vv, "c"), swap(b_oo, "c"), swap(b_ov, "c")
+    )(
+        s,
+        *(
+            pltpu.with_memory_space_constraint(a, pltpu.HBM)
+            for a in (rhs, eps_vir[None, :], eps_occ[None, :], b_ov)
+        ),
+    )
+    vv2, oo2 = swap(b_vv, "c"), swap(b_oo, "c")
     oth = None
     for step in range(ITERS):
         msg = lax.all_to_all(msg, PLANE, 0, 0, tiled=True)
+        if oth is None:
+            msg, b_ov, fit_pert, s = lax.optimization_barrier((msg, b_ov, fit_pert, s))
+            ov2 = swap(b_ov, "c")
+            (vv,) = kernel(
+                load_body,
+                "load",
+                [pltpu.VMEM((8, 256, V), BF)],
+                [pltpu.SemaphoreType.DMA((8,))],
+                far=(1, 2),
+            )(
+                s,
+                *(
+                    pltpu.with_memory_space_constraint(a, pltpu.HBM)
+                    for a in (b_vv, vv2)
+                ),
+                msg[:1, :8, :128],
+            )
         keep, send, part = kernel(
             main_body,
             "main",
             [sds(256, COLS), sds(256, COLS), sds(8, 128)],
             [
-                pltpu.VMEM((8, 256, V), BF),
-                pltpu.VMEM((8, 256, O), BF),
                 pltpu.VMEM((V, COLS), BF),
                 pltpu.VMEM((256, V), BF),
                 pltpu.VMEM((GROWS, COLS), F32),
-                pltpu.SemaphoreType.DMA((5,)),
+                pltpu.VMEM((256, O), F32),
             ],
-            limit=52,
-            far=range(2, 6),
+            limit=12,
             flops=2 * 8 * 256 * 256 * (V + O),
             scalars=2,
-        )(s, fit_pert, b_vv, vv2, b_oo, oo2, msg)
+        )(s, fit_pert, vv, b_oo, oo2, msg)
         mine, other = kernel(
             pair_body, "pair", [tile, half], [pltpu.VMEM((256, COLS), F32)]
         )(s, keep, swap(send, "c"), part, swap(part, "c"), b_ov, ov2)

time: 190 us -> 177 us (0.932)
  blocking collectives: 51.7 us -> 75.7 us
  waiting for transfers between devices: 44.2 us -> 30.3 us
  Pallas kernels: 35 us -> 23.3 us
  starting transfers between devices: 58.1 us -> 46.9 us
    all_to_all x2 -> x3, blocking collectives: 31.4 us -> 56.1 us  [local(): msg = lax.all_to_all(msg, PLANE, 0, 0, tiled=True)]
    all_to_all x1 -> x0, waiting for transfers between devices: 17.2 us -> none  [local(): msg = lax.all_to_all(msg, PLANE, 0, 0, tiled=True)]
    pallas_call x16 -> x17, Pallas kernels: 35 us -> 23.3 us  [call(): pl.pallas_call(body, out_shape=list(outputs), in_specs=[pl.BlockSpec(memo...]
    ppermute x16, starting transfers between devices: 35.9 us -> 29.5 us  [swap(): return lax.ppermute(value, axis, [(0, 1), (1, 0)])]
    all_to_all x1 -> x0, starting transfers between devices: 5.19 us -> none  [local(): msg = lax.all_to_all(msg, PLANE, 0, 0, tiled=True)]
    ppermute x16, waiting for transfers between devices: 14.6 us -> 17.2 us  [swap(): return lax.ppermute(value, axis, [(0, 1), (1, 0)])]
  transfers between devices with their start and end apart: 25 -> 24, of which waited for: 16 -> 15; matrix products, arithmetic and copies ran while one was open for 0% -> 0% of each run, Pallas kernels for 6% -> 6%
where the time goes in v5:
time: 177 us; the launch traced here: 176 us
  blocking collectives  75.7 us (43%)
  starting transfers between devices  46.9 us (26%)
  waiting for transfers between devices  30.3 us (17%)
  Pallas kernels  23.3 us (13%)
    all_to_all x3, blocking collectives, local(): msg = lax.all_to_all(msg, PLANE, 0, 0, tiled=True)  56.1 us
    ppermute x16, starting transfers between devices, swap(): return lax.ppermute(value, axis, [(0, 1), (1, 0)])  29.5 us
    pallas_call x17, Pallas kernels, call(): pl.pallas_call(body, out_shape=list(outputs), in_specs=[pl.BlockSpec(memo...  23.3 us
    all_to_all x1, blocking collectives, local(): zm = lax.all_to_all(zm, 'z', 0, 0, tiled=True)  19.7 us
    ppermute x8, starting transfers between devices, along_z(): return lax.ppermute(value, 'z', [(i, (i + shift) % n) for i in range(n)])  17.4 us
    ppermute x16, waiting for transfers between devices, swap(): return lax.ppermute(value, axis, [(0, 1), (1, 0)])  17.2 us
    ppermute x8, waiting for transfers between devices, along_z(): return lax.ppermute(value, 'z', [(i, (i + shift) % n) for i in range(n)])  13 us
  transfers between devices with their start and end apart: 24, of which 15 were waited for; matrix products, arithmetic and copies ran while one was open for 0% of the time, Pallas kernels for 6%

profile of v5, /device:TPU:1, one launch (start us, length us, event | category | flops | bytes accessed | tf_op | source)
XLA Modules:
  0.0 176.5 jit_solution(3147898535392177332)
XLA Ops:
  0.0 3.2 %collective-permute-start = (bf16[4,256,2048]{2,1,0:T(8,128)(2,1)}, bf16[4,256,2048]{2,1,0:T(8,128)(2,1)}, u32[]{:S(2)}, u32[]{:S(2)}) collective-permute-start(bf16[4,256,2048]{2,1,0:T(8,128)(2,1)} %v1.1), channel_id=1, source_target_pairs={{0,8},{8,0},{1,9},{9,1},{2,10},{10,2},{3,11},{11,3},{4,12},{12,4},... | collective-permute-start | bytes 12582920 | tf_op jit(solution)/shard_map/ppermute | solution.py:233
  3.3 2.4 %start.1 = (bf16[16,136,256]{2,1,0:T(8,128)(2,1)S(1)}, f32[128,256]{1,0:T(8,128)S(1)}, f32[128,256]{1,0:T(8,128)S(1)}) custom-call(s32[2]{0:T(128)S(1)} %pad_add_fusion.s, f32[256,512]{1,0:T(8,128)} %rhs_h.1, f32[1,256]{1,0:T(1,128)} %bitcast.5, f32[1,512]{1,0:T(1,128)} %bitcast.4, bf16[4,256,512]{2,1,0:T(8,128)(2,1)} %ov.5), custom_call_target="tpu_custom_call" | custom-call | bytes 2952200 | tf_op jit(solution)/shard_map/start/pallas_call | solution.py:31
  5.7 22.2 %all_to_all.20.u = bf16[16,136,256]{2,1,0:T(8,128)(2,1)S(1)} all-to-all(bf16[16,136,256]{2,1,0:T(8,128)(2,1)S(1)} %get-tuple-element.38), channel_id=1, replica_groups=mesh['yh'=2,'z'=8,'c'=2,'x'=4,'yl'=2] {'x','yl','yh'}, dimensions={0} | all-to-all | bytes 2228224 | tf_op jit(solution)/shard_map/all_to_all | solution.py:271
  27.9 1.9 %collective-permute-start.4 = (bf16[4,256,512]{2,1,0:T(8,128)(2,1)S(1)}, bf16[4,256,512]{2,1,0:T(8,128)(2,1)S(1)}, u32[]{:S(2)}, u32[]{:S(2)}) collective-permute-start(bf16[4,256,512]{2,1,0:T(8,128)(2,1)S(1)} %copy-done), channel_id=1, source_target_pairs={{0,8},{8,0},{1,9},{9,1},{2,10},{10,2},{3,11},{11,3},{4,12},{12,4},... | collective-permute-start | bytes 3145736 | tf_op jit(solution)/shard_map/ppermute | solution.py:233
  29.8 4.1 %load.1.v = bf16[8,256,2048]{2,1,0:T(8,128)(2,1)S(1)} custom-call(s32[2]{0:T(128)S(1)} %pad_add_fusion.s, bf16[4,256,2048]{2,1,0:T(8,128)(2,1)} %v1.1, bf16[4,256,2048]{2,1,0:T(8,128)(2,1)} %collective-permute-done.v2, bf16[1,8,128]{2,1,0:T(8,128)(2,1)S(1)} %slice.3.after), custom_call_target="tpu_custom_call" | custom-call | bytes 16779272 | tf_op jit(solution)/shard_map/load/pallas_call | solution.py:31
  34.0 3.4 %main.3 = (f32[256,256]{1,0:T(8,128)S(1)}, f32[256,256]{1,0:T(8,128)S(1)}, f32[8,128]{1,0:T(8,128)S(1)}) custom-call(s32[2]{0:T(128)S(1)} %pad_add_fusion.s, f32[4]{0:T(128)S(1)} %copy-done.2, bf16[8,256,2048]{2,1,0:T(8,128)(2,1)S(1)} %load.1.v, bf16[4,512,512]{2,1,0:T(8,128)(2,1)S(1)} %copy-done.1, bf16[4,512,512]{2,1,0:T(8,128)(2,1)S(1)} %collective-permute-done.1.o2, ...), custom_call_target="tpu_custom_call" | custom-call | flops 2684354560 | bytes 14225432 | tf_op jit(solution)/shard_map/main/pallas_call | solution.py:31
  40.6 4.4 %collective-permute-done.5.recv = bf16[128,256]{1,0:T(8,128)(2,1)S(1)} collective-permute-done((bf16[128,256]{1,0:T(8,128)(2,1)S(1)}, bf16[128,256]{1,0:T(8,128)(2,1)S(1)}, u32[]{:S(2)}, u32[]{:S(2)}) %collective-permute-start.5) | collective-permute-done | bytes 65568 | tf_op jit(solution)/shard_map/ppermute | solution.py:233
  46.3 1.6 collective-permute-start.6
  47.9 3.9 %collective-permute-start.7 = (bf16[128,256]{1,0:T(8,128)(2,1)S(1)}, bf16[128,256]{1,0:T(8,128)(2,1)S(1)}, u32[]{:S(2)}, u32[]{:S(2)}) collective-permute-start(bf16[128,256]{1,0:T(8,128)(2,1)S(1)} %get-tuple-element.49), channel_id=1, source_target_pairs={{0,112},{16,0},{32,16},{48,32},{64,48},{80,64},{96,80},{112,96},{1... | collective-permute-start | bytes 196616 | tf_op jit(solution)/shard_map/ppermute | solution.py:238
  51.9 1.9 %collective-permute-done.6.before = bf16[128,256]{1,0:T(8,128)(2,1)S(1)} collective-permute-done((bf16[128,256]{1,0:T(8,128)(2,1)S(1)}, bf16[128,256]{1,0:T(8,128)(2,1)S(1)}, u32[]{:S(2)}, u32[]{:S(2)}) %collective-permute-start.6) | collective-permute-done | bytes 65568 | tf_op jit(solution)/shard_map/ppermute | solution.py:238
  53.9 4.4 %collective-permute-start.8 = (bf16[128,256]{1,0:T(8,128)(2,1)S(1)}, bf16[128,256]{1,0:T(8,128)(2,1)S(1)}, u32[]{:S(2)}, u32[]{:S(2)}) collective-permute-start(bf16[128,256]{1,0:T(8,128)(2,1)S(1)} %get-tuple-element.51), channel_id=1, source_target_pairs={{0,48},{16,64},{32,80},{48,96},{64,112},{80,0},{96,16},{112,32},{1... | collective-permute-start | bytes 196616 | tf_op jit(solution)/shard_map/ppermute | solution.py:238
  58.4 1.8 collective-permute-done.8.before
  60.2 3.1 %collective-permute-done.9.after = bf16[128,256]{1,0:T(8,128)(2,1)S(1)} collective-permute-done((bf16[128,256]{1,0:T(8,128)(2,1)S(1)}, bf16[128,256]{1,0:T(8,128)(2,1)S(1)}, u32[]{:S(2)}, u32[]{:S(2)}) %collective-permute-start.9) | collective-permute-done | bytes 65568 | tf_op jit(solution)/shard_map/ppermute | solution.py:238
  64.2 18.2 %all_to_all.21.u = bf16[16,136,256]{2,1,0:T(8,128)(2,1)S(1)} all-to-all(bf16[16,136,256]{2,1,0:T(8,128)(2,1)S(1)} %update.2), channel_id=1, replica_groups=mesh['yh'=2,'z'=8,'c'=2,'x'=4,'yl'=2] {'x','yl','yh'}, dimensions={0} | all-to-all | bytes 2228224 | tf_op jit(solution)/shard_map/all_to_all | solution.py:271
  82.4 3.4 %main.4 = (f32[256,256]{1,0:T(8,128)S(1)}, f32[256,256]{1,0:T(8,128)S(1)}, f32[8,128]{1,0:T(8,128)S(1)}) custom-call(s32[2]{0:T(128)S(1)} %pad_add_fusion.s, f32[4]{0:T(128)S(1)} %copy-done.2, bf16[8,256,2048]{2,1,0:T(8,128)(2,1)S(1)} %load.1.v, bf16[4,512,512]{2,1,0:T(8,128)(2,1)S(1)} %copy-done.1, bf16[4,512,512]{2,1,0:T(8,128)(2,1)S(1)} %collective-permute-done.1.o2, ...), custom_call_target="tpu_custom_call" | custom-call | flops 2684354560 | bytes 14225432 | tf_op jit(solution)/shard_map/main/pallas_call | solution.py:31
  85.9 5.0 %collective-permute-start.11 = (f32[256,256]{1,0:T(8,128)S(1)}, f32[256,256]{1,0:T(8,128)S(1)}, u32[]{:S(2)}, u32[]{:S(2)}) collective-permute-start(f32[256,256]{1,0:T(8,128)S(1)} %get-tuple-element.57), channel_id=1, source_target_pairs={{0,8},{8,0},{1,9},{9,1},{2,10},{10,2},{3,11},{11,3},{4,12},{12,4},... | collective-permute-start | bytes 786440 | tf_op jit(solution)/shard_map/ppermute | solution.py:233
  90.9 1.1 collective-permute-done.12.partsw
  93.6 3.9 %collective-permute-done.13.recv = bf16[128,256]{1,0:T(8,128)(2,1)S(1)} collective-permute-done((bf16[128,256]{1,0:T(8,128)(2,1)S(1)}, bf16[128,256]{1,0:T(8,128)(2,1)S(1)}, u32[]{:S(2)}, u32[]{:S(2)}) %collective-permute-start.13) | collective-permute-done | bytes 65568 | tf_op jit(solution)/shard_map/ppermute | solution.py:233
  97.5 2.6 %collective-permute-start.14 = (bf16[128,256]{1,0:T(8,128)(2,1)S(1)}, bf16[128,256]{1,0:T(8,128)(2,1)S(1)}, u32[]{:S(2)}, u32[]{:S(2)}) collective-permute-start(bf16[128,256]{1,0:T(8,128)(2,1)S(1)} %get-tuple-element.62), channel_id=1, source_target_pairs={{0,16},{16,32},{32,48},{48,64},{64,80},{80,96},{96,112},{112,0},{1... | collective-permute-start | bytes 196616 | tf_op jit(solution)/shard_map/ppermute | solution.py:238
  100.3 1.6 collective-permute-done.14.before
  102.0 1.3 collective-permute-done.15.after
  103.3 2.1 %collective-permute-start.16 = (bf16[128,256]{1,0:T(8,128)(2,1)S(1)}, bf16[128,256]{1,0:T(8,128)(2,1)S(1)}, u32[]{:S(2)}, u32[]{:S(2)}) collective-permute-start(bf16[128,256]{1,0:T(8,128)(2,1)S(1)} %get-tuple-element.64), channel_id=1, source_target_pairs={{0,48},{16,64},{32,80},{48,96},{64,112},{80,0},{96,16},{112,32},{1... | collective-permute-start | bytes 196616 | tf_op jit(solution)/shard_map/ppermute | solution.py:238
  105.4 2.5 %collective-permute-start.17 = (bf16[128,256]{1,0:T(8,128)(2,1)S(1)}, bf16[128,256]{1,0:T(8,128)(2,1)S(1)}, u32[]{:S(2)}, u32[]{:S(2)}) collective-permute-start(bf16[128,256]{1,0:T(8,128)(2,1)S(1)} %get-tuple-element.65), channel_id=1, source_target_pairs={{0,80},{16,96},{32,112},{48,0},{64,16},{80,32},{96,48},{112,64},{1... | collective-permute-start | bytes 196616 | tf_op jit(solution)/shard_map/ppermute | solution.py:238
  107.8 3.1 %collective-permute-done.16.before = bf16[128,256]{1,0:T(8,128)(2,1)S(1)} collective-permute-done((bf16[128,256]{1,0:T(8,128)(2,1)S(1)}, bf16[128,256]{1,0:T(8,128)(2,1)S(1)}, u32[]{:S(2)}, u32[]{:S(2)}) %collective-permute-start.16) | collective-permute-done | bytes 65568 | tf_op jit(solution)/shard_map/ppermute | solution.py:238
  112.1 15.6 %all_to_all.22.u = bf16[16,136,256]{2,1,0:T(8,128)(2,1)S(1)} all-to-all(bf16[16,136,256]{2,1,0:T(8,128)(2,1)S(1)} %update.3), channel_id=1, replica_groups=mesh['yh'=2,'z'=8,'c'=2,'x'=4,'yl'=2] {'x','yl','yh'}, dimensions={0} | all-to-all | bytes 2228224 | tf_op jit(solution)/shard_map/all_to_all | solution.py:271
  127.7 3.4 %main.5 = (f32[256,256]{1,0:T(8,128)S(1)}, f32[256,256]{1,0:T(8,128)S(1)}, f32[8,128]{1,0:T(8,128)S(1)}) custom-call(s32[2]{0:T(128)S(1)} %pad_add_fusion.s, f32[4]{0:T(128)S(1)} %copy-done.2, bf16[8,256,2048]{2,1,0:T(8,128)(2,1)S(1)} %load.1.v, bf16[4,512,512]{2,1,0:T(8,128)(2,1)S(1)} %copy-done.1, bf16[4,512,512]{2,1,0:T(8,128)(2,1)S(1)} %collective-permute-done.1.o2, ...), custom_call_target="tpu_custom_call" | custom-call | flops 2684354560 | bytes 14225432 | tf_op jit(solution)/shard_map/main/pallas_call | solution.py:31
  131.2 6.3 %collective-permute-start.18 = (f32[256,256]{1,0:T(8,128)S(1)}, f32[256,256]{1,0:T(8,128)S(1)}, u32[]{:S(2)}, u32[]{:S(2)}) collective-permute-start(f32[256,256]{1,0:T(8,128)S(1)} %get-tuple-element.67), channel_id=1, source_target_pairs={{0,8},{8,0},{1,9},{9,1},{2,10},{10,2},{3,11},{11,3},{4,12},{12,4},... | collective-permute-start | bytes 786440 | tf_op jit(solution)/shard_map/ppermute | solution.py:233
  140.2 4.0 %collective-permute-done.20.recv = bf16[128,256]{1,0:T(8,128)(2,1)S(1)} collective-permute-done((bf16[128,256]{1,0:T(8,128)(2,1)S(1)}, bf16[128,256]{1,0:T(8,128)(2,1)S(1)}, u32[]{:S(2)}, u32[]{:S(2)}) %collective-permute-start.20) | collective-permute-done | bytes 65568 | tf_op jit(solution)/shard_map/ppermute | solution.py:233
  144.2 19.7 %all_to_all.23.zm = bf16[8,128,256]{2,1,0:T(8,128)(2,1)S(1)} all-to-all(bf16[8,128,256]{2,1,0:T(8,128)(2,1)S(1)} %wide.1), channel_id=1, replica_groups=mesh['yh'=2,'z'=8,'c'=2,'x'=4,'yl'=2] {'z'}, dimensions={0} | all-to-all | bytes 1048576 | tf_op jit(solution)/shard_map/all_to_all | solution.py:335
  164.7 3.9 %collective-permute-start.22 = (f32[128,256]{1,0:T(8,128)S(1)}, f32[128,256]{1,0:T(8,128)S(1)}, u32[]{:S(2)}, u32[]{:S(2)}) collective-permute-start(f32[128,256]{1,0:T(8,128)S(1)} %last.1.w), channel_id=1, source_target_pairs={{0,8},{8,0},{1,9},{9,1},{2,10},{10,2},{3,11},{11,3},{4,12},{12,4},... | collective-permute-start | bytes 393224 | tf_op jit(solution)/shard_map/ppermute | solution.py:233
  169.4 4.7 %collective-permute-start.23 = (f32[128,256]{1,0:T(8,128)S(1)}, f32[128,256]{1,0:T(8,128)S(1)}, u32[]{:S(2)}, u32[]{:S(2)}) collective-permute-start(f32[128,256]{1,0:T(8,128)S(1)} %collective-permute-done.21.wy), channel_id=1, source_target_pairs={{0,8},{8,0},{1,9},{9,1},{2,10},{10,2},{3,11},{11,3},{4,12},{12,4},... | collective-permute-start | bytes 393224 | tf_op jit(solution)/shard_map/ppermute | solution.py:233
  175.1 1.4 join.1
  (45 shorter events, 14.2 us)
Async XLA Ops:
  0.0 29.8 %collective-permute-start = (bf16[4,256,2048]{2,1,0:T(8,128)(2,1)}, bf16[4,256,2048]{2,1,0:T(8,128)(2,1)}, u32[]{:S(2)}, u32[]{:S(2)}) collective-permute-start(bf16[4,256,2048]{2,1,0:T(8,128)(2,1)} %v1.1), channel_id=1, source_target_pairs={{0,8},{8,0},{1,9},{9,1},{2,10},{10,2},{3,11},{11,3},{4,12},{12,4},... | collective-permute-start | bytes 12582920 | tf_op jit(solution)/shard_map/ppermute | solution.py:233
  3.2 30.7 %collective-permute-start.1 = (bf16[4,512,512]{2,1,0:T(8,128)(2,1)}, bf16[4,512,512]{2,1,0:T(8,128)(2,1)S(1)}, u32[]{:S(2)}, u32[]{:S(2)}) collective-permute-start(bf16[4,512,512]{2,1,0:T(8,128)(2,1)} %o1.5), channel_id=1, source_target_pairs={{0,8},{8,0},{1,9},{9,1},{2,10},{10,2},{3,11},{11,3},{4,12},{12,4},... | collective-permute-start | bytes 6291464 | tf_op jit(solution)/shard_map/ppermute | solution.py:233
  5.7 22.2 %copy-start = (bf16[4,256,512]{2,1,0:T(8,128)(2,1)S(1)}, bf16[4,256,512]{2,1,0:T(8,128)(2,1)}, u32[]{:S(2)}) copy-start(bf16[4,256,512]{2,1,0:T(8,128)(2,1)} %ov.5) | copy-start | bytes 3145732
  27.9 10.1 %collective-permute-start.4 = (bf16[4,256,512]{2,1,0:T(8,128)(2,1)S(1)}, bf16[4,256,512]{2,1,0:T(8,128)(2,1)S(1)}, u32[]{:S(2)}, u32[]{:S(2)}) collective-permute-start(bf16[4,256,512]{2,1,0:T(8,128)(2,1)S(1)} %copy-done), channel_id=1, source_target_pairs={{0,8},{8,0},{1,9},{9,1},{2,10},{10,2},{3,11},{11,3},{4,12},{12,4},... | collective-permute-start | bytes 3145736 | tf_op jit(solution)/shard_map/ppermute | solution.py:233
  29.8 4.1 %copy-start.2 = (f32[4]{0:T(128)S(1)}, f32[4]{0:T(128)}, u32[]{:S(2)}) copy-start(f32[4]{0:T(128)} %fit.2) | copy-start | bytes 52
  29.8 4.1 %copy-start.1 = (bf16[4,512,512]{2,1,0:T(8,128)(2,1)S(1)}, bf16[4,512,512]{2,1,0:T(8,128)(2,1)}, u32[]{:S(2)}) copy-start(bf16[4,512,512]{2,1,0:T(8,128)(2,1)} %o1.5) | copy-start | bytes 6291460
  37.4 1.6 collective-permute-start.2
  37.5 1.5 collective-permute-start.3
  39.9 5.1 %collective-permute-start.5 = (bf16[128,256]{1,0:T(8,128)(2,1)S(1)}, bf16[128,256]{1,0:T(8,128)(2,1)S(1)}, u32[]{:S(2)}, u32[]{:S(2)}) collective-permute-start(bf16[128,256]{1,0:T(8,128)(2,1)S(1)} %get-tuple-element.47), channel_id=1, source_target_pairs={{0,128},{128,0},{1,129},{129,1},{2,130},{130,2},{3,131},{131,3},{4... | collective-permute-start | bytes 196616 | tf_op jit(solution)/shard_map/ppermute | solution.py:233
  45.6 17.7 %collective-permute-start.10 = (bf16[8,128,256]{2,1,0:T(8,128)(2,1)S(1)}, bf16[8,128,256]{2,1,0:T(8,128)(2,1)S(1)}, u32[]{:S(2)}, u32[]{:S(2)}) collective-permute-start(bf16[8,128,256]{2,1,0:T(8,128)(2,1)S(1)} %get-tuple-element.55), channel_id=1, source_target_pairs={{0,128},{128,0},{1,129},{129,1},{2,130},{130,2},{3,131},{131,3},{4... | collective-permute-start | bytes 1572872 | tf_op jit(solution)/shard_map/ppermute | solution.py:233
  46.3 7.5 %collective-permute-start.6 = (bf16[128,256]{1,0:T(8,128)(2,1)S(1)}, bf16[128,256]{1,0:T(8,128)(2,1)S(1)}, u32[]{:S(2)}, u32[]{:S(2)}) collective-permute-start(bf16[128,256]{1,0:T(8,128)(2,1)S(1)} %get-tuple-element.49), channel_id=1, source_target_pairs={{0,16},{16,32},{32,48},{48,64},{64,80},{80,96},{96,112},{112,0},{1... | collective-permute-start | bytes 196616 | tf_op jit(solution)/shard_map/ppermute | solution.py:238
  47.9 5.9 %collective-permute-start.7 = (bf16[128,256]{1,0:T(8,128)(2,1)S(1)}, bf16[128,256]{1,0:T(8,128)(2,1)S(1)}, u32[]{:S(2)}, u32[]{:S(2)}) collective-permute-start(bf16[128,256]{1,0:T(8,128)(2,1)S(1)} %get-tuple-element.49), channel_id=1, source_target_pairs={{0,112},{16,0},{32,16},{48,32},{64,48},{80,64},{96,80},{112,96},{1... | collective-permute-start | bytes 196616 | tf_op jit(solution)/shard_map/ppermute | solution.py:238
  53.9 6.3 %collective-permute-start.8 = (bf16[128,256]{1,0:T(8,128)(2,1)S(1)}, bf16[128,256]{1,0:T(8,128)(2,1)S(1)}, u32[]{:S(2)}, u32[]{:S(2)}) collective-permute-start(bf16[128,256]{1,0:T(8,128)(2,1)S(1)} %get-tuple-element.51), channel_id=1, source_target_pairs={{0,48},{16,64},{32,80},{48,96},{64,112},{80,0},{96,16},{112,32},{1... | collective-permute-start | bytes 196616 | tf_op jit(solution)/shard_map/ppermute | solution.py:238
  58.2 5.0 %collective-permute-start.9 = (bf16[128,256]{1,0:T(8,128)(2,1)S(1)}, bf16[128,256]{1,0:T(8,128)(2,1)S(1)}, u32[]{:S(2)}, u32[]{:S(2)}) collective-permute-start(bf16[128,256]{1,0:T(8,128)(2,1)S(1)} %get-tuple-element.52), channel_id=1, source_target_pairs={{0,80},{16,96},{32,112},{48,0},{64,16},{80,32},{96,48},{112,64},{1... | collective-permute-start | bytes 196616 | tf_op jit(solution)/shard_map/ppermute | solution.py:238
  85.9 6.1 %collective-permute-start.11 = (f32[256,256]{1,0:T(8,128)S(1)}, f32[256,256]{1,0:T(8,128)S(1)}, u32[]{:S(2)}, u32[]{:S(2)}) collective-permute-start(f32[256,256]{1,0:T(8,128)S(1)} %get-tuple-element.57), channel_id=1, source_target_pairs={{0,8},{8,0},{1,9},{9,1},{2,10},{10,2},{3,11},{11,3},{4,12},{12,4},... | collective-permute-start | bytes 786440 | tf_op jit(solution)/shard_map/ppermute | solution.py:233
  90.8 1.2 collective-permute-start.12
  92.8 4.7 %collective-permute-start.13 = (bf16[128,256]{1,0:T(8,128)(2,1)S(1)}, bf16[128,256]{1,0:T(8,128)(2,1)S(1)}, u32[]{:S(2)}, u32[]{:S(2)}) collective-permute-start(bf16[128,256]{1,0:T(8,128)(2,1)S(1)} %get-tuple-element.60), channel_id=1, source_target_pairs={{0,128},{128,0},{1,129},{129,1},{2,130},{130,2},{3,131},{131,3},{4... | collective-permute-start | bytes 196616 | tf_op jit(solution)/shard_map/ppermute | solution.py:233
  97.5 4.4 %collective-permute-start.14 = (bf16[128,256]{1,0:T(8,128)(2,1)S(1)}, bf16[128,256]{1,0:T(8,128)(2,1)S(1)}, u32[]{:S(2)}, u32[]{:S(2)}) collective-permute-start(bf16[128,256]{1,0:T(8,128)(2,1)S(1)} %get-tuple-element.62), channel_id=1, source_target_pairs={{0,16},{16,32},{32,48},{48,64},{64,80},{80,96},{96,112},{112,0},{1... | collective-permute-start | bytes 196616 | tf_op jit(solution)/shard_map/ppermute | solution.py:238
  100.1 3.1 %collective-permute-start.15 = (bf16[128,256]{1,0:T(8,128)(2,1)S(1)}, bf16[128,256]{1,0:T(8,128)(2,1)S(1)}, u32[]{:S(2)}, u32[]{:S(2)}) collective-permute-start(bf16[128,256]{1,0:T(8,128)(2,1)S(1)} %get-tuple-element.62), channel_id=1, source_target_pairs={{0,112},{16,0},{32,16},{48,32},{64,48},{80,64},{96,80},{112,96},{1... | collective-permute-start | bytes 196616 | tf_op jit(solution)/shard_map/ppermute | solution.py:238
  103.3 7.7 %collective-permute-start.16 = (bf16[128,256]{1,0:T(8,128)(2,1)S(1)}, bf16[128,256]{1,0:T(8,128)(2,1)S(1)}, u32[]{:S(2)}, u32[]{:S(2)}) collective-permute-start(bf16[128,256]{1,0:T(8,128)(2,1)S(1)} %get-tuple-element.64), channel_id=1, source_target_pairs={{0,48},{16,64},{32,80},{48,96},{64,112},{80,0},{96,16},{112,32},{1... | collective-permute-start | bytes 196616 | tf_op jit(solution)/shard_map/ppermute | solution.py:238
  105.4 5.8 %collective-permute-start.17 = (bf16[128,256]{1,0:T(8,128)(2,1)S(1)}, bf16[128,256]{1,0:T(8,128)(2,1)S(1)}, u32[]{:S(2)}, u32[]{:S(2)}) collective-permute-start(bf16[128,256]{1,0:T(8,128)(2,1)S(1)} %get-tuple-element.65), channel_id=1, source_target_pairs={{0,80},{16,96},{32,112},{48,0},{64,16},{80,32},{96,48},{112,64},{1... | collective-permute-start | bytes 196616 | tf_op jit(solution)/shard_map/ppermute | solution.py:238
  131.2 7.4 %collective-permute-start.18 = (f32[256,256]{1,0:T(8,128)S(1)}, f32[256,256]{1,0:T(8,128)S(1)}, u32[]{:S(2)}, u32[]{:S(2)}) collective-permute-start(f32[256,256]{1,0:T(8,128)S(1)} %get-tuple-element.67), channel_id=1, source_target_pairs={{0,8},{8,0},{1,9},{9,1},{2,10},{10,2},{3,11},{11,3},{4,12},{12,4},... | collective-permute-start | bytes 786440 | tf_op jit(solution)/shard_map/ppermute | solution.py:233
  137.4 1.2 collective-permute-start.19
  139.4 4.7 %collective-permute-start.20 = (bf16[128,256]{1,0:T(8,128)(2,1)S(1)}, bf16[128,256]{1,0:T(8,128)(2,1)S(1)}, u32[]{:S(2)}, u32[]{:S(2)}) collective-permute-start(bf16[128,256]{1,0:T(8,128)(2,1)S(1)} %get-tuple-element.70), channel_id=1, source_target_pairs={{0,128},{128,0},{1,129},{129,1},{2,130},{130,2},{3,131},{131,3},{4... | collective-permute-start | bytes 196616 | tf_op jit(solution)/shard_map/ppermute | solution.py:233
  164.0 5.4 %collective-permute-start.21 = (f32[128,256]{1,0:T(8,128)S(1)}, f32[128,256]{1,0:T(8,128)S(1)}, u32[]{:S(2)}, u32[]{:S(2)}) collective-permute-start(f32[128,256]{1,0:T(8,128)S(1)} %last.1.w), channel_id=1, source_target_pairs={{0,128},{128,0},{1,129},{129,1},{2,130},{130,2},{3,131},{131,3},{4... | collective-permute-start | bytes 393224 | tf_op jit(solution)/shard_map/ppermute | solution.py:233
  164.7 9.4 %collective-permute-start.22 = (f32[128,256]{1,0:T(8,128)S(1)}, f32[128,256]{1,0:T(8,128)S(1)}, u32[]{:S(2)}, u32[]{:S(2)}) collective-permute-start(f32[128,256]{1,0:T(8,128)S(1)} %last.1.w), channel_id=1, source_target_pairs={{0,8},{8,0},{1,9},{9,1},{2,10},{10,2},{3,11},{11,3},{4,12},{12,4},... | collective-permute-start | bytes 393224 | tf_op jit(solution)/shard_map/ppermute | solution.py:233
  169.4 5.7 %collective-permute-start.23 = (f32[128,256]{1,0:T(8,128)S(1)}, f32[128,256]{1,0:T(8,128)S(1)}, u32[]{:S(2)}, u32[]{:S(2)}) collective-permute-start(f32[128,256]{1,0:T(8,128)S(1)} %collective-permute-done.21.wy), channel_id=1, source_target_pairs={{0,8},{8,0},{1,9},{9,1},{2,10},{10,2},{3,11},{11,3},{4,12},{12,4},... | collective-permute-start | bytes 393224 | tf_op jit(solution)/shard_map/ppermute | solution.py:233

commit v6 on v5

--- a/solution.py
+++ b/solution.py
@@ -87,13 +87,13 @@
 
 
 def start_body(
-    s, rhs_h, ev_h, eo_h, ov_h, msg, rq, dq, rhs, ev, eo, ov, keep, den, sems
+    s, rhs_h, ev_h, eo_h, ov_h, v_h, msg, rq, dq, v, rhs, ev, eo, ov, keep, den, sems
 ):
     c, yh = s[0], s[1]
     copies = [
         pltpu.make_async_copy(src, dst, sems.at[k])
         for k, (src, dst) in enumerate(
-            ((ev_h, ev), (eo_h, eo), (rhs_h, rhs), (ov_h, ov))
+            ((ev_h, ev), (eo_h, eo), (rhs_h, rhs), (ov_h, ov), (v_h, v))
         )
     ]
     for copy in copies:
@@ -121,21 +121,18 @@
         jnp.where(yh == 0, g, zero),
         jnp.where(yh == 0, zero, g),
     )
-
-
-def load_body(s, v1, v2, after, v, sems):
-    copies = [
-        pltpu.make_async_copy(src.at[q], v.at[4 * k + q], sems.at[4 * k + q])
-        for k, src in enumerate((v1, v2))
-        for q in range(4)
-    ]
+    copies[4].wait()
+
+
+def load_body(s, v_h, after, v, sems):
+    copies = [pltpu.make_async_copy(v_h.at[q], v.at[q], sems.at[q]) for q in range(4)]
     for copy in copies:
         copy.start()
     for copy in copies:
         copy.wait()
 
 
-def main_body(s, fit, v, o1, o2, u, keep, send, part, full, zs, gs, ac):
+def main_body(s, fit, v1, v2, o1, o2, u, keep, send, part, full, zs, gs, ac):
     c, yh = s[0], s[1]
     g = jnp.zeros((GROWS, COLS), F32)
     for p in range(16):
@@ -146,11 +143,9 @@
     g = g + pltpu.roll(g, 1, 1)
     own = [jnp.full((1, 128), SCALE * fit[q], F32) for q in range(4)]
     part[...] = jnp.concatenate([*own, jnp.zeros((4, 128), F32)], axis=0) - 4.0 * g
-    for k in range(2):
+    for k, v in enumerate((v1, v2)):
         z = jnp.dot(
-            v[4 * k : 4 * k + 4].reshape(4 * 256, V),
-            full[...],
-            preferred_element_type=F32,
+            v[...].reshape(4 * 256, V), full[...], preferred_element_type=F32
         ).astype(BF)
         for q in range(4):
             zs[:, (k * 4 + q) * 256 : (k * 4 + q + 1) * 256] = z[q * 256 : (q + 1) * 256]
@@ -160,8 +155,8 @@
     send[...] = ac[:, at(1 - c, COLS)]
 
 
-def pair_body(s, keep, got, part, partsw, ov, ov2, mine, other, tot):
-    c, yh = s[0], s[1]
+def chip_total(s, keep, got, part, partsw, ov, ov2, tot):
+    c = s[0]
     w = part[...] + jnp.concatenate([partsw[4:8, :], partsw[0:4, :]], axis=0)
     for h in range(2):
         lanes = slice(h * 128, (h + 1) * 128)
@@ -170,6 +165,11 @@
             ref = (ov, ov2)[q // 4]
             acc += ref[q % 4, :, at(c * 2 + h, 128)].astype(F32) * w[q : q + 1, :]
         tot[:, lanes] = acc
+
+
+def pair_body(s, keep, got, part, partsw, ov, ov2, mine, other, tot):
+    yh = s[1]
+    chip_total(s, keep, got, part, partsw, ov, ov2, tot)
     mine[...] = tot[at(yh, ROWS), :]
     other[...] = tot[at(1 - yh, ROWS), :].astype(BF)
 
@@ -195,10 +195,10 @@
     two_half[...] = two.astype(BF)
 
 
-def wide_body(mine, recv, out):
-    total = (mine[...] + recv[...].astype(F32)).astype(BF)
-    for p in range(8):
-        out[p] = total
+def pieces_body(s, keep, got, part, partsw, ov, ov2, out, tot):
+    chip_total(s, keep, got, part, partsw, ov, ov2, tot)
+    for p in range(16):
+        out[p] = tot[p * 16 : (p + 1) * 16, :].astype(BF)
 
 
 def update_body(s, three, before, after, rq, dq, ov, ov2, oth, msg):
@@ -214,19 +214,20 @@
     )
 
 
-def last_body(zm, rq, dq, out):
-    share = zm[0].astype(F32)
-    for p in range(1, 8):
-        share += zm[p].astype(F32)
-    out[...] = (rq[...] + share) / dq[...]
-
-
-def join_body(s, w, wy, wc, wyc, out):
-    c, yh = s[0], s[1]
-    out[at(yh, ROWS), at(c, COLS)] = w[...]
-    out[at(1 - yh, ROWS), at(c, COLS)] = wy[...]
-    out[at(yh, ROWS), at(1 - c, COLS)] = wc[...]
-    out[at(1 - yh, ROWS), at(1 - c, COLS)] = wyc[...]
+def last_body(s, pieces, rq, dq, out):
+    share = pieces[0].astype(F32)
+    for p in range(1, 16):
+        share += pieces[p].astype(F32)
+    rows = at(s[2], 16)
+    w = (rq[rows, :] + share) / dq[rows, :]
+    for p in range(16):
+        out[p] = w
+
+
+def join_body(s, w, wc, out):
+    c = s[0]
+    out[:, at(c, COLS)] = w[...]
+    out[:, at(1 - c, COLS)] = wc[...]
 
 
 def swap(value, axis):
@@ -239,14 +240,14 @@
 
 
 def local(b_ov, b_vv, b_oo, rhs, fit_pert, eps_vir, eps_occ):
-    s = jnp.stack([lax.axis_index("c"), lax.axis_index("yh")]).astype(jnp.int32)
+    s = jnp.stack([lax.axis_index(a) for a in ("c", "yh", "z")]).astype(jnp.int32)
     tile = sds(ROWS, COLS)
     half = sds(ROWS, COLS, dtype=BF)
     message = sds(16, PIECE, COLS, dtype=BF)
-    msg, rq, dq = kernel(
+    msg, rq, dq, v1 = kernel(
         start_body,
         "start",
-        [message, tile, tile],
+        [message, tile, tile, pltpu.VMEM((4, 256, V), BF)],
         [
             pltpu.VMEM((256, O), F32),
             pltpu.VMEM((1, 256), F32),
@@ -257,12 +258,12 @@
             pltpu.SemaphoreType.DMA((5,)),
         ],
         limit=12,
-        far=range(1, 5),
+        far=range(1, 6),
     )(
         s,
         *(
             pltpu.with_memory_space_constraint(a, pltpu.HBM)
-            for a in (rhs, eps_vir[None, :], eps_occ[None, :], b_ov)
+            for a in (rhs, eps_vir[None, :], eps_occ[None, :], b_ov, b_vv)
         ),
     )
     vv2, oo2 = swap(b_vv, "c"), swap(b_oo, "c")
@@ -272,18 +273,15 @@
         if oth is None:
             msg, b_ov, fit_pert, s = lax.optimization_barrier((msg, b_ov, fit_pert, s))
             ov2 = swap(b_ov, "c")
-            (vv,) = kernel(
+            (v2,) = kernel(
                 load_body,
                 "load",
-                [pltpu.VMEM((8, 256, V), BF)],
-                [pltpu.SemaphoreType.DMA((8,))],
-                far=(1, 2),
+                [pltpu.VMEM((4, 256, V), BF)],
+                [pltpu.SemaphoreType.DMA((4,))],
+                far=(1,),
             )(
                 s,
-                *(
-                    pltpu.with_memory_space_constraint(a, pltpu.HBM)
-                    for a in (b_vv, vv2)
-                ),
+                pltpu.with_memory_space_constraint(vv2, pltpu.HBM),
                 msg[:1, :8, :128],
             )
         keep, send, part = kernel(
@@ -299,13 +297,13 @@
             limit=12,
             flops=2 * 8 * 256 * 256 * (V + O),
             scalars=2,
-        )(s, fit_pert, vv, b_oo, oo2, msg)
-        mine, other = kernel(
-            pair_body, "pair", [tile, half], [pltpu.VMEM((256, COLS), F32)]
-        )(s, keep, swap(send, "c"), part, swap(part, "c"), b_ov, ov2)
-        recv = swap(other, "yh")
+        )(s, fit_pert, v1, v2, b_oo, oo2, msg)
+        chip = (s, keep, swap(send, "c"), part, swap(part, "c"), b_ov, ov2)
+        sums = [pltpu.VMEM((256, COLS), F32)]
         if step == ITERS - 1:
             break
+        mine, other = kernel(pair_body, "pair", [tile, half], sums)(*chip)
+        recv = swap(other, "yh")
         if oth is None:
             total, out, ovs = kernel(
                 first_rows_body,
@@ -329,13 +327,11 @@
             ov2,
             oth,
         )
-    (zm,) = kernel(wide_body, "wide", [sds(8, ROWS, COLS, dtype=BF)], scalars=0)(
-        mine, recv
-    )
-    zm = lax.all_to_all(zm, "z", 0, 0, tiled=True)
-    (w,) = kernel(last_body, "last", [tile], scalars=0)(zm, rq, dq)
-    wy, wc = swap(w, "yh"), swap(w, "c")
-    return kernel(join_body, "join", [sds(256, O)])(s, w, wy, wc, swap(wy, "c"))[0]
+    (pieces,) = kernel(pieces_body, "pieces", [sds(16, 16, COLS, dtype=BF)], sums)(*chip)
+    pieces = lax.all_to_all(pieces, ("yh", "z"), 0, 0, tiled=True)
+    (pieces,) = kernel(last_body, "last", [sds(16, 16, COLS)])(s, pieces, rq, dq)
+    w = lax.all_to_all(pieces, ("yh", "z"), 0, 0, tiled=True).reshape(256, COLS)
+    return kernel(join_body, "join", [sds(256, O)])(s, w, swap(w, "c"))[0]
 
 
 def solution(mesh):

time: 177 us -> 173 us (0.977)
  blocking collectives: 75.7 us -> 83.5 us
  starting transfers between devices: 46.9 us -> 39.8 us
  waiting for transfers between devices: 30.3 us -> 25.7 us
    all_to_all x1 -> x2, blocking collectives: 19.7 us -> 27.4 us  [the longest x1 14.2 us: local(): pieces = lax.all_to_all(pieces, ('yh', 'z'), 0, 0, tiled=True)]
    ppermute x16 -> x13, starting transfers between devices: 29.5 us -> 22.4 us  [swap(): return lax.ppermute(value, axis, [(0, 1), (1, 0)])]
    ppermute x16 -> x13, waiting for transfers between devices: 17.2 us -> 12.7 us  [swap(): return lax.ppermute(value, axis, [(0, 1), (1, 0)])]
    pallas_call x17 -> x16, Pallas kernels: 23.3 us -> 23.4 us  [call(): pl.pallas_call(body, out_shape=list(outputs), in_specs=[pl.BlockSpec(memo...]
  transfers between devices with their start and end apart: 24 -> 21, of which waited for: 15 -> 13; matrix products, arithmetic and copies ran while one was open for 0% -> 0% of each run, Pallas kernels for 6% -> 6%
where the time goes in v6:
time: 173 us
  blocking collectives  83.5 us (48%)
  starting transfers between devices  39.8 us (23%)
  waiting for transfers between devices  25.7 us (15%)
  Pallas kernels  23.4 us (14%)
    all_to_all x3, blocking collectives, local(): msg = lax.all_to_all(msg, PLANE, 0, 0, tiled=True)  56.1 us
    pallas_call x16, Pallas kernels, call(): pl.pallas_call(body, out_shape=list(outputs), in_specs=[pl.BlockSpec(memo...  23.4 us
    ppermute x13, starting transfers between devices, swap(): return lax.ppermute(value, axis, [(0, 1), (1, 0)])  22.4 us
    ppermute x8, starting transfers between devices, along_z(): return lax.ppermute(value, 'z', [(i, (i + shift) % n) for i in range(n)])  17.4 us
    all_to_all x1, blocking collectives, local(): pieces = lax.all_to_all(pieces, ('yh', 'z'), 0, 0, tiled=True)  14.2 us
    all_to_all x1, blocking collectives, local(): w = lax.all_to_all(pieces, ('yh', 'z'), 0, 0, tiled=True).reshape(256, COLS)  13.2 us
    ppermute x8, waiting for transfers between devices, along_z(): return lax.ppermute(value, 'z', [(i, (i + shift) % n) for i in range(n)])  13 us
    ppermute x13, waiting for transfers between devices, swap(): return lax.ppermute(value, axis, [(0, 1), (1, 0)])  12.7 us
  transfers between devices with their start and end apart: 21, of which 13 were waited for; matrix products, arithmetic and copies ran while one was open for 0% of the time, Pallas kernels for 6%

profile of v6, /device:TPU:1, one launch (start us, length us, event | category | flops | bytes accessed | tf_op | source)
XLA Modules:
  0.0 172.7 jit_solution(393060842472842776)
XLA Ops:
  0.0 3.2 %collective-permute-start = (bf16[4,256,2048]{2,1,0:T(8,128)(2,1)}, bf16[4,256,2048]{2,1,0:T(8,128)(2,1)}, u32[]{:S(2)}, u32[]{:S(2)}) collective-permute-start(bf16[4,256,2048]{2,1,0:T(8,128)(2,1)} %v_h.1), channel_id=1, source_target_pairs={{0,8},{8,0},{1,9},{9,1},{2,10},{10,2},{3,11},{11,3},{4,12},{12,4},... | collective-permute-start | bytes 12582920 | tf_op jit(solution)/shard_map/ppermute | solution.py:234
  3.3 3.3 %start.1 = (bf16[16,136,256]{2,1,0:T(8,128)(2,1)S(1)}, f32[128,256]{1,0:T(8,128)S(1)}, f32[128,256]{1,0:T(8,128)S(1)}, bf16[4,256,2048]{2,1,0:T(8,128)(2,1)S(1)}) custom-call(s32[3]{0:T(128)S(1)} %pad_add_fusion.s, f32[256,512]{1,0:T(8,128)} %rhs_h.1, f32[1,256]{1,0:T(1,128)} %bitcast.9, f32[1,512]{1,0:T(1,128)} %bitcast.8, bf16[4,256,512]{2,1,0:T(8,128)(2,1)} %ov.5, ...), custom_call_target="tpu_custom_call" | custom-call | bytes 11340812 | tf_op jit(solution)/shard_map/start/pallas_call | solution.py:31
  6.6 22.2 %all_to_all.25.u = bf16[16,136,256]{2,1,0:T(8,128)(2,1)S(1)} all-to-all(bf16[16,136,256]{2,1,0:T(8,128)(2,1)S(1)} %get-tuple-element.37), channel_id=1, replica_groups=mesh['yh'=2,'z'=8,'c'=2,'x'=4,'yl'=2] {'x','yl','yh'}, dimensions={0} | all-to-all | bytes 2228224 | tf_op jit(solution)/shard_map/all_to_all | solution.py:272
  28.8 1.9 %collective-permute-start.4 = (bf16[4,256,512]{2,1,0:T(8,128)(2,1)S(1)}, bf16[4,256,512]{2,1,0:T(8,128)(2,1)S(1)}, u32[]{:S(2)}, u32[]{:S(2)}) collective-permute-start(bf16[4,256,512]{2,1,0:T(8,128)(2,1)S(1)} %copy-done), channel_id=1, source_target_pairs={{0,8},{8,0},{1,9},{9,1},{2,10},{10,2},{3,11},{11,3},{4,12},{12,4},... | collective-permute-start | bytes 3145736 | tf_op jit(solution)/shard_map/ppermute | solution.py:234
  30.7 2.8 %load.1.v2 = bf16[4,256,2048]{2,1,0:T(8,128)(2,1)S(1)} custom-call(s32[3]{0:T(128)S(1)} %pad_add_fusion.s, bf16[4,256,2048]{2,1,0:T(8,128)(2,1)} %collective-permute-done.v_h, bf16[1,8,128]{2,1,0:T(8,128)(2,1)S(1)} %slice.3.after), custom_call_target="tpu_custom_call" | custom-call | bytes 8390668 | tf_op jit(solution)/shard_map/load/pallas_call | solution.py:31
  33.6 3.5 %main.3 = (f32[256,256]{1,0:T(8,128)S(1)}, f32[256,256]{1,0:T(8,128)S(1)}, f32[8,128]{1,0:T(8,128)S(1)}) custom-call(s32[3]{0:T(128)S(1)} %pad_add_fusion.s, f32[4]{0:T(128)S(1)} %copy-done.2, bf16[4,256,2048]{2,1,0:T(8,128)(2,1)S(1)} %get-tuple-element.40.v1, bf16[4,256,2048]{2,1,0:T(8,128)(2,1)S(1)} %load.1.v2, bf16[4,512,512]{2,1,0:T(8,128)(2,1)S(1)} %copy-done.1, ...), custom_call_target="tpu_custom_call" | custom-call | flops 2684354560 | bytes 14225436 | tf_op jit(solution)/shard_map/main/pallas_call | solution.py:31
  40.3 4.4 %collective-permute-done.5.recv = bf16[128,256]{1,0:T(8,128)(2,1)S(1)} collective-permute-done((bf16[128,256]{1,0:T(8,128)(2,1)S(1)}, bf16[128,256]{1,0:T(8,128)(2,1)S(1)}, u32[]{:S(2)}, u32[]{:S(2)}) %collective-permute-start.5) | collective-permute-done | bytes 65568 | tf_op jit(solution)/shard_map/ppermute | solution.py:234
  46.0 1.6 collective-permute-start.6
  47.6 3.9 %collective-permute-start.7 = (bf16[128,256]{1,0:T(8,128)(2,1)S(1)}, bf16[128,256]{1,0:T(8,128)(2,1)S(1)}, u32[]{:S(2)}, u32[]{:S(2)}) collective-permute-start(bf16[128,256]{1,0:T(8,128)(2,1)S(1)} %get-tuple-element.49), channel_id=1, source_target_pairs={{0,112},{16,0},{32,16},{48,32},{64,48},{80,64},{96,80},{112,96},{1... | collective-permute-start | bytes 196616 | tf_op jit(solution)/shard_map/ppermute | solution.py:239
  51.5 1.9 %collective-permute-done.6.before = bf16[128,256]{1,0:T(8,128)(2,1)S(1)} collective-permute-done((bf16[128,256]{1,0:T(8,128)(2,1)S(1)}, bf16[128,256]{1,0:T(8,128)(2,1)S(1)}, u32[]{:S(2)}, u32[]{:S(2)}) %collective-permute-start.6) | collective-permute-done | bytes 65568 | tf_op jit(solution)/shard_map/ppermute | solution.py:239
  53.5 4.4 %collective-permute-start.8 = (bf16[128,256]{1,0:T(8,128)(2,1)S(1)}, bf16[128,256]{1,0:T(8,128)(2,1)S(1)}, u32[]{:S(2)}, u32[]{:S(2)}) collective-permute-start(bf16[128,256]{1,0:T(8,128)(2,1)S(1)} %get-tuple-element.51), channel_id=1, source_target_pairs={{0,48},{16,64},{32,80},{48,96},{64,112},{80,0},{96,16},{112,32},{1... | collective-permute-start | bytes 196616 | tf_op jit(solution)/shard_map/ppermute | solution.py:239
  58.1 1.7 %collective-permute-done.8.before = bf16[128,256]{1,0:T(8,128)(2,1)S(1)} collective-permute-done((bf16[128,256]{1,0:T(8,128)(2,1)S(1)}, bf16[128,256]{1,0:T(8,128)(2,1)S(1)}, u32[]{:S(2)}, u32[]{:S(2)}) %collective-permute-start.8) | collective-permute-done | bytes 65568 | tf_op jit(solution)/shard_map/ppermute | solution.py:239
  59.8 3.1 %collective-permute-done.9.after = bf16[128,256]{1,0:T(8,128)(2,1)S(1)} collective-permute-done((bf16[128,256]{1,0:T(8,128)(2,1)S(1)}, bf16[128,256]{1,0:T(8,128)(2,1)S(1)}, u32[]{:S(2)}, u32[]{:S(2)}) %collective-permute-start.9) | collective-permute-done | bytes 65568 | tf_op jit(solution)/shard_map/ppermute | solution.py:239
  63.8 18.3 %all_to_all.26.u = bf16[16,136,256]{2,1,0:T(8,128)(2,1)S(1)} all-to-all(bf16[16,136,256]{2,1,0:T(8,128)(2,1)S(1)} %update.2), channel_id=1, replica_groups=mesh['yh'=2,'z'=8,'c'=2,'x'=4,'yl'=2] {'x','yl','yh'}, dimensions={0} | all-to-all | bytes 2228224 | tf_op jit(solution)/shard_map/all_to_all | solution.py:272
  82.1 3.4 %main.4 = (f32[256,256]{1,0:T(8,128)S(1)}, f32[256,256]{1,0:T(8,128)S(1)}, f32[8,128]{1,0:T(8,128)S(1)}) custom-call(s32[3]{0:T(128)S(1)} %pad_add_fusion.s, f32[4]{0:T(128)S(1)} %copy-done.2, bf16[4,256,2048]{2,1,0:T(8,128)(2,1)S(1)} %get-tuple-element.40.v1, bf16[4,256,2048]{2,1,0:T(8,128)(2,1)S(1)} %load.1.v2, bf16[4,512,512]{2,1,0:T(8,128)(2,1)S(1)} %copy-done.1, ...), custom_call_target="tpu_custom_call" | custom-call | flops 2684354560 | bytes 14225436 | tf_op jit(solution)/shard_map/main/pallas_call | solution.py:31
  85.5 4.9 %collective-permute-start.11 = (f32[256,256]{1,0:T(8,128)S(1)}, f32[256,256]{1,0:T(8,128)S(1)}, u32[]{:S(2)}, u32[]{:S(2)}) collective-permute-start(f32[256,256]{1,0:T(8,128)S(1)} %get-tuple-element.57), channel_id=1, source_target_pairs={{0,8},{8,0},{1,9},{9,1},{2,10},{10,2},{3,11},{11,3},{4,12},{12,4},... | collective-permute-start | bytes 786440 | tf_op jit(solution)/shard_map/ppermute | solution.py:234
  93.2 3.9 %collective-permute-done.13.recv = bf16[128,256]{1,0:T(8,128)(2,1)S(1)} collective-permute-done((bf16[128,256]{1,0:T(8,128)(2,1)S(1)}, bf16[128,256]{1,0:T(8,128)(2,1)S(1)}, u32[]{:S(2)}, u32[]{:S(2)}) %collective-permute-start.13) | collective-permute-done | bytes 65568 | tf_op jit(solution)/shard_map/ppermute | solution.py:234
  97.2 2.6 %collective-permute-start.14 = (bf16[128,256]{1,0:T(8,128)(2,1)S(1)}, bf16[128,256]{1,0:T(8,128)(2,1)S(1)}, u32[]{:S(2)}, u32[]{:S(2)}) collective-permute-start(bf16[128,256]{1,0:T(8,128)(2,1)S(1)} %get-tuple-element.62), channel_id=1, source_target_pairs={{0,16},{16,32},{32,48},{48,64},{64,80},{80,96},{96,112},{112,0},{1... | collective-permute-start | bytes 196616 | tf_op jit(solution)/shard_map/ppermute | solution.py:239
  100.0 1.6 collective-permute-done.14.before
  101.6 1.3 collective-permute-done.15.after
  102.9 2.1 %collective-permute-start.16 = (bf16[128,256]{1,0:T(8,128)(2,1)S(1)}, bf16[128,256]{1,0:T(8,128)(2,1)S(1)}, u32[]{:S(2)}, u32[]{:S(2)}) collective-permute-start(bf16[128,256]{1,0:T(8,128)(2,1)S(1)} %get-tuple-element.64), channel_id=1, source_target_pairs={{0,48},{16,64},{32,80},{48,96},{64,112},{80,0},{96,16},{112,32},{1... | collective-permute-start | bytes 196616 | tf_op jit(solution)/shard_map/ppermute | solution.py:239
  105.0 2.5 %collective-permute-start.17 = (bf16[128,256]{1,0:T(8,128)(2,1)S(1)}, bf16[128,256]{1,0:T(8,128)(2,1)S(1)}, u32[]{:S(2)}, u32[]{:S(2)}) collective-permute-start(bf16[128,256]{1,0:T(8,128)(2,1)S(1)} %get-tuple-element.65), channel_id=1, source_target_pairs={{0,80},{16,96},{32,112},{48,0},{64,16},{80,32},{96,48},{112,64},{1... | collective-permute-start | bytes 196616 | tf_op jit(solution)/shard_map/ppermute | solution.py:239
  107.5 3.1 %collective-permute-done.16.before = bf16[128,256]{1,0:T(8,128)(2,1)S(1)} collective-permute-done((bf16[128,256]{1,0:T(8,128)(2,1)S(1)}, bf16[128,256]{1,0:T(8,128)(2,1)S(1)}, u32[]{:S(2)}, u32[]{:S(2)}) %collective-permute-start.16) | collective-permute-done | bytes 65568 | tf_op jit(solution)/shard_map/ppermute | solution.py:239
  111.7 15.7 %all_to_all.27.u = bf16[16,136,256]{2,1,0:T(8,128)(2,1)S(1)} all-to-all(bf16[16,136,256]{2,1,0:T(8,128)(2,1)S(1)} %update.3), channel_id=1, replica_groups=mesh['yh'=2,'z'=8,'c'=2,'x'=4,'yl'=2] {'x','yl','yh'}, dimensions={0} | all-to-all | bytes 2228224 | tf_op jit(solution)/shard_map/all_to_all | solution.py:272
  127.4 3.4 %main.5 = (f32[256,256]{1,0:T(8,128)S(1)}, f32[256,256]{1,0:T(8,128)S(1)}, f32[8,128]{1,0:T(8,128)S(1)}) custom-call(s32[3]{0:T(128)S(1)} %pad_add_fusion.s, f32[4]{0:T(128)S(1)} %copy-done.2, bf16[4,256,2048]{2,1,0:T(8,128)(2,1)S(1)} %get-tuple-element.40.v1, bf16[4,256,2048]{2,1,0:T(8,128)(2,1)S(1)} %load.1.v2, bf16[4,512,512]{2,1,0:T(8,128)(2,1)S(1)} %copy-done.1, ...), custom_call_target="tpu_custom_call" | custom-call | flops 2684354560 | bytes 14225436 | tf_op jit(solution)/shard_map/main/pallas_call | solution.py:31
  130.8 6.3 %collective-permute-start.18 = (f32[256,256]{1,0:T(8,128)S(1)}, f32[256,256]{1,0:T(8,128)S(1)}, u32[]{:S(2)}, u32[]{:S(2)}) collective-permute-start(f32[256,256]{1,0:T(8,128)S(1)} %get-tuple-element.67), channel_id=1, source_target_pairs={{0,8},{8,0},{1,9},{9,1},{2,10},{10,2},{3,11},{11,3},{4,12},{12,4},... | collective-permute-start | bytes 786440 | tf_op jit(solution)/shard_map/ppermute | solution.py:234
  137.2 1.1 collective-permute-done.19.partsw
  139.1 14.2 %all_to_all.28.pieces = bf16[16,16,256]{2,1,0:T(8,128)(2,1)S(1)} all-to-all(bf16[16,16,256]{2,1,0:T(8,128)(2,1)S(1)} %pieces.1), channel_id=1, replica_groups=mesh['yh'=2,'z'=8,'c'=2,'x'=4,'yl'=2] {'yh','z'}, dimensions={0} | all-to-all | bytes 262144 | tf_op jit(solution)/shard_map/all_to_all | solution.py:331
  153.9 13.2 %all_to_all.29 = f32[16,16,256]{2,1,0:T(8,128)S(1)} all-to-all(f32[16,16,256]{2,1,0:T(8,128)S(1)} %last.1), channel_id=1, replica_groups=mesh['yh'=2,'z'=8,'c'=2,'x'=4,'yl'=2] {'yh','z'}, dimensions={0} | all-to-all | bytes 524288 | tf_op jit(solution)/shard_map/all_to_all | solution.py:333
  167.1 3.0 %collective-permute-start.20 = (f32[256,256]{1,0:T(8,128)S(1)}, f32[256,256]{1,0:T(8,128)S(1)}, u32[]{:S(2)}, u32[]{:S(2)}) collective-permute-start(f32[256,256]{1,0:T(8,128)S(1)} %bitcast.6), channel_id=1, source_target_pairs={{0,8},{8,0},{1,9},{9,1},{2,10},{10,2},{3,11},{11,3},{4,12},{12,4},... | collective-permute-start | bytes 786440 | tf_op jit(solution)/shard_map/ppermute | solution.py:234
  170.1 1.2 collective-permute-done.20.wc
  171.3 1.4 join.1
  (39 shorter events, 11.3 us)
Async XLA Ops:
  0.0 30.7 %collective-permute-start = (bf16[4,256,2048]{2,1,0:T(8,128)(2,1)}, bf16[4,256,2048]{2,1,0:T(8,128)(2,1)}, u32[]{:S(2)}, u32[]{:S(2)}) collective-permute-start(bf16[4,256,2048]{2,1,0:T(8,128)(2,1)} %v_h.1), channel_id=1, source_target_pairs={{0,8},{8,0},{1,9},{9,1},{2,10},{10,2},{3,11},{11,3},{4,12},{12,4},... | collective-permute-start | bytes 12582920 | tf_op jit(solution)/shard_map/ppermute | solution.py:234
  3.2 30.4 %collective-permute-start.1 = (bf16[4,512,512]{2,1,0:T(8,128)(2,1)}, bf16[4,512,512]{2,1,0:T(8,128)(2,1)S(1)}, u32[]{:S(2)}, u32[]{:S(2)}) collective-permute-start(bf16[4,512,512]{2,1,0:T(8,128)(2,1)} %o1.5), channel_id=1, source_target_pairs={{0,8},{8,0},{1,9},{9,1},{2,10},{10,2},{3,11},{11,3},{4,12},{12,4},... | collective-permute-start | bytes 6291464 | tf_op jit(solution)/shard_map/ppermute | solution.py:234
  6.6 22.2 %copy-start = (bf16[4,256,512]{2,1,0:T(8,128)(2,1)S(1)}, bf16[4,256,512]{2,1,0:T(8,128)(2,1)}, u32[]{:S(2)}) copy-start(bf16[4,256,512]{2,1,0:T(8,128)(2,1)} %ov.5) | copy-start | bytes 3145732
  28.8 8.9 %collective-permute-start.4 = (bf16[4,256,512]{2,1,0:T(8,128)(2,1)S(1)}, bf16[4,256,512]{2,1,0:T(8,128)(2,1)S(1)}, u32[]{:S(2)}, u32[]{:S(2)}) collective-permute-start(bf16[4,256,512]{2,1,0:T(8,128)(2,1)S(1)} %copy-done), channel_id=1, source_target_pairs={{0,8},{8,0},{1,9},{9,1},{2,10},{10,2},{3,11},{11,3},{4,12},{12,4},... | collective-permute-start | bytes 3145736 | tf_op jit(solution)/shard_map/ppermute | solution.py:234
  30.7 2.9 %copy-start.1 = (bf16[4,512,512]{2,1,0:T(8,128)(2,1)S(1)}, bf16[4,512,512]{2,1,0:T(8,128)(2,1)}, u32[]{:S(2)}) copy-start(bf16[4,512,512]{2,1,0:T(8,128)(2,1)} %o1.5) | copy-start | bytes 6291460
  30.7 2.9 %copy-start.2 = (f32[4]{0:T(128)S(1)}, f32[4]{0:T(128)}, u32[]{:S(2)}) copy-start(f32[4]{0:T(128)} %fit.2) | copy-start | bytes 52
  37.1 1.6 collective-permute-start.2
  37.2 1.5 collective-permute-start.3
  39.5 5.1 %collective-permute-start.5 = (bf16[128,256]{1,0:T(8,128)(2,1)S(1)}, bf16[128,256]{1,0:T(8,128)(2,1)S(1)}, u32[]{:S(2)}, u32[]{:S(2)}) collective-permute-start(bf16[128,256]{1,0:T(8,128)(2,1)S(1)} %get-tuple-element.47), channel_id=1, source_target_pairs={{0,128},{128,0},{1,129},{129,1},{2,130},{130,2},{3,131},{131,3},{4... | collective-permute-start | bytes 196616 | tf_op jit(solution)/shard_map/ppermute | solution.py:234
  45.2 17.7 %collective-permute-start.10 = (bf16[8,128,256]{2,1,0:T(8,128)(2,1)S(1)}, bf16[8,128,256]{2,1,0:T(8,128)(2,1)S(1)}, u32[]{:S(2)}, u32[]{:S(2)}) collective-permute-start(bf16[8,128,256]{2,1,0:T(8,128)(2,1)S(1)} %get-tuple-element.55), channel_id=1, source_target_pairs={{0,128},{128,0},{1,129},{129,1},{2,130},{130,2},{3,131},{131,3},{4... | collective-permute-start | bytes 1572872 | tf_op jit(solution)/shard_map/ppermute | solution.py:234
  46.0 7.5 %collective-permute-start.6 = (bf16[128,256]{1,0:T(8,128)(2,1)S(1)}, bf16[128,256]{1,0:T(8,128)(2,1)S(1)}, u32[]{:S(2)}, u32[]{:S(2)}) collective-permute-start(bf16[128,256]{1,0:T(8,128)(2,1)S(1)} %get-tuple-element.49), channel_id=1, source_target_pairs={{0,16},{16,32},{32,48},{48,64},{64,80},{80,96},{96,112},{112,0},{1... | collective-permute-start | bytes 196616 | tf_op jit(solution)/shard_map/ppermute | solution.py:239
  47.6 5.9 %collective-permute-start.7 = (bf16[128,256]{1,0:T(8,128)(2,1)S(1)}, bf16[128,256]{1,0:T(8,128)(2,1)S(1)}, u32[]{:S(2)}, u32[]{:S(2)}) collective-permute-start(bf16[128,256]{1,0:T(8,128)(2,1)S(1)} %get-tuple-element.49), channel_id=1, source_target_pairs={{0,112},{16,0},{32,16},{48,32},{64,48},{80,64},{96,80},{112,96},{1... | collective-permute-start | bytes 196616 | tf_op jit(solution)/shard_map/ppermute | solution.py:239
  53.5 6.3 %collective-permute-start.8 = (bf16[128,256]{1,0:T(8,128)(2,1)S(1)}, bf16[128,256]{1,0:T(8,128)(2,1)S(1)}, u32[]{:S(2)}, u32[]{:S(2)}) collective-permute-start(bf16[128,256]{1,0:T(8,128)(2,1)S(1)} %get-tuple-element.51), channel_id=1, source_target_pairs={{0,48},{16,64},{32,80},{48,96},{64,112},{80,0},{96,16},{112,32},{1... | collective-permute-start | bytes 196616 | tf_op jit(solution)/shard_map/ppermute | solution.py:239
  57.9 5.0 %collective-permute-start.9 = (bf16[128,256]{1,0:T(8,128)(2,1)S(1)}, bf16[128,256]{1,0:T(8,128)(2,1)S(1)}, u32[]{:S(2)}, u32[]{:S(2)}) collective-permute-start(bf16[128,256]{1,0:T(8,128)(2,1)S(1)} %get-tuple-element.52), channel_id=1, source_target_pairs={{0,80},{16,96},{32,112},{48,0},{64,16},{80,32},{96,48},{112,64},{1... | collective-permute-start | bytes 196616 | tf_op jit(solution)/shard_map/ppermute | solution.py:239
  85.5 6.1 %collective-permute-start.11 = (f32[256,256]{1,0:T(8,128)S(1)}, f32[256,256]{1,0:T(8,128)S(1)}, u32[]{:S(2)}, u32[]{:S(2)}) collective-permute-start(f32[256,256]{1,0:T(8,128)S(1)} %get-tuple-element.57), channel_id=1, source_target_pairs={{0,8},{8,0},{1,9},{9,1},{2,10},{10,2},{3,11},{11,3},{4,12},{12,4},... | collective-permute-start | bytes 786440 | tf_op jit(solution)/shard_map/ppermute | solution.py:234
  90.5 1.2 collective-permute-start.12
  92.5 4.7 %collective-permute-start.13 = (bf16[128,256]{1,0:T(8,128)(2,1)S(1)}, bf16[128,256]{1,0:T(8,128)(2,1)S(1)}, u32[]{:S(2)}, u32[]{:S(2)}) collective-permute-start(bf16[128,256]{1,0:T(8,128)(2,1)S(1)} %get-tuple-element.60), channel_id=1, source_target_pairs={{0,128},{128,0},{1,129},{129,1},{2,130},{130,2},{3,131},{131,3},{4... | collective-permute-start | bytes 196616 | tf_op jit(solution)/shard_map/ppermute | solution.py:234
  97.2 4.4 %collective-permute-start.14 = (bf16[128,256]{1,0:T(8,128)(2,1)S(1)}, bf16[128,256]{1,0:T(8,128)(2,1)S(1)}, u32[]{:S(2)}, u32[]{:S(2)}) collective-permute-start(bf16[128,256]{1,0:T(8,128)(2,1)S(1)} %get-tuple-element.62), channel_id=1, source_target_pairs={{0,16},{16,32},{32,48},{48,64},{64,80},{80,96},{96,112},{112,0},{1... | collective-permute-start | bytes 196616 | tf_op jit(solution)/shard_map/ppermute | solution.py:239
  99.8 3.1 %collective-permute-start.15 = (bf16[128,256]{1,0:T(8,128)(2,1)S(1)}, bf16[128,256]{1,0:T(8,128)(2,1)S(1)}, u32[]{:S(2)}, u32[]{:S(2)}) collective-permute-start(bf16[128,256]{1,0:T(8,128)(2,1)S(1)} %get-tuple-element.62), channel_id=1, source_target_pairs={{0,112},{16,0},{32,16},{48,32},{64,48},{80,64},{96,80},{112,96},{1... | collective-permute-start | bytes 196616 | tf_op jit(solution)/shard_map/ppermute | solution.py:239
  102.9 7.7 %collective-permute-start.16 = (bf16[128,256]{1,0:T(8,128)(2,1)S(1)}, bf16[128,256]{1,0:T(8,128)(2,1)S(1)}, u32[]{:S(2)}, u32[]{:S(2)}) collective-permute-start(bf16[128,256]{1,0:T(8,128)(2,1)S(1)} %get-tuple-element.64), channel_id=1, source_target_pairs={{0,48},{16,64},{32,80},{48,96},{64,112},{80,0},{96,16},{112,32},{1... | collective-permute-start | bytes 196616 | tf_op jit(solution)/shard_map/ppermute | solution.py:239
  105.0 5.8 %collective-permute-start.17 = (bf16[128,256]{1,0:T(8,128)(2,1)S(1)}, bf16[128,256]{1,0:T(8,128)(2,1)S(1)}, u32[]{:S(2)}, u32[]{:S(2)}) collective-permute-start(bf16[128,256]{1,0:T(8,128)(2,1)S(1)} %get-tuple-element.65), channel_id=1, source_target_pairs={{0,80},{16,96},{32,112},{48,0},{64,16},{80,32},{96,48},{112,64},{1... | collective-permute-start | bytes 196616 | tf_op jit(solution)/shard_map/ppermute | solution.py:239
  130.8 7.4 %collective-permute-start.18 = (f32[256,256]{1,0:T(8,128)S(1)}, f32[256,256]{1,0:T(8,128)S(1)}, u32[]{:S(2)}, u32[]{:S(2)}) collective-permute-start(f32[256,256]{1,0:T(8,128)S(1)} %get-tuple-element.67), channel_id=1, source_target_pairs={{0,8},{8,0},{1,9},{9,1},{2,10},{10,2},{3,11},{11,3},{4,12},{12,4},... | collective-permute-start | bytes 786440 | tf_op jit(solution)/shard_map/ppermute | solution.py:234
  137.1 1.2 collective-permute-start.19
  167.1 4.2 %collective-permute-start.20 = (f32[256,256]{1,0:T(8,128)S(1)}, f32[256,256]{1,0:T(8,128)S(1)}, u32[]{:S(2)}, u32[]{:S(2)}) collective-permute-start(f32[256,256]{1,0:T(8,128)S(1)} %bitcast.6), channel_id=1, source_target_pairs={{0,8},{8,0},{1,9},{9,1},{2,10},{10,2},{3,11},{11,3},{4,12},{12,4},... | collective-permute-start | bytes 786440 | tf_op jit(solution)/shard_map/ppermute | solution.py:234

commit v7 on v6

--- a/solution.py
+++ b/solution.py
@@ -7,6 +7,7 @@
 from jax.experimental.pallas import tpu as pltpu
 from jax.sharding import Mesh
 from jax.sharding import PartitionSpec as P
+
 
 V = 2048
 O = 512
@@ -25,7 +26,7 @@
     return jax.ShapeDtypeStruct(shape, dtype)
 
 
-def kernel(body, name, outputs, scratch=(), limit=8, flops=0, scalars=1, far=(), out=()):
+def kernel(body, outputs, scratch=(), limit=8, flops=0, scalars=1, far=(), out=()):
     def call(*args):
         moved = sum(math.prod(a.shape) * jnp.dtype(a.dtype).itemsize for a in (*args, *outputs))
         return pl.pallas_call(
@@ -50,7 +51,6 @@
             cost_estimate=pl.CostEstimate(
                 flops=flops, bytes_accessed=moved, transcendentals=0
             ),
-            name=name,
         )(*args)
 
     return call
@@ -142,7 +142,9 @@
     g = gs[:, at(yh, 128)]
     g = g + pltpu.roll(g, 1, 1)
     own = [jnp.full((1, 128), SCALE * fit[q], F32) for q in range(4)]
-    part[...] = jnp.concatenate([*own, jnp.zeros((4, 128), F32)], axis=0) - 4.0 * g
+    w = jnp.concatenate([*own, jnp.zeros((4, 128), F32)], axis=0) - 4.0 * g
+    part[...] = w
+    send[256:, :] = jnp.concatenate([w, w], axis=1)
     for k, v in enumerate((v1, v2)):
         z = jnp.dot(
             v[...].reshape(4 * 256, V), full[...], preferred_element_type=F32
@@ -152,24 +154,25 @@
     o = jnp.concatenate([r[q, at(c, 256), :] for r in (o1, o2) for q in range(4)], axis=0)
     ac[...] = jnp.dot(zs[...], o, preferred_element_type=F32)
     keep[...] = ac[:, at(c, COLS)]
-    send[...] = ac[:, at(1 - c, COLS)]
-
-
-def chip_total(s, keep, got, part, partsw, ov, ov2, tot):
+    send[:256, :] = ac[:, at(1 - c, COLS)]
+
+
+def chip_total(s, keep, got, part, ov, ov2, tot):
     c = s[0]
-    w = part[...] + jnp.concatenate([partsw[4:8, :], partsw[0:4, :]], axis=0)
+    other = got[256:, :128]
+    w = part[...] + jnp.concatenate([other[4:8, :], other[0:4, :]], axis=0)
     for h in range(2):
         lanes = slice(h * 128, (h + 1) * 128)
-        acc = keep[:, lanes] + got[:, lanes]
+        acc = keep[:, lanes] + got[:256, lanes]
         for q in range(8):
             ref = (ov, ov2)[q // 4]
             acc += ref[q % 4, :, at(c * 2 + h, 128)].astype(F32) * w[q : q + 1, :]
         tot[:, lanes] = acc
 
 
-def pair_body(s, keep, got, part, partsw, ov, ov2, mine, other, tot):
+def pair_body(s, keep, got, part, ov, ov2, mine, other, tot):
     yh = s[1]
-    chip_total(s, keep, got, part, partsw, ov, ov2, tot)
+    chip_total(s, keep, got, part, ov, ov2, tot)
     mine[...] = tot[at(yh, ROWS), :]
     other[...] = tot[at(1 - yh, ROWS), :].astype(BF)
 
@@ -180,9 +183,9 @@
     out[...] = t.astype(BF)
 
 
-def first_rows_body(s, mine, recv, ov, ov2, total, out, ovs):
+def first_pair_body(s, keep, got, part, ov, ov2, mine, other, ovs, tot):
     c, yh = s[0], s[1]
-    rows_body(mine, recv, total, out)
+    pair_body(s, keep, got, part, ov, ov2, mine, other, tot)
     for q in range(8):
         ovs[q] = (ov, ov2)[q // 4][q % 4, at(1 - yh, ROWS), at(c, COLS)]
 
@@ -195,8 +198,8 @@
     two_half[...] = two.astype(BF)
 
 
-def pieces_body(s, keep, got, part, partsw, ov, ov2, out, tot):
-    chip_total(s, keep, got, part, partsw, ov, ov2, tot)
+def pieces_body(s, keep, got, part, ov, ov2, out, tot):
+    chip_total(s, keep, got, part, ov, ov2, tot)
     for p in range(16):
         out[p] = tot[p * 16 : (p + 1) * 16, :].astype(BF)
 
@@ -246,7 +249,6 @@
     message = sds(16, PIECE, COLS, dtype=BF)
     msg, rq, dq, v1 = kernel(
         start_body,
-        "start",
         [message, tile, tile, pltpu.VMEM((4, 256, V), BF)],
         [
             pltpu.VMEM((256, O), F32),
@@ -274,11 +276,7 @@
             msg, b_ov, fit_pert, s = lax.optimization_barrier((msg, b_ov, fit_pert, s))
             ov2 = swap(b_ov, "c")
             (v2,) = kernel(
-                load_body,
-                "load",
-                [pltpu.VMEM((4, 256, V), BF)],
-                [pltpu.SemaphoreType.DMA((4,))],
-                far=(1,),
+                load_body, [pltpu.VMEM((4, 256, V), BF)], [pltpu.SemaphoreType.DMA((4,))], far=(1,)
             )(
                 s,
                 pltpu.with_memory_space_constraint(vv2, pltpu.HBM),
@@ -286,8 +284,7 @@
             )
         keep, send, part = kernel(
             main_body,
-            "main",
-            [sds(256, COLS), sds(256, COLS), sds(8, 128)],
+            [sds(256, COLS), sds(256 + 8, COLS), sds(8, 128)],
             [
                 pltpu.VMEM((V, COLS), BF),
                 pltpu.VMEM((256, V), BF),
@@ -298,25 +295,24 @@
             flops=2 * 8 * 256 * 256 * (V + O),
             scalars=2,
         )(s, fit_pert, v1, v2, b_oo, oo2, msg)
-        chip = (s, keep, swap(send, "c"), part, swap(part, "c"), b_ov, ov2)
+        chip = (s, keep, swap(send, "c"), part, b_ov, ov2)
         sums = [pltpu.VMEM((256, COLS), F32)]
         if step == ITERS - 1:
             break
-        mine, other = kernel(pair_body, "pair", [tile, half], sums)(*chip)
-        recv = swap(other, "yh")
         if oth is None:
-            total, out, ovs = kernel(
-                first_rows_body,
-                "first_rows",
-                [tile, half, sds(8, ROWS, COLS, dtype=BF)],
-            )(s, mine, recv, b_ov, ov2)
+            mine, other, ovs = kernel(
+                first_pair_body, [tile, half, sds(8, ROWS, COLS, dtype=BF)], sums
+            )(*chip)
+            recv = swap(other, "yh")
             oth = swap(ovs, "yh")
         else:
-            total, out = kernel(rows_body, "rows", [tile, half], scalars=0)(mine, recv)
+            mine, other = kernel(pair_body, [tile, half], sums)(*chip)
+            recv = swap(other, "yh")
+        total, out = kernel(rows_body, [tile, half], scalars=0)(mine, recv)
         three, three_half, two_half = kernel(
-            near_body, "near", [tile, half, half], scalars=0
+            near_body, [tile, half, half], scalars=0
         )(total, along_z(out, 1), along_z(out, -1))
-        (msg,) = kernel(update_body, "update", [message])(
+        (msg,) = kernel(update_body, [message])(
             s,
             three,
             along_z(two_half, 3),
@@ -327,11 +323,11 @@
             ov2,
             oth,
         )
-    (pieces,) = kernel(pieces_body, "pieces", [sds(16, 16, COLS, dtype=BF)], sums)(*chip)
+    (pieces,) = kernel(pieces_body, [sds(16, 16, COLS, dtype=BF)], sums)(*chip)
     pieces = lax.all_to_all(pieces, ("yh", "z"), 0, 0, tiled=True)
-    (pieces,) = kernel(last_body, "last", [sds(16, 16, COLS)])(s, pieces, rq, dq)
+    (pieces,) = kernel(last_body, [sds(16, 16, COLS)])(s, pieces, rq, dq)
     w = lax.all_to_all(pieces, ("yh", "z"), 0, 0, tiled=True).reshape(256, COLS)
-    return kernel(join_body, "join", [sds(256, O)])(s, w, swap(w, "c"))[0]
+    return kernel(join_body, [sds(256, O)])(s, w, swap(w, "c"))[0]
 
 
 def solution(mesh):

time: 173 us -> 182 us (1.052)
  waiting for transfers between devices: 25.7 us -> 34.8 us
    ppermute x13 -> x10, waiting for transfers between devices: 12.7 us -> 22.3 us  [swap(): return lax.ppermute(value, axis, [(0, 1), (1, 0)])]
    ppermute x13 -> x10, starting transfers between devices: 22.4 us -> 23.1 us  [swap(): return lax.ppermute(value, axis, [(0, 1), (1, 0)])]
  transfers between devices with their start and end apart: 21 -> 18, of which waited for: 13 -> 12; matrix products, arithmetic and copies ran while one was open for 0% -> 0% of each run, Pallas kernels for 6% -> 5%
where the time goes in v7:
time: 182 us; the launch traced here: 181 us
  blocking collectives  82.7 us (45%)
  starting transfers between devices  40.7 us (22%)
  waiting for transfers between devices  34.8 us (19%)
  Pallas kernels  22.8 us (13%)
    all_to_all x3, blocking collectives, local(): msg = lax.all_to_all(msg, PLANE, 0, 0, tiled=True)  55.1 us
    ppermute x10, starting transfers between devices, swap(): return lax.ppermute(value, axis, [(0, 1), (1, 0)])  23.1 us
    pallas_call x16, Pallas kernels, call(): pl.pallas_call(body, out_shape=list(outputs), in_specs=[pl.BlockSpec(memo...  22.8 us
    ppermute x10, waiting for transfers between devices, swap(): return lax.ppermute(value, axis, [(0, 1), (1, 0)])  22.3 us
    ppermute x8, starting transfers between devices, along_z(): return lax.ppermute(value, 'z', [(i, (i + shift) % n) for i in range(n)])  17.6 us
    all_to_all x1, blocking collectives, local(): pieces = lax.all_to_all(pieces, ('yh', 'z'), 0, 0, tiled=True)  14.5 us
    all_to_all x1, blocking collectives, local(): w = lax.all_to_all(pieces, ('yh', 'z'), 0, 0, tiled=True).reshape(256, COLS)  13.2 us
    ppermute x8, waiting for transfers between devices, along_z(): return lax.ppermute(value, 'z', [(i, (i + shift) % n) for i in range(n)])  12.5 us
  transfers between devices with their start and end apart: 18, of which 12 were waited for; matrix products, arithmetic and copies ran while one was open for 0% of the time, Pallas kernels for 5%

profile of v7, /device:TPU:1, one launch (start us, length us, event | category | flops | bytes accessed | tf_op | source)
XLA Modules:
  0.0 181.3 jit_solution(10093527667379839154)
XLA Ops:
  0.0 3.2 %collective-permute-start = (bf16[4,256,2048]{2,1,0:T(8,128)(2,1)}, bf16[4,256,2048]{2,1,0:T(8,128)(2,1)}, u32[]{:S(2)}, u32[]{:S(2)}) collective-permute-start(bf16[4,256,2048]{2,1,0:T(8,128)(2,1)} %v_h.1), channel_id=1, source_target_pairs={{0,8},{8,0},{1,9},{9,1},{2,10},{10,2},{3,11},{11,3},{4,12},{12,4},... | collective-permute-start | bytes 12582920 | tf_op jit(solution)/shard_map/ppermute | solution.py:237
  3.3 3.3 %shard_map.73 = (bf16[16,136,256]{2,1,0:T(8,128)(2,1)S(1)}, f32[128,256]{1,0:T(8,128)S(1)}, f32[128,256]{1,0:T(8,128)S(1)}, bf16[4,256,2048]{2,1,0:T(8,128)(2,1)S(1)}) custom-call(s32[3]{0:T(128)S(1)} %pad_add_fusion.s, f32[256,512]{1,0:T(8,128)} %rhs_h.1, f32[1,256]{1,0:T(1,128)} %bitcast.9, f32[1,512]{1,0:T(1,128)} %bitcast.8, bf16[4,256,512]{2,1,0:T(8,128)(2,1)} %ov.4, ...), custom_call_target="tpu_custom_call" | custom-call | bytes 11340812 | tf_op jit(solution)/shard_map/pallas_call | solution.py:32
  6.6 22.2 %all_to_all.25.u = bf16[16,136,256]{2,1,0:T(8,128)(2,1)S(1)} all-to-all(bf16[16,136,256]{2,1,0:T(8,128)(2,1)S(1)} %get-tuple-element.37), channel_id=1, replica_groups=mesh['yh'=2,'z'=8,'c'=2,'x'=4,'yl'=2] {'x','yl','yh'}, dimensions={0} | all-to-all | bytes 2228224 | tf_op jit(solution)/shard_map/all_to_all | solution.py:274
  28.8 1.9 %collective-permute-start.3 = (bf16[4,256,512]{2,1,0:T(8,128)(2,1)S(1)}, bf16[4,256,512]{2,1,0:T(8,128)(2,1)S(1)}, u32[]{:S(2)}, u32[]{:S(2)}) collective-permute-start(bf16[4,256,512]{2,1,0:T(8,128)(2,1)S(1)} %copy-done), channel_id=1, source_target_pairs={{0,8},{8,0},{1,9},{9,1},{2,10},{10,2},{3,11},{11,3},{4,12},{12,4},... | collective-permute-start | bytes 3145736 | tf_op jit(solution)/shard_map/ppermute | solution.py:237
  30.7 2.8 %shard_map.74.v2 = bf16[4,256,2048]{2,1,0:T(8,128)(2,1)S(1)} custom-call(s32[3]{0:T(128)S(1)} %pad_add_fusion.s, bf16[4,256,2048]{2,1,0:T(8,128)(2,1)} %collective-permute-done.v_h, bf16[1,8,128]{2,1,0:T(8,128)(2,1)S(1)} %slice.3.after), custom_call_target="tpu_custom_call" | custom-call | bytes 8390668 | tf_op jit(solution)/shard_map/pallas_call | solution.py:32
  33.6 3.4 %shard_map.75 = (f32[256,256]{1,0:T(8,128)S(1)}, f32[264,256]{1,0:T(8,128)S(1)}, f32[8,128]{1,0:T(8,128)S(1)}) custom-call(s32[3]{0:T(128)S(1)} %pad_add_fusion.s, f32[4]{0:T(128)S(1)} %copy-done.2, bf16[4,256,2048]{2,1,0:T(8,128)(2,1)S(1)} %get-tuple-element.40.v1, bf16[4,256,2048]{2,1,0:T(8,128)(2,1)S(1)} %shard_map.74.v2, ...), custom_call_target="tpu_custom_call" | custom-call | flops 2684354560 | bytes 14233628 | tf_op jit(solution)/shard_map/pallas_call | solution.py:32
  37.2 1.5 collective-permute-done.2.got
  40.3 2.3 %collective-permute-start.4 = (bf16[128,256]{1,0:T(8,128)(2,1)S(1)}, bf16[128,256]{1,0:T(8,128)(2,1)S(1)}, u32[]{:S(2)}, u32[]{:S(2)}) collective-permute-start(bf16[128,256]{1,0:T(8,128)(2,1)S(1)} %get-tuple-element.47), channel_id=1, source_target_pairs={{0,128},{128,0},{1,129},{129,1},{2,130},{130,2},{3,131},{131,3},{4... | collective-permute-start | bytes 196616 | tf_op jit(solution)/shard_map/ppermute | solution.py:237
  42.6 13.3 %collective-permute-done.4.recv = bf16[128,256]{1,0:T(8,128)(2,1)S(1)} collective-permute-done((bf16[128,256]{1,0:T(8,128)(2,1)S(1)}, bf16[128,256]{1,0:T(8,128)(2,1)S(1)}, u32[]{:S(2)}, u32[]{:S(2)}) %collective-permute-start.4) | collective-permute-done | bytes 65568 | tf_op jit(solution)/shard_map/ppermute | solution.py:237
  55.9 1.7 collective-permute-start.5
  57.6 4.0 %collective-permute-start.6 = (bf16[128,256]{1,0:T(8,128)(2,1)S(1)}, bf16[128,256]{1,0:T(8,128)(2,1)S(1)}, u32[]{:S(2)}, u32[]{:S(2)}) collective-permute-start(bf16[128,256]{1,0:T(8,128)(2,1)S(1)} %get-tuple-element.49), channel_id=1, source_target_pairs={{0,112},{16,0},{32,16},{48,32},{64,48},{80,64},{96,80},{112,96},{1... | collective-permute-start | bytes 196616 | tf_op jit(solution)/shard_map/ppermute | solution.py:242
  61.7 1.6 collective-permute-done.5.before
  63.3 4.4 %collective-permute-start.7 = (bf16[128,256]{1,0:T(8,128)(2,1)S(1)}, bf16[128,256]{1,0:T(8,128)(2,1)S(1)}, u32[]{:S(2)}, u32[]{:S(2)}) collective-permute-start(bf16[128,256]{1,0:T(8,128)(2,1)S(1)} %get-tuple-element.51), channel_id=1, source_target_pairs={{0,48},{16,64},{32,80},{48,96},{64,112},{80,0},{96,16},{112,32},{1... | collective-permute-start | bytes 196616 | tf_op jit(solution)/shard_map/ppermute | solution.py:242
  67.8 1.8 collective-permute-done.7.before
  69.6 3.1 %collective-permute-done.8.after = bf16[128,256]{1,0:T(8,128)(2,1)S(1)} collective-permute-done((bf16[128,256]{1,0:T(8,128)(2,1)S(1)}, bf16[128,256]{1,0:T(8,128)(2,1)S(1)}, u32[]{:S(2)}, u32[]{:S(2)}) %collective-permute-start.8) | collective-permute-done | bytes 65568 | tf_op jit(solution)/shard_map/ppermute | solution.py:242
  73.6 16.9 %all_to_all.26.u = bf16[16,136,256]{2,1,0:T(8,128)(2,1)S(1)} all-to-all(bf16[16,136,256]{2,1,0:T(8,128)(2,1)S(1)} %shard_map.79), channel_id=1, replica_groups=mesh['yh'=2,'z'=8,'c'=2,'x'=4,'yl'=2] {'x','yl','yh'}, dimensions={0} | all-to-all | bytes 2228224 | tf_op jit(solution)/shard_map/all_to_all | solution.py:274
  90.5 3.4 %shard_map.80 = (f32[256,256]{1,0:T(8,128)S(1)}, f32[264,256]{1,0:T(8,128)S(1)}, f32[8,128]{1,0:T(8,128)S(1)}) custom-call(s32[3]{0:T(128)S(1)} %pad_add_fusion.s, f32[4]{0:T(128)S(1)} %copy-done.2, bf16[4,256,2048]{2,1,0:T(8,128)(2,1)S(1)} %get-tuple-element.40.v1, bf16[4,256,2048]{2,1,0:T(8,128)(2,1)S(1)} %shard_map.74.v2, ...), custom_call_target="tpu_custom_call" | custom-call | flops 2684354560 | bytes 14233628 | tf_op jit(solution)/shard_map/pallas_call | solution.py:32
  93.9 4.9 %collective-permute-start.10 = (f32[264,256]{1,0:T(8,128)S(1)}, f32[264,256]{1,0:T(8,128)S(1)}, u32[]{:S(2)}, u32[]{:S(2)}) collective-permute-start(f32[264,256]{1,0:T(8,128)S(1)} %get-tuple-element.57), channel_id=1, source_target_pairs={{0,8},{8,0},{1,9},{9,1},{2,10},{10,2},{3,11},{11,3},{4,12},{12,4},... | collective-permute-start | bytes 811016 | tf_op jit(solution)/shard_map/ppermute | solution.py:237
  101.6 3.9 %collective-permute-done.11.recv = bf16[128,256]{1,0:T(8,128)(2,1)S(1)} collective-permute-done((bf16[128,256]{1,0:T(8,128)(2,1)S(1)}, bf16[128,256]{1,0:T(8,128)(2,1)S(1)}, u32[]{:S(2)}, u32[]{:S(2)}) %collective-permute-start.11) | collective-permute-done | bytes 65568 | tf_op jit(solution)/shard_map/ppermute | solution.py:237
  105.6 2.6 %collective-permute-start.12 = (bf16[128,256]{1,0:T(8,128)(2,1)S(1)}, bf16[128,256]{1,0:T(8,128)(2,1)S(1)}, u32[]{:S(2)}, u32[]{:S(2)}) collective-permute-start(bf16[128,256]{1,0:T(8,128)(2,1)S(1)} %get-tuple-element.62), channel_id=1, source_target_pairs={{0,16},{16,32},{32,48},{48,64},{64,80},{80,96},{96,112},{112,0},{1... | collective-permute-start | bytes 196616 | tf_op jit(solution)/shard_map/ppermute | solution.py:242
  108.4 1.6 collective-permute-done.12.before
  110.0 1.6 collective-permute-done.13.after
  111.6 1.6 collective-permute-start.14
  113.2 3.0 %collective-permute-start.15 = (bf16[128,256]{1,0:T(8,128)(2,1)S(1)}, bf16[128,256]{1,0:T(8,128)(2,1)S(1)}, u32[]{:S(2)}, u32[]{:S(2)}) collective-permute-start(bf16[128,256]{1,0:T(8,128)(2,1)S(1)} %get-tuple-element.65), channel_id=1, source_target_pairs={{0,80},{16,96},{32,112},{48,0},{64,16},{80,32},{96,48},{112,64},{1... | collective-permute-start | bytes 196616 | tf_op jit(solution)/shard_map/ppermute | solution.py:242
  116.2 2.9 %collective-permute-done.14.before = bf16[128,256]{1,0:T(8,128)(2,1)S(1)} collective-permute-done((bf16[128,256]{1,0:T(8,128)(2,1)S(1)}, bf16[128,256]{1,0:T(8,128)(2,1)S(1)}, u32[]{:S(2)}, u32[]{:S(2)}) %collective-permute-start.14) | collective-permute-done | bytes 65568 | tf_op jit(solution)/shard_map/ppermute | solution.py:242
  120.0 16.0 %all_to_all.27.u = bf16[16,136,256]{2,1,0:T(8,128)(2,1)S(1)} all-to-all(bf16[16,136,256]{2,1,0:T(8,128)(2,1)S(1)} %shard_map.84), channel_id=1, replica_groups=mesh['yh'=2,'z'=8,'c'=2,'x'=4,'yl'=2] {'x','yl','yh'}, dimensions={0} | all-to-all | bytes 2228224 | tf_op jit(solution)/shard_map/all_to_all | solution.py:274
  136.0 3.4 %shard_map.85 = (f32[256,256]{1,0:T(8,128)S(1)}, f32[264,256]{1,0:T(8,128)S(1)}, f32[8,128]{1,0:T(8,128)S(1)}) custom-call(s32[3]{0:T(128)S(1)} %pad_add_fusion.s, f32[4]{0:T(128)S(1)} %copy-done.2, bf16[4,256,2048]{2,1,0:T(8,128)(2,1)S(1)} %get-tuple-element.40.v1, bf16[4,256,2048]{2,1,0:T(8,128)(2,1)S(1)} %shard_map.74.v2, ...), custom_call_target="tpu_custom_call" | custom-call | flops 2684354560 | bytes 14233628 | tf_op jit(solution)/shard_map/pallas_call | solution.py:32
  139.4 6.1 %collective-permute-start.16 = (f32[264,256]{1,0:T(8,128)S(1)}, f32[264,256]{1,0:T(8,128)S(1)}, u32[]{:S(2)}, u32[]{:S(2)}) collective-permute-start(f32[264,256]{1,0:T(8,128)S(1)} %get-tuple-element.67), channel_id=1, source_target_pairs={{0,8},{8,0},{1,9},{9,1},{2,10},{10,2},{3,11},{11,3},{4,12},{12,4},... | collective-permute-start | bytes 811016 | tf_op jit(solution)/shard_map/ppermute | solution.py:237
  147.4 14.5 %all_to_all.28.pieces = bf16[16,16,256]{2,1,0:T(8,128)(2,1)S(1)} all-to-all(bf16[16,16,256]{2,1,0:T(8,128)(2,1)S(1)} %shard_map.86), channel_id=1, replica_groups=mesh['yh'=2,'z'=8,'c'=2,'x'=4,'yl'=2] {'yh','z'}, dimensions={0} | all-to-all | bytes 262144 | tf_op jit(solution)/shard_map/all_to_all | solution.py:327
  162.5 13.2 %all_to_all.29 = f32[16,16,256]{2,1,0:T(8,128)S(1)} all-to-all(f32[16,16,256]{2,1,0:T(8,128)S(1)} %shard_map.87), channel_id=1, replica_groups=mesh['yh'=2,'z'=8,'c'=2,'x'=4,'yl'=2] {'yh','z'}, dimensions={0} | all-to-all | bytes 524288 | tf_op jit(solution)/shard_map/all_to_all | solution.py:329
  175.7 3.0 %collective-permute-start.17 = (f32[256,256]{1,0:T(8,128)S(1)}, f32[256,256]{1,0:T(8,128)S(1)}, u32[]{:S(2)}, u32[]{:S(2)}) collective-permute-start(f32[256,256]{1,0:T(8,128)S(1)} %bitcast.6), channel_id=1, source_target_pairs={{0,8},{8,0},{1,9},{9,1},{2,10},{10,2},{3,11},{11,3},{4,12},{12,4},... | collective-permute-start | bytes 786440 | tf_op jit(solution)/shard_map/ppermute | solution.py:237
  179.9 1.4 shard_map.88
  (33 shorter events, 10.5 us)
Async XLA Ops:
  0.0 30.7 %collective-permute-start = (bf16[4,256,2048]{2,1,0:T(8,128)(2,1)}, bf16[4,256,2048]{2,1,0:T(8,128)(2,1)}, u32[]{:S(2)}, u32[]{:S(2)}) collective-permute-start(bf16[4,256,2048]{2,1,0:T(8,128)(2,1)} %v_h.1), channel_id=1, source_target_pairs={{0,8},{8,0},{1,9},{9,1},{2,10},{10,2},{3,11},{11,3},{4,12},{12,4},... | collective-permute-start | bytes 12582920 | tf_op jit(solution)/shard_map/ppermute | solution.py:237
  3.2 30.4 %collective-permute-start.1 = (bf16[4,512,512]{2,1,0:T(8,128)(2,1)}, bf16[4,512,512]{2,1,0:T(8,128)(2,1)S(1)}, u32[]{:S(2)}, u32[]{:S(2)}) collective-permute-start(bf16[4,512,512]{2,1,0:T(8,128)(2,1)} %o1.5), channel_id=1, source_target_pairs={{0,8},{8,0},{1,9},{9,1},{2,10},{10,2},{3,11},{11,3},{4,12},{12,4},... | collective-permute-start | bytes 6291464 | tf_op jit(solution)/shard_map/ppermute | solution.py:237
  6.6 22.2 %copy-start = (bf16[4,256,512]{2,1,0:T(8,128)(2,1)S(1)}, bf16[4,256,512]{2,1,0:T(8,128)(2,1)}, u32[]{:S(2)}) copy-start(bf16[4,256,512]{2,1,0:T(8,128)(2,1)} %ov.4) | copy-start | bytes 3145732
  28.8 8.4 %collective-permute-start.3 = (bf16[4,256,512]{2,1,0:T(8,128)(2,1)S(1)}, bf16[4,256,512]{2,1,0:T(8,128)(2,1)S(1)}, u32[]{:S(2)}, u32[]{:S(2)}) collective-permute-start(bf16[4,256,512]{2,1,0:T(8,128)(2,1)S(1)} %copy-done), channel_id=1, source_target_pairs={{0,8},{8,0},{1,9},{9,1},{2,10},{10,2},{3,11},{11,3},{4,12},{12,4},... | collective-permute-start | bytes 3145736 | tf_op jit(solution)/shard_map/ppermute | solution.py:237
  30.7 2.9 %copy-start.1 = (bf16[4,512,512]{2,1,0:T(8,128)(2,1)S(1)}, bf16[4,512,512]{2,1,0:T(8,128)(2,1)}, u32[]{:S(2)}) copy-start(bf16[4,512,512]{2,1,0:T(8,128)(2,1)} %o1.5) | copy-start | bytes 6291460
  30.7 2.9 %copy-start.2 = (f32[4]{0:T(128)S(1)}, f32[4]{0:T(128)}, u32[]{:S(2)}) copy-start(f32[4]{0:T(128)} %fit.2) | copy-start | bytes 52
  37.1 1.6 collective-permute-start.2
  39.6 33.1 %collective-permute-start.9 = (bf16[8,128,256]{2,1,0:T(8,128)(2,1)S(1)}, bf16[8,128,256]{2,1,0:T(8,128)(2,1)S(1)}, u32[]{:S(2)}, u32[]{:S(2)}) collective-permute-start(bf16[8,128,256]{2,1,0:T(8,128)(2,1)S(1)} %get-tuple-element.55), channel_id=1, source_target_pairs={{0,128},{128,0},{1,129},{129,1},{2,130},{130,2},{3,131},{131,3},{4... | collective-permute-start | bytes 1572872 | tf_op jit(solution)/shard_map/ppermute | solution.py:237
  40.3 15.6 %collective-permute-start.4 = (bf16[128,256]{1,0:T(8,128)(2,1)S(1)}, bf16[128,256]{1,0:T(8,128)(2,1)S(1)}, u32[]{:S(2)}, u32[]{:S(2)}) collective-permute-start(bf16[128,256]{1,0:T(8,128)(2,1)S(1)} %get-tuple-element.47), channel_id=1, source_target_pairs={{0,128},{128,0},{1,129},{129,1},{2,130},{130,2},{3,131},{131,3},{4... | collective-permute-start | bytes 196616 | tf_op jit(solution)/shard_map/ppermute | solution.py:237
  55.9 7.3 %collective-permute-start.5 = (bf16[128,256]{1,0:T(8,128)(2,1)S(1)}, bf16[128,256]{1,0:T(8,128)(2,1)S(1)}, u32[]{:S(2)}, u32[]{:S(2)}) collective-permute-start(bf16[128,256]{1,0:T(8,128)(2,1)S(1)} %get-tuple-element.49), channel_id=1, source_target_pairs={{0,16},{16,32},{32,48},{48,64},{64,80},{80,96},{96,112},{112,0},{1... | collective-permute-start | bytes 196616 | tf_op jit(solution)/shard_map/ppermute | solution.py:242
  57.6 5.6 %collective-permute-start.6 = (bf16[128,256]{1,0:T(8,128)(2,1)S(1)}, bf16[128,256]{1,0:T(8,128)(2,1)S(1)}, u32[]{:S(2)}, u32[]{:S(2)}) collective-permute-start(bf16[128,256]{1,0:T(8,128)(2,1)S(1)} %get-tuple-element.49), channel_id=1, source_target_pairs={{0,112},{16,0},{32,16},{48,32},{64,48},{80,64},{96,80},{112,96},{1... | collective-permute-start | bytes 196616 | tf_op jit(solution)/shard_map/ppermute | solution.py:242
  63.3 6.3 %collective-permute-start.7 = (bf16[128,256]{1,0:T(8,128)(2,1)S(1)}, bf16[128,256]{1,0:T(8,128)(2,1)S(1)}, u32[]{:S(2)}, u32[]{:S(2)}) collective-permute-start(bf16[128,256]{1,0:T(8,128)(2,1)S(1)} %get-tuple-element.51), channel_id=1, source_target_pairs={{0,48},{16,64},{32,80},{48,96},{64,112},{80,0},{96,16},{112,32},{1... | collective-permute-start | bytes 196616 | tf_op jit(solution)/shard_map/ppermute | solution.py:242
  67.6 5.0 %collective-permute-start.8 = (bf16[128,256]{1,0:T(8,128)(2,1)S(1)}, bf16[128,256]{1,0:T(8,128)(2,1)S(1)}, u32[]{:S(2)}, u32[]{:S(2)}) collective-permute-start(bf16[128,256]{1,0:T(8,128)(2,1)S(1)} %get-tuple-element.52), channel_id=1, source_target_pairs={{0,80},{16,96},{32,112},{48,0},{64,16},{80,32},{96,48},{112,64},{1... | collective-permute-start | bytes 196616 | tf_op jit(solution)/shard_map/ppermute | solution.py:242
  93.9 6.1 %collective-permute-start.10 = (f32[264,256]{1,0:T(8,128)S(1)}, f32[264,256]{1,0:T(8,128)S(1)}, u32[]{:S(2)}, u32[]{:S(2)}) collective-permute-start(f32[264,256]{1,0:T(8,128)S(1)} %get-tuple-element.57), channel_id=1, source_target_pairs={{0,8},{8,0},{1,9},{9,1},{2,10},{10,2},{3,11},{11,3},{4,12},{12,4},... | collective-permute-start | bytes 811016 | tf_op jit(solution)/shard_map/ppermute | solution.py:237
  100.9 4.7 %collective-permute-start.11 = (bf16[128,256]{1,0:T(8,128)(2,1)S(1)}, bf16[128,256]{1,0:T(8,128)(2,1)S(1)}, u32[]{:S(2)}, u32[]{:S(2)}) collective-permute-start(bf16[128,256]{1,0:T(8,128)(2,1)S(1)} %get-tuple-element.60), channel_id=1, source_target_pairs={{0,128},{128,0},{1,129},{129,1},{2,130},{130,2},{3,131},{131,3},{4... | collective-permute-start | bytes 196616 | tf_op jit(solution)/shard_map/ppermute | solution.py:237
  105.6 4.4 %collective-permute-start.12 = (bf16[128,256]{1,0:T(8,128)(2,1)S(1)}, bf16[128,256]{1,0:T(8,128)(2,1)S(1)}, u32[]{:S(2)}, u32[]{:S(2)}) collective-permute-start(bf16[128,256]{1,0:T(8,128)(2,1)S(1)} %get-tuple-element.62), channel_id=1, source_target_pairs={{0,16},{16,32},{32,48},{48,64},{64,80},{80,96},{96,112},{112,0},{1... | collective-permute-start | bytes 196616 | tf_op jit(solution)/shard_map/ppermute | solution.py:242
  108.2 3.4 %collective-permute-start.13 = (bf16[128,256]{1,0:T(8,128)(2,1)S(1)}, bf16[128,256]{1,0:T(8,128)(2,1)S(1)}, u32[]{:S(2)}, u32[]{:S(2)}) collective-permute-start(bf16[128,256]{1,0:T(8,128)(2,1)S(1)} %get-tuple-element.62), channel_id=1, source_target_pairs={{0,112},{16,0},{32,16},{48,32},{64,48},{80,64},{96,80},{112,96},{1... | collective-permute-start | bytes 196616 | tf_op jit(solution)/shard_map/ppermute | solution.py:242
  111.6 7.4 %collective-permute-start.14 = (bf16[128,256]{1,0:T(8,128)(2,1)S(1)}, bf16[128,256]{1,0:T(8,128)(2,1)S(1)}, u32[]{:S(2)}, u32[]{:S(2)}) collective-permute-start(bf16[128,256]{1,0:T(8,128)(2,1)S(1)} %get-tuple-element.64), channel_id=1, source_target_pairs={{0,48},{16,64},{32,80},{48,96},{64,112},{80,0},{96,16},{112,32},{1... | collective-permute-start | bytes 196616 | tf_op jit(solution)/shard_map/ppermute | solution.py:242
  113.2 5.9 %collective-permute-start.15 = (bf16[128,256]{1,0:T(8,128)(2,1)S(1)}, bf16[128,256]{1,0:T(8,128)(2,1)S(1)}, u32[]{:S(2)}, u32[]{:S(2)}) collective-permute-start(bf16[128,256]{1,0:T(8,128)(2,1)S(1)} %get-tuple-element.65), channel_id=1, source_target_pairs={{0,80},{16,96},{32,112},{48,0},{64,16},{80,32},{96,48},{112,64},{1... | collective-permute-start | bytes 196616 | tf_op jit(solution)/shard_map/ppermute | solution.py:242
  139.4 7.2 %collective-permute-start.16 = (f32[264,256]{1,0:T(8,128)S(1)}, f32[264,256]{1,0:T(8,128)S(1)}, u32[]{:S(2)}, u32[]{:S(2)}) collective-permute-start(f32[264,256]{1,0:T(8,128)S(1)} %get-tuple-element.67), channel_id=1, source_target_pairs={{0,8},{8,0},{1,9},{9,1},{2,10},{10,2},{3,11},{11,3},{4,12},{12,4},... | collective-permute-start | bytes 811016 | tf_op jit(solution)/shard_map/ppermute | solution.py:237
  175.7 4.2 %collective-permute-start.17 = (f32[256,256]{1,0:T(8,128)S(1)}, f32[256,256]{1,0:T(8,128)S(1)}, u32[]{:S(2)}, u32[]{:S(2)}) collective-permute-start(f32[256,256]{1,0:T(8,128)S(1)} %bitcast.6), channel_id=1, source_target_pairs={{0,8},{8,0},{1,9},{9,1},{2,10},{10,2},{3,11},{11,3},{4,12},{12,4},... | collective-permute-start | bytes 786440 | tf_op jit(solution)/shard_map/ppermute | solution.py:237

commit v8 on v7

--- a/solution.py
+++ b/solution.py
@@ -190,12 +190,16 @@
         ovs[q] = (ov, ov2)[q // 4][q % 4, at(1 - yh, ROWS), at(c, COLS)]
 
 
-def near_body(total, before, after, three, three_half, two_half):
-    two = total[...] + after[...].astype(F32)
-    t = two + before[...].astype(F32)
+def two_body(total, after, two, two_half):
+    t = total[...] + after[...].astype(F32)
+    two[...] = t
+    two_half[...] = t.astype(BF)
+
+
+def three_body(two, before, three, three_half):
+    t = two[...] + before[...].astype(F32)
     three[...] = t
     three_half[...] = t.astype(BF)
-    two_half[...] = two.astype(BF)
 
 
 def pieces_body(s, keep, got, part, ov, ov2, out, tot):
@@ -309,14 +313,21 @@
             mine, other = kernel(pair_body, [tile, half], sums)(*chip)
             recv = swap(other, "yh")
         total, out = kernel(rows_body, [tile, half], scalars=0)(mine, recv)
-        three, three_half, two_half = kernel(
-            near_body, [tile, half, half], scalars=0
-        )(total, along_z(out, 1), along_z(out, -1))
+        after = along_z(out, -1)
+        before = along_z(out, 1)
+        two, two_half = kernel(two_body, [tile, half], scalars=0)(
+            total, after
+        )
+        far_two = along_z(two_half, 3)
+        three, three_half = kernel(three_body, [tile, half], scalars=0)(
+            two, before
+        )
+        far_three = along_z(three_half, -3)
         (msg,) = kernel(update_body, [message])(
             s,
             three,
-            along_z(two_half, 3),
-            along_z(three_half, -3),
+            far_two,
+            far_three,
             rq,
             dq,
             b_ov,

time: 182 us -> 181 us (level)
  starting transfers between devices: 40.7 us -> 37.7 us
  waiting for transfers between devices: 34.8 us -> 37.4 us
    ppermute x8, starting transfers between devices: 17.6 us -> 14.1 us  [along_z(): return lax.ppermute(value, 'z', [(i, (i + shift) % n) for i in range(n)])]
    ppermute x8, waiting for transfers between devices: 12.5 us -> 15.1 us  [along_z(): return lax.ppermute(value, 'z', [(i, (i + shift) % n) for i in range(n)])]
    pallas_call x16 -> x18, Pallas kernels: 22.8 us -> 22.8 us  [call(): pl.pallas_call(body, out_shape=list(outputs), in_specs=[pl.BlockSpec(memo...]
  transfers between devices with their start and end apart: 18 -> 18, of which waited for: 12 -> 14; matrix products, arithmetic and copies ran while one was open for 0% -> 0% of each run, Pallas kernels for 5% -> 5%
where the time goes in v8:
time: 181 us
  blocking collectives  82.5 us (46%)
  starting transfers between devices  37.7 us (21%)
  waiting for transfers between devices  37.4 us (21%)
  Pallas kernels  22.8 us (13%)
    all_to_all x3, blocking collectives, local(): msg = lax.all_to_all(msg, PLANE, 0, 0, tiled=True)  54.2 us
    ppermute x10, starting transfers between devices, swap(): return lax.ppermute(value, axis, [(0, 1), (1, 0)])  23.6 us
    pallas_call x18, Pallas kernels, call(): pl.pallas_call(body, out_shape=list(outputs), in_specs=[pl.BlockSpec(memo...  22.8 us
    ppermute x10, waiting for transfers between devices, swap(): return lax.ppermute(value, axis, [(0, 1), (1, 0)])  22.3 us
    ppermute x8, waiting for transfers between devices, along_z(): return lax.ppermute(value, 'z', [(i, (i + shift) % n) for i in range(n)])  15.1 us
    all_to_all x1, blocking collectives, local(): pieces = lax.all_to_all(pieces, ('yh', 'z'), 0, 0, tiled=True)  15.1 us
    ppermute x8, starting transfers between devices, along_z(): return lax.ppermute(value, 'z', [(i, (i + shift) % n) for i in range(n)])  14.1 us
    all_to_all x1, blocking collectives, local(): w = lax.all_to_all(pieces, ('yh', 'z'), 0, 0, tiled=True).reshape(256, COLS)  13.2 us
  transfers between devices with their start and end apart: 18, of which 14 were waited for; matrix products, arithmetic and copies ran while one was open for 0% of the time, Pallas kernels for 5%

profile of v8, /device:TPU:1, one launch (start us, length us, event | category | flops | bytes accessed | tf_op | source)
XLA Modules:
  0.0 180.7 jit_solution(4007691815175861094)
XLA Ops:
  0.0 3.2 %collective-permute-start = (bf16[4,256,2048]{2,1,0:T(8,128)(2,1)}, bf16[4,256,2048]{2,1,0:T(8,128)(2,1)}, u32[]{:S(2)}, u32[]{:S(2)}) collective-permute-start(bf16[4,256,2048]{2,1,0:T(8,128)(2,1)} %v_h.1), channel_id=1, source_target_pairs={{0,8},{8,0},{1,9},{9,1},{2,10},{10,2},{3,11},{11,3},{4,12},{12,4},... | collective-permute-start | bytes 12582920 | tf_op jit(solution)/shard_map/ppermute | solution.py:241
  3.3 3.3 %shard_map.73 = (bf16[16,136,256]{2,1,0:T(8,128)(2,1)S(1)}, f32[128,256]{1,0:T(8,128)S(1)}, f32[128,256]{1,0:T(8,128)S(1)}, bf16[4,256,2048]{2,1,0:T(8,128)(2,1)S(1)}) custom-call(s32[3]{0:T(128)S(1)} %pad_add_fusion.s, f32[256,512]{1,0:T(8,128)} %rhs_h.1, f32[1,256]{1,0:T(1,128)} %bitcast.9, f32[1,512]{1,0:T(1,128)} %bitcast.8, bf16[4,256,512]{2,1,0:T(8,128)(2,1)} %ov.4, ...), custom_call_target="tpu_custom_call" | custom-call | bytes 11340812 | tf_op jit(solution)/shard_map/pallas_call | solution.py:32
  6.6 22.2 %all_to_all.25.u = bf16[16,136,256]{2,1,0:T(8,128)(2,1)S(1)} all-to-all(bf16[16,136,256]{2,1,0:T(8,128)(2,1)S(1)} %get-tuple-element.39), channel_id=1, replica_groups=mesh['yh'=2,'z'=8,'c'=2,'x'=4,'yl'=2] {'x','yl','yh'}, dimensions={0} | all-to-all | bytes 2228224 | tf_op jit(solution)/shard_map/all_to_all | solution.py:278
  28.8 1.9 %collective-permute-start.3 = (bf16[4,256,512]{2,1,0:T(8,128)(2,1)S(1)}, bf16[4,256,512]{2,1,0:T(8,128)(2,1)S(1)}, u32[]{:S(2)}, u32[]{:S(2)}) collective-permute-start(bf16[4,256,512]{2,1,0:T(8,128)(2,1)S(1)} %copy-done), channel_id=1, source_target_pairs={{0,8},{8,0},{1,9},{9,1},{2,10},{10,2},{3,11},{11,3},{4,12},{12,4},... | collective-permute-start | bytes 3145736 | tf_op jit(solution)/shard_map/ppermute | solution.py:241
  30.7 2.8 %shard_map.74.v2 = bf16[4,256,2048]{2,1,0:T(8,128)(2,1)S(1)} custom-call(s32[3]{0:T(128)S(1)} %pad_add_fusion.s, bf16[4,256,2048]{2,1,0:T(8,128)(2,1)} %collective-permute-done.v_h, bf16[1,8,128]{2,1,0:T(8,128)(2,1)S(1)} %slice.3.after), custom_call_target="tpu_custom_call" | custom-call | bytes 8390668 | tf_op jit(solution)/shard_map/pallas_call | solution.py:32
  33.6 3.4 %shard_map.75 = (f32[256,256]{1,0:T(8,128)S(1)}, f32[264,256]{1,0:T(8,128)S(1)}, f32[8,128]{1,0:T(8,128)S(1)}) custom-call(s32[3]{0:T(128)S(1)} %pad_add_fusion.s, f32[4]{0:T(128)S(1)} %copy-done.2, bf16[4,256,2048]{2,1,0:T(8,128)(2,1)S(1)} %get-tuple-element.42.v1, bf16[4,256,2048]{2,1,0:T(8,128)(2,1)S(1)} %shard_map.74.v2, ...), custom_call_target="tpu_custom_call" | custom-call | flops 2684354560 | bytes 14233628 | tf_op jit(solution)/shard_map/pallas_call | solution.py:32
  37.2 1.5 collective-permute-done.2.got
  40.3 2.3 %collective-permute-start.4 = (bf16[128,256]{1,0:T(8,128)(2,1)S(1)}, bf16[128,256]{1,0:T(8,128)(2,1)S(1)}, u32[]{:S(2)}, u32[]{:S(2)}) collective-permute-start(bf16[128,256]{1,0:T(8,128)(2,1)S(1)} %get-tuple-element.49), channel_id=1, source_target_pairs={{0,128},{128,0},{1,129},{129,1},{2,130},{130,2},{3,131},{131,3},{4... | collective-permute-start | bytes 196616 | tf_op jit(solution)/shard_map/ppermute | solution.py:241
  42.6 13.3 %collective-permute-done.4.recv = bf16[128,256]{1,0:T(8,128)(2,1)S(1)} collective-permute-done((bf16[128,256]{1,0:T(8,128)(2,1)S(1)}, bf16[128,256]{1,0:T(8,128)(2,1)S(1)}, u32[]{:S(2)}, u32[]{:S(2)}) %collective-permute-start.4) | collective-permute-done | bytes 65568 | tf_op jit(solution)/shard_map/ppermute | solution.py:241
  55.9 5.7 %collective-permute-start.5 = (bf16[128,256]{1,0:T(8,128)(2,1)S(1)}, bf16[128,256]{1,0:T(8,128)(2,1)S(1)}, u32[]{:S(2)}, u32[]{:S(2)}) collective-permute-start(bf16[128,256]{1,0:T(8,128)(2,1)S(1)} %get-tuple-element.51), channel_id=1, source_target_pairs={{0,112},{16,0},{32,16},{48,32},{64,48},{80,64},{96,80},{112,96},{1... | collective-permute-start | bytes 196616 | tf_op jit(solution)/shard_map/ppermute | solution.py:246
  61.6 1.3 collective-permute-done.5.after
  62.9 3.0 %collective-permute-done.6.before = bf16[128,256]{1,0:T(8,128)(2,1)S(1)} collective-permute-done((bf16[128,256]{1,0:T(8,128)(2,1)S(1)}, bf16[128,256]{1,0:T(8,128)(2,1)S(1)}, u32[]{:S(2)}, u32[]{:S(2)}) %collective-permute-start.6) | collective-permute-done | bytes 65568 | tf_op jit(solution)/shard_map/ppermute | solution.py:246
  66.4 2.9 %collective-permute-start.7 = (bf16[128,256]{1,0:T(8,128)(2,1)S(1)}, bf16[128,256]{1,0:T(8,128)(2,1)S(1)}, u32[]{:S(2)}, u32[]{:S(2)}) collective-permute-start(bf16[128,256]{1,0:T(8,128)(2,1)S(1)} %get-tuple-element.54), channel_id=1, source_target_pairs={{0,48},{16,64},{32,80},{48,96},{64,112},{80,0},{96,16},{112,32},{1... | collective-permute-start | bytes 196616 | tf_op jit(solution)/shard_map/ppermute | solution.py:246
  69.3 1.7 collective-permute-done.8.after
  70.9 2.0 %collective-permute-done.7.before = bf16[128,256]{1,0:T(8,128)(2,1)S(1)} collective-permute-done((bf16[128,256]{1,0:T(8,128)(2,1)S(1)}, bf16[128,256]{1,0:T(8,128)(2,1)S(1)}, u32[]{:S(2)}, u32[]{:S(2)}) %collective-permute-start.7) | collective-permute-done | bytes 65568 | tf_op jit(solution)/shard_map/ppermute | solution.py:246
  73.9 16.2 %all_to_all.26.u = bf16[16,136,256]{2,1,0:T(8,128)(2,1)S(1)} all-to-all(bf16[16,136,256]{2,1,0:T(8,128)(2,1)S(1)} %shard_map.80), channel_id=1, replica_groups=mesh['yh'=2,'z'=8,'c'=2,'x'=4,'yl'=2] {'x','yl','yh'}, dimensions={0} | all-to-all | bytes 2228224 | tf_op jit(solution)/shard_map/all_to_all | solution.py:278
  90.1 3.4 %shard_map.81 = (f32[256,256]{1,0:T(8,128)S(1)}, f32[264,256]{1,0:T(8,128)S(1)}, f32[8,128]{1,0:T(8,128)S(1)}) custom-call(s32[3]{0:T(128)S(1)} %pad_add_fusion.s, f32[4]{0:T(128)S(1)} %copy-done.2, bf16[4,256,2048]{2,1,0:T(8,128)(2,1)S(1)} %get-tuple-element.42.v1, bf16[4,256,2048]{2,1,0:T(8,128)(2,1)S(1)} %shard_map.74.v2, ...), custom_call_target="tpu_custom_call" | custom-call | flops 2684354560 | bytes 14233628 | tf_op jit(solution)/shard_map/pallas_call | solution.py:32
  93.6 5.6 %collective-permute-start.10 = (f32[264,256]{1,0:T(8,128)S(1)}, f32[264,256]{1,0:T(8,128)S(1)}, u32[]{:S(2)}, u32[]{:S(2)}) collective-permute-start(f32[264,256]{1,0:T(8,128)S(1)} %get-tuple-element.60), channel_id=1, source_target_pairs={{0,8},{8,0},{1,9},{9,1},{2,10},{10,2},{3,11},{11,3},{4,12},{12,4},... | collective-permute-start | bytes 811016 | tf_op jit(solution)/shard_map/ppermute | solution.py:241
  99.2 1.2 collective-permute-done.10.got
  102.0 3.9 %collective-permute-done.11.recv = bf16[128,256]{1,0:T(8,128)(2,1)S(1)} collective-permute-done((bf16[128,256]{1,0:T(8,128)(2,1)S(1)}, bf16[128,256]{1,0:T(8,128)(2,1)S(1)}, u32[]{:S(2)}, u32[]{:S(2)}) %collective-permute-start.11) | collective-permute-done | bytes 65568 | tf_op jit(solution)/shard_map/ppermute | solution.py:241
  105.9 1.2 collective-permute-start.12
  107.7 1.6 collective-permute-done.12.after
  109.3 2.2 %collective-permute-done.13.before = bf16[128,256]{1,0:T(8,128)(2,1)S(1)} collective-permute-done((bf16[128,256]{1,0:T(8,128)(2,1)S(1)}, bf16[128,256]{1,0:T(8,128)(2,1)S(1)}, u32[]{:S(2)}, u32[]{:S(2)}) %collective-permute-start.13) | collective-permute-done | bytes 65568 | tf_op jit(solution)/shard_map/ppermute | solution.py:246
  112.0 2.9 %collective-permute-start.14 = (bf16[128,256]{1,0:T(8,128)(2,1)S(1)}, bf16[128,256]{1,0:T(8,128)(2,1)S(1)}, u32[]{:S(2)}, u32[]{:S(2)}) collective-permute-start(bf16[128,256]{1,0:T(8,128)(2,1)S(1)} %get-tuple-element.68), channel_id=1, source_target_pairs={{0,48},{16,64},{32,80},{48,96},{64,112},{80,0},{96,16},{112,32},{1... | collective-permute-start | bytes 196616 | tf_op jit(solution)/shard_map/ppermute | solution.py:246
  114.9 3.2 %collective-permute-done.15.after = bf16[128,256]{1,0:T(8,128)(2,1)S(1)} collective-permute-done((bf16[128,256]{1,0:T(8,128)(2,1)S(1)}, bf16[128,256]{1,0:T(8,128)(2,1)S(1)}, u32[]{:S(2)}, u32[]{:S(2)}) %collective-permute-start.15) | collective-permute-done | bytes 65568 | tf_op jit(solution)/shard_map/ppermute | solution.py:246
  119.1 15.8 %all_to_all.27.u = bf16[16,136,256]{2,1,0:T(8,128)(2,1)S(1)} all-to-all(bf16[16,136,256]{2,1,0:T(8,128)(2,1)S(1)} %shard_map.86), channel_id=1, replica_groups=mesh['yh'=2,'z'=8,'c'=2,'x'=4,'yl'=2] {'x','yl','yh'}, dimensions={0} | all-to-all | bytes 2228224 | tf_op jit(solution)/shard_map/all_to_all | solution.py:278
  134.9 3.4 %shard_map.87 = (f32[256,256]{1,0:T(8,128)S(1)}, f32[264,256]{1,0:T(8,128)S(1)}, f32[8,128]{1,0:T(8,128)S(1)}) custom-call(s32[3]{0:T(128)S(1)} %pad_add_fusion.s, f32[4]{0:T(128)S(1)} %copy-done.2, bf16[4,256,2048]{2,1,0:T(8,128)(2,1)S(1)} %get-tuple-element.42.v1, bf16[4,256,2048]{2,1,0:T(8,128)(2,1)S(1)} %shard_map.74.v2, ...), custom_call_target="tpu_custom_call" | custom-call | flops 2684354560 | bytes 14233628 | tf_op jit(solution)/shard_map/pallas_call | solution.py:32
  138.3 5.9 %collective-permute-start.16 = (f32[264,256]{1,0:T(8,128)S(1)}, f32[264,256]{1,0:T(8,128)S(1)}, u32[]{:S(2)}, u32[]{:S(2)}) collective-permute-start(f32[264,256]{1,0:T(8,128)S(1)} %get-tuple-element.71), channel_id=1, source_target_pairs={{0,8},{8,0},{1,9},{9,1},{2,10},{10,2},{3,11},{11,3},{4,12},{12,4},... | collective-permute-start | bytes 811016 | tf_op jit(solution)/shard_map/ppermute | solution.py:241
  146.2 15.1 %all_to_all.28.pieces = bf16[16,16,256]{2,1,0:T(8,128)(2,1)S(1)} all-to-all(bf16[16,16,256]{2,1,0:T(8,128)(2,1)S(1)} %shard_map.88), channel_id=1, replica_groups=mesh['yh'=2,'z'=8,'c'=2,'x'=4,'yl'=2] {'yh','z'}, dimensions={0} | all-to-all | bytes 262144 | tf_op jit(solution)/shard_map/all_to_all | solution.py:338
  161.9 13.2 %all_to_all.29 = f32[16,16,256]{2,1,0:T(8,128)S(1)} all-to-all(f32[16,16,256]{2,1,0:T(8,128)S(1)} %shard_map.89), channel_id=1, replica_groups=mesh['yh'=2,'z'=8,'c'=2,'x'=4,'yl'=2] {'yh','z'}, dimensions={0} | all-to-all | bytes 524288 | tf_op jit(solution)/shard_map/all_to_all | solution.py:340
  175.1 3.0 %collective-permute-start.17 = (f32[256,256]{1,0:T(8,128)S(1)}, f32[256,256]{1,0:T(8,128)S(1)}, u32[]{:S(2)}, u32[]{:S(2)}) collective-permute-start(f32[256,256]{1,0:T(8,128)S(1)} %bitcast.6), channel_id=1, source_target_pairs={{0,8},{8,0},{1,9},{9,1},{2,10},{10,2},{3,11},{11,3},{4,12},{12,4},... | collective-permute-start | bytes 786440 | tf_op jit(solution)/shard_map/ppermute | solution.py:241
  179.3 1.4 shard_map.90
  (35 shorter events, 10.6 us)
Async XLA Ops:
  0.0 30.7 %collective-permute-start = (bf16[4,256,2048]{2,1,0:T(8,128)(2,1)}, bf16[4,256,2048]{2,1,0:T(8,128)(2,1)}, u32[]{:S(2)}, u32[]{:S(2)}) collective-permute-start(bf16[4,256,2048]{2,1,0:T(8,128)(2,1)} %v_h.1), channel_id=1, source_target_pairs={{0,8},{8,0},{1,9},{9,1},{2,10},{10,2},{3,11},{11,3},{4,12},{12,4},... | collective-permute-start | bytes 12582920 | tf_op jit(solution)/shard_map/ppermute | solution.py:241
  3.2 30.4 %collective-permute-start.1 = (bf16[4,512,512]{2,1,0:T(8,128)(2,1)}, bf16[4,512,512]{2,1,0:T(8,128)(2,1)S(1)}, u32[]{:S(2)}, u32[]{:S(2)}) collective-permute-start(bf16[4,512,512]{2,1,0:T(8,128)(2,1)} %o1.5), channel_id=1, source_target_pairs={{0,8},{8,0},{1,9},{9,1},{2,10},{10,2},{3,11},{11,3},{4,12},{12,4},... | collective-permute-start | bytes 6291464 | tf_op jit(solution)/shard_map/ppermute | solution.py:241
  6.6 22.2 %copy-start = (bf16[4,256,512]{2,1,0:T(8,128)(2,1)S(1)}, bf16[4,256,512]{2,1,0:T(8,128)(2,1)}, u32[]{:S(2)}) copy-start(bf16[4,256,512]{2,1,0:T(8,128)(2,1)} %ov.4) | copy-start | bytes 3145732
  28.8 8.4 %collective-permute-start.3 = (bf16[4,256,512]{2,1,0:T(8,128)(2,1)S(1)}, bf16[4,256,512]{2,1,0:T(8,128)(2,1)S(1)}, u32[]{:S(2)}, u32[]{:S(2)}) collective-permute-start(bf16[4,256,512]{2,1,0:T(8,128)(2,1)S(1)} %copy-done), channel_id=1, source_target_pairs={{0,8},{8,0},{1,9},{9,1},{2,10},{10,2},{3,11},{11,3},{4,12},{12,4},... | collective-permute-start | bytes 3145736 | tf_op jit(solution)/shard_map/ppermute | solution.py:241
  30.7 2.9 %copy-start.1 = (bf16[4,512,512]{2,1,0:T(8,128)(2,1)S(1)}, bf16[4,512,512]{2,1,0:T(8,128)(2,1)}, u32[]{:S(2)}) copy-start(bf16[4,512,512]{2,1,0:T(8,128)(2,1)} %o1.5) | copy-start | bytes 6291460
  30.7 2.9 %copy-start.2 = (f32[4]{0:T(128)S(1)}, f32[4]{0:T(128)}, u32[]{:S(2)}) copy-start(f32[4]{0:T(128)} %fit.2) | copy-start | bytes 52
  37.1 1.6 collective-permute-start.2
  39.6 33.4 %collective-permute-start.9 = (bf16[8,128,256]{2,1,0:T(8,128)(2,1)S(1)}, bf16[8,128,256]{2,1,0:T(8,128)(2,1)S(1)}, u32[]{:S(2)}, u32[]{:S(2)}) collective-permute-start(bf16[8,128,256]{2,1,0:T(8,128)(2,1)S(1)} %get-tuple-element.58), channel_id=1, source_target_pairs={{0,128},{128,0},{1,129},{129,1},{2,130},{130,2},{3,131},{131,3},{4... | collective-permute-start | bytes 1572872 | tf_op jit(solution)/shard_map/ppermute | solution.py:241
  40.3 15.6 %collective-permute-start.4 = (bf16[128,256]{1,0:T(8,128)(2,1)S(1)}, bf16[128,256]{1,0:T(8,128)(2,1)S(1)}, u32[]{:S(2)}, u32[]{:S(2)}) collective-permute-start(bf16[128,256]{1,0:T(8,128)(2,1)S(1)} %get-tuple-element.49), channel_id=1, source_target_pairs={{0,128},{128,0},{1,129},{129,1},{2,130},{130,2},{3,131},{131,3},{4... | collective-permute-start | bytes 196616 | tf_op jit(solution)/shard_map/ppermute | solution.py:241
  55.9 7.0 %collective-permute-start.5 = (bf16[128,256]{1,0:T(8,128)(2,1)S(1)}, bf16[128,256]{1,0:T(8,128)(2,1)S(1)}, u32[]{:S(2)}, u32[]{:S(2)}) collective-permute-start(bf16[128,256]{1,0:T(8,128)(2,1)S(1)} %get-tuple-element.51), channel_id=1, source_target_pairs={{0,112},{16,0},{32,16},{48,32},{64,48},{80,64},{96,80},{112,96},{1... | collective-permute-start | bytes 196616 | tf_op jit(solution)/shard_map/ppermute | solution.py:246
  61.6 4.3 %collective-permute-start.6 = (bf16[128,256]{1,0:T(8,128)(2,1)S(1)}, bf16[128,256]{1,0:T(8,128)(2,1)S(1)}, u32[]{:S(2)}, u32[]{:S(2)}) collective-permute-start(bf16[128,256]{1,0:T(8,128)(2,1)S(1)} %get-tuple-element.51), channel_id=1, source_target_pairs={{0,16},{16,32},{32,48},{48,64},{64,80},{80,96},{96,112},{112,0},{1... | collective-permute-start | bytes 196616 | tf_op jit(solution)/shard_map/ppermute | solution.py:246
  65.9 5.0 %collective-permute-start.8 = (bf16[128,256]{1,0:T(8,128)(2,1)S(1)}, bf16[128,256]{1,0:T(8,128)(2,1)S(1)}, u32[]{:S(2)}, u32[]{:S(2)}) collective-permute-start(bf16[128,256]{1,0:T(8,128)(2,1)S(1)} %get-tuple-element.55), channel_id=1, source_target_pairs={{0,80},{16,96},{32,112},{48,0},{64,16},{80,32},{96,48},{112,64},{1... | collective-permute-start | bytes 196616 | tf_op jit(solution)/shard_map/ppermute | solution.py:246
  66.4 6.6 %collective-permute-start.7 = (bf16[128,256]{1,0:T(8,128)(2,1)S(1)}, bf16[128,256]{1,0:T(8,128)(2,1)S(1)}, u32[]{:S(2)}, u32[]{:S(2)}) collective-permute-start(bf16[128,256]{1,0:T(8,128)(2,1)S(1)} %get-tuple-element.54), channel_id=1, source_target_pairs={{0,48},{16,64},{32,80},{48,96},{64,112},{80,0},{96,16},{112,32},{1... | collective-permute-start | bytes 196616 | tf_op jit(solution)/shard_map/ppermute | solution.py:246
  93.6 6.8 %collective-permute-start.10 = (f32[264,256]{1,0:T(8,128)S(1)}, f32[264,256]{1,0:T(8,128)S(1)}, u32[]{:S(2)}, u32[]{:S(2)}) collective-permute-start(f32[264,256]{1,0:T(8,128)S(1)} %get-tuple-element.60), channel_id=1, source_target_pairs={{0,8},{8,0},{1,9},{9,1},{2,10},{10,2},{3,11},{11,3},{4,12},{12,4},... | collective-permute-start | bytes 811016 | tf_op jit(solution)/shard_map/ppermute | solution.py:241
  101.2 4.7 %collective-permute-start.11 = (bf16[128,256]{1,0:T(8,128)(2,1)S(1)}, bf16[128,256]{1,0:T(8,128)(2,1)S(1)}, u32[]{:S(2)}, u32[]{:S(2)}) collective-permute-start(bf16[128,256]{1,0:T(8,128)(2,1)S(1)} %get-tuple-element.63), channel_id=1, source_target_pairs={{0,128},{128,0},{1,129},{129,1},{2,130},{130,2},{3,131},{131,3},{4... | collective-permute-start | bytes 196616 | tf_op jit(solution)/shard_map/ppermute | solution.py:241
  105.9 3.3 %collective-permute-start.12 = (bf16[128,256]{1,0:T(8,128)(2,1)S(1)}, bf16[128,256]{1,0:T(8,128)(2,1)S(1)}, u32[]{:S(2)}, u32[]{:S(2)}) collective-permute-start(bf16[128,256]{1,0:T(8,128)(2,1)S(1)} %get-tuple-element.65), channel_id=1, source_target_pairs={{0,112},{16,0},{32,16},{48,32},{64,48},{80,64},{96,80},{112,96},{1... | collective-permute-start | bytes 196616 | tf_op jit(solution)/shard_map/ppermute | solution.py:246
  107.2 4.3 %collective-permute-start.13 = (bf16[128,256]{1,0:T(8,128)(2,1)S(1)}, bf16[128,256]{1,0:T(8,128)(2,1)S(1)}, u32[]{:S(2)}, u32[]{:S(2)}) collective-permute-start(bf16[128,256]{1,0:T(8,128)(2,1)S(1)} %get-tuple-element.65), channel_id=1, source_target_pairs={{0,16},{16,32},{32,48},{48,64},{64,80},{80,96},{96,112},{112,0},{1... | collective-permute-start | bytes 196616 | tf_op jit(solution)/shard_map/ppermute | solution.py:246
  111.5 6.5 %collective-permute-start.15 = (bf16[128,256]{1,0:T(8,128)(2,1)S(1)}, bf16[128,256]{1,0:T(8,128)(2,1)S(1)}, u32[]{:S(2)}, u32[]{:S(2)}) collective-permute-start(bf16[128,256]{1,0:T(8,128)(2,1)S(1)} %get-tuple-element.69), channel_id=1, source_target_pairs={{0,80},{16,96},{32,112},{48,0},{64,16},{80,32},{96,48},{112,64},{1... | collective-permute-start | bytes 196616 | tf_op jit(solution)/shard_map/ppermute | solution.py:246
  112.0 6.3 %collective-permute-start.14 = (bf16[128,256]{1,0:T(8,128)(2,1)S(1)}, bf16[128,256]{1,0:T(8,128)(2,1)S(1)}, u32[]{:S(2)}, u32[]{:S(2)}) collective-permute-start(bf16[128,256]{1,0:T(8,128)(2,1)S(1)} %get-tuple-element.68), channel_id=1, source_target_pairs={{0,48},{16,64},{32,80},{48,96},{64,112},{80,0},{96,16},{112,32},{1... | collective-permute-start | bytes 196616 | tf_op jit(solution)/shard_map/ppermute | solution.py:246
  138.3 7.1 %collective-permute-start.16 = (f32[264,256]{1,0:T(8,128)S(1)}, f32[264,256]{1,0:T(8,128)S(1)}, u32[]{:S(2)}, u32[]{:S(2)}) collective-permute-start(f32[264,256]{1,0:T(8,128)S(1)} %get-tuple-element.71), channel_id=1, source_target_pairs={{0,8},{8,0},{1,9},{9,1},{2,10},{10,2},{3,11},{11,3},{4,12},{12,4},... | collective-permute-start | bytes 811016 | tf_op jit(solution)/shard_map/ppermute | solution.py:241
  175.1 4.2 %collective-permute-start.17 = (f32[256,256]{1,0:T(8,128)S(1)}, f32[256,256]{1,0:T(8,128)S(1)}, u32[]{:S(2)}, u32[]{:S(2)}) collective-permute-start(f32[256,256]{1,0:T(8,128)S(1)} %bitcast.6), channel_id=1, source_target_pairs={{0,8},{8,0},{1,9},{9,1},{2,10},{10,2},{3,11},{11,3},{4,12},{12,4},... | collective-permute-start | bytes 786440 | tf_op jit(solution)/shard_map/ppermute | solution.py:241

commit v9 on v8

--- a/solution.py
+++ b/solution.py
@@ -221,20 +221,23 @@
     )
 
 
-def last_body(s, pieces, rq, dq, out):
+def last_body(pieces, out):
     share = pieces[0].astype(F32)
     for p in range(1, 16):
         share += pieces[p].astype(F32)
-    rows = at(s[2], 16)
-    w = (rq[rows, :] + share) / dq[rows, :]
+    share = share.astype(BF)
     for p in range(16):
-        out[p] = w
-
-
-def join_body(s, w, wc, out):
+        out[p] = share
+
+
+def join_body(s, own, other, rhs, ev, eo, out, share):
     c = s[0]
-    out[:, at(c, COLS)] = w[...]
-    out[:, at(1 - c, COLS)] = wc[...]
+    share[:, at(c, COLS)] = own[...].astype(F32)
+    share[:, at(1 - c, COLS)] = other[...].astype(F32)
+    column = jnp.broadcast_to(ev[...], (128, 256)).T
+    for h in range(4):
+        lanes = slice(h * 128, (h + 1) * 128)
+        out[:, lanes] = (rhs[:, lanes] + share[:, lanes]) / (column - eo[:, lanes])
 
 
 def swap(value, axis):
@@ -336,9 +339,13 @@
         )
     (pieces,) = kernel(pieces_body, [sds(16, 16, COLS, dtype=BF)], sums)(*chip)
     pieces = lax.all_to_all(pieces, ("yh", "z"), 0, 0, tiled=True)
-    (pieces,) = kernel(last_body, [sds(16, 16, COLS)])(s, pieces, rq, dq)
-    w = lax.all_to_all(pieces, ("yh", "z"), 0, 0, tiled=True).reshape(256, COLS)
-    return kernel(join_body, [sds(256, O)])(s, w, swap(w, "c"))[0]
+    (pieces,) = kernel(last_body, [sds(16, 16, COLS, dtype=BF)], scalars=0)(
+        pieces
+    )
+    own = lax.all_to_all(pieces, ("yh", "z"), 0, 0, tiled=True).reshape(256, COLS)
+    return kernel(join_body, [sds(256, O)], [pltpu.VMEM((256, O), F32)])(
+        s, own, swap(own, "c"), rhs, eps_vir[None, :], eps_occ[None, :]
+    )[0]
 
 
 def solution(mesh):

time: 181 us -> 179 us (0.989)
  no operation moved by 1% of the time
where the time goes in v9:
time: 179 us
  blocking collectives  82 us (46%)
  starting transfers between devices  37.2 us (21%)
  waiting for transfers between devices  37.2 us (21%)
  Pallas kernels  22.4 us (13%)
    all_to_all x3, blocking collectives, local(): msg = lax.all_to_all(msg, PLANE, 0, 0, tiled=True)  54.2 us
    ppermute x10, starting transfers between devices, swap(): return lax.ppermute(value, axis, [(0, 1), (1, 0)])  23.1 us
    pallas_call x18, Pallas kernels, call(): pl.pallas_call(body, out_shape=list(outputs), in_specs=[pl.BlockSpec(memo...  22.4 us
    ppermute x10, waiting for transfers between devices, swap(): return lax.ppermute(value, axis, [(0, 1), (1, 0)])  22.1 us
    ppermute x8, waiting for transfers between devices, along_z(): return lax.ppermute(value, 'z', [(i, (i + shift) % n) for i in range(n)])  15.1 us
    all_to_all x1, blocking collectives, local(): pieces = lax.all_to_all(pieces, ('yh', 'z'), 0, 0, tiled=True)  15.1 us
    ppermute x8, starting transfers between devices, along_z(): return lax.ppermute(value, 'z', [(i, (i + shift) % n) for i in range(n)])  14.1 us
    all_to_all x1, blocking collectives, local(): lax.all_to_all(pieces, ('yh', 'z'), 0, 0, tiled=True).reshape(256, COLS)  12.7 us
  transfers between devices with their start and end apart: 18, of which 14 were waited for; matrix products, arithmetic and copies ran while one was open for 0% of the time, Pallas kernels for 5%

profile of v9, /device:TPU:1, one launch (start us, length us, event | category | flops | bytes accessed | tf_op | source)
XLA Modules:
  0.0 179.1 jit_solution(9521672900722219036)
XLA Ops:
  0.0 3.2 %collective-permute-start = (bf16[4,256,2048]{2,1,0:T(8,128)(2,1)}, bf16[4,256,2048]{2,1,0:T(8,128)(2,1)}, u32[]{:S(2)}, u32[]{:S(2)}) collective-permute-start(bf16[4,256,2048]{2,1,0:T(8,128)(2,1)} %v_h.1), channel_id=1, source_target_pairs={{0,8},{8,0},{1,9},{9,1},{2,10},{10,2},{3,11},{11,3},{4,12},{12,4},... | collective-permute-start | bytes 12582920 | tf_op jit(solution)/shard_map/ppermute | solution.py:244
  3.3 3.3 %shard_map.73 = (bf16[16,136,256]{2,1,0:T(8,128)(2,1)S(1)}, f32[128,256]{1,0:T(8,128)S(1)}, f32[128,256]{1,0:T(8,128)S(1)}, bf16[4,256,2048]{2,1,0:T(8,128)(2,1)S(1)}) custom-call(s32[3]{0:T(128)S(1)} %pad_add_fusion.s, f32[256,512]{1,0:T(8,128)} %rhs.1, f32[1,256]{1,0:T(1,128)} %bitcast.10, f32[1,512]{1,0:T(1,128)} %bitcast.8, bf16[4,256,512]{2,1,0:T(8,128)(2,1)} %ov.4, ...), custom_call_target="tpu_custom_call" | custom-call | bytes 11340812 | tf_op jit(solution)/shard_map/pallas_call | solution.py:32
  6.6 22.2 %all_to_all.25.u = bf16[16,136,256]{2,1,0:T(8,128)(2,1)S(1)} all-to-all(bf16[16,136,256]{2,1,0:T(8,128)(2,1)S(1)} %get-tuple-element.39), channel_id=1, replica_groups=mesh['yh'=2,'z'=8,'c'=2,'x'=4,'yl'=2] {'x','yl','yh'}, dimensions={0} | all-to-all | bytes 2228224 | tf_op jit(solution)/shard_map/all_to_all | solution.py:281
  28.8 1.9 %collective-permute-start.3 = (bf16[4,256,512]{2,1,0:T(8,128)(2,1)S(1)}, bf16[4,256,512]{2,1,0:T(8,128)(2,1)S(1)}, u32[]{:S(2)}, u32[]{:S(2)}) collective-permute-start(bf16[4,256,512]{2,1,0:T(8,128)(2,1)S(1)} %copy-done), channel_id=1, source_target_pairs={{0,8},{8,0},{1,9},{9,1},{2,10},{10,2},{3,11},{11,3},{4,12},{12,4},... | collective-permute-start | bytes 3145736 | tf_op jit(solution)/shard_map/ppermute | solution.py:244
  30.7 2.8 %shard_map.74.v2 = bf16[4,256,2048]{2,1,0:T(8,128)(2,1)S(1)} custom-call(s32[3]{0:T(128)S(1)} %pad_add_fusion.s, bf16[4,256,2048]{2,1,0:T(8,128)(2,1)} %collective-permute-done.v_h, bf16[1,8,128]{2,1,0:T(8,128)(2,1)S(1)} %slice.3.after), custom_call_target="tpu_custom_call" | custom-call | bytes 8390668 | tf_op jit(solution)/shard_map/pallas_call | solution.py:32
  33.6 3.4 %shard_map.75 = (f32[256,256]{1,0:T(8,128)S(1)}, f32[264,256]{1,0:T(8,128)S(1)}, f32[8,128]{1,0:T(8,128)S(1)}) custom-call(s32[3]{0:T(128)S(1)} %pad_add_fusion.s, f32[4]{0:T(128)S(1)} %copy-done.4, bf16[4,256,2048]{2,1,0:T(8,128)(2,1)S(1)} %get-tuple-element.42.v1, bf16[4,256,2048]{2,1,0:T(8,128)(2,1)S(1)} %shard_map.74.v2, ...), custom_call_target="tpu_custom_call" | custom-call | flops 2684354560 | bytes 14233628 | tf_op jit(solution)/shard_map/pallas_call | solution.py:32
  37.2 1.5 collective-permute-done.2.got
  40.3 2.3 %collective-permute-start.4 = (bf16[128,256]{1,0:T(8,128)(2,1)S(1)}, bf16[128,256]{1,0:T(8,128)(2,1)S(1)}, u32[]{:S(2)}, u32[]{:S(2)}) collective-permute-start(bf16[128,256]{1,0:T(8,128)(2,1)S(1)} %get-tuple-element.49), channel_id=1, source_target_pairs={{0,128},{128,0},{1,129},{129,1},{2,130},{130,2},{3,131},{131,3},{4... | collective-permute-start | bytes 196616 | tf_op jit(solution)/shard_map/ppermute | solution.py:244
  42.6 13.3 %collective-permute-done.4.recv = bf16[128,256]{1,0:T(8,128)(2,1)S(1)} collective-permute-done((bf16[128,256]{1,0:T(8,128)(2,1)S(1)}, bf16[128,256]{1,0:T(8,128)(2,1)S(1)}, u32[]{:S(2)}, u32[]{:S(2)}) %collective-permute-start.4) | collective-permute-done | bytes 65568 | tf_op jit(solution)/shard_map/ppermute | solution.py:244
  55.9 5.7 %collective-permute-start.5 = (bf16[128,256]{1,0:T(8,128)(2,1)S(1)}, bf16[128,256]{1,0:T(8,128)(2,1)S(1)}, u32[]{:S(2)}, u32[]{:S(2)}) collective-permute-start(bf16[128,256]{1,0:T(8,128)(2,1)S(1)} %get-tuple-element.51), channel_id=1, source_target_pairs={{0,112},{16,0},{32,16},{48,32},{64,48},{80,64},{96,80},{112,96},{1... | collective-permute-start | bytes 196616 | tf_op jit(solution)/shard_map/ppermute | solution.py:249
  61.6 1.3 collective-permute-done.5.after
  62.9 3.0 %collective-permute-done.6.before = bf16[128,256]{1,0:T(8,128)(2,1)S(1)} collective-permute-done((bf16[128,256]{1,0:T(8,128)(2,1)S(1)}, bf16[128,256]{1,0:T(8,128)(2,1)S(1)}, u32[]{:S(2)}, u32[]{:S(2)}) %collective-permute-start.6) | collective-permute-done | bytes 65568 | tf_op jit(solution)/shard_map/ppermute | solution.py:249
  66.4 2.9 %collective-permute-start.7 = (bf16[128,256]{1,0:T(8,128)(2,1)S(1)}, bf16[128,256]{1,0:T(8,128)(2,1)S(1)}, u32[]{:S(2)}, u32[]{:S(2)}) collective-permute-start(bf16[128,256]{1,0:T(8,128)(2,1)S(1)} %get-tuple-element.54), channel_id=1, source_target_pairs={{0,48},{16,64},{32,80},{48,96},{64,112},{80,0},{96,16},{112,32},{1... | collective-permute-start | bytes 196616 | tf_op jit(solution)/shard_map/ppermute | solution.py:249
  69.3 1.7 collective-permute-done.8.after
  71.0 2.0 %collective-permute-done.7.before = bf16[128,256]{1,0:T(8,128)(2,1)S(1)} collective-permute-done((bf16[128,256]{1,0:T(8,128)(2,1)S(1)}, bf16[128,256]{1,0:T(8,128)(2,1)S(1)}, u32[]{:S(2)}, u32[]{:S(2)}) %collective-permute-start.7) | collective-permute-done | bytes 65568 | tf_op jit(solution)/shard_map/ppermute | solution.py:249
  73.9 16.2 %all_to_all.26.u = bf16[16,136,256]{2,1,0:T(8,128)(2,1)S(1)} all-to-all(bf16[16,136,256]{2,1,0:T(8,128)(2,1)S(1)} %shard_map.80), channel_id=1, replica_groups=mesh['yh'=2,'z'=8,'c'=2,'x'=4,'yl'=2] {'x','yl','yh'}, dimensions={0} | all-to-all | bytes 2228224 | tf_op jit(solution)/shard_map/all_to_all | solution.py:281
  90.1 3.4 %shard_map.81 = (f32[256,256]{1,0:T(8,128)S(1)}, f32[264,256]{1,0:T(8,128)S(1)}, f32[8,128]{1,0:T(8,128)S(1)}) custom-call(s32[3]{0:T(128)S(1)} %pad_add_fusion.s, f32[4]{0:T(128)S(1)} %copy-done.4, bf16[4,256,2048]{2,1,0:T(8,128)(2,1)S(1)} %get-tuple-element.42.v1, bf16[4,256,2048]{2,1,0:T(8,128)(2,1)S(1)} %shard_map.74.v2, ...), custom_call_target="tpu_custom_call" | custom-call | flops 2684354560 | bytes 14233628 | tf_op jit(solution)/shard_map/pallas_call | solution.py:32
  93.6 5.6 %collective-permute-start.10 = (f32[264,256]{1,0:T(8,128)S(1)}, f32[264,256]{1,0:T(8,128)S(1)}, u32[]{:S(2)}, u32[]{:S(2)}) collective-permute-start(f32[264,256]{1,0:T(8,128)S(1)} %get-tuple-element.60), channel_id=1, source_target_pairs={{0,8},{8,0},{1,9},{9,1},{2,10},{10,2},{3,11},{11,3},{4,12},{12,4},... | collective-permute-start | bytes 811016 | tf_op jit(solution)/shard_map/ppermute | solution.py:244
  99.2 1.2 collective-permute-done.10.got
  102.0 4.0 %collective-permute-done.11.recv = bf16[128,256]{1,0:T(8,128)(2,1)S(1)} collective-permute-done((bf16[128,256]{1,0:T(8,128)(2,1)S(1)}, bf16[128,256]{1,0:T(8,128)(2,1)S(1)}, u32[]{:S(2)}, u32[]{:S(2)}) %collective-permute-start.11) | collective-permute-done | bytes 65568 | tf_op jit(solution)/shard_map/ppermute | solution.py:244
  106.0 1.2 collective-permute-start.12
  107.7 1.6 collective-permute-done.12.after
  109.3 2.2 %collective-permute-done.13.before = bf16[128,256]{1,0:T(8,128)(2,1)S(1)} collective-permute-done((bf16[128,256]{1,0:T(8,128)(2,1)S(1)}, bf16[128,256]{1,0:T(8,128)(2,1)S(1)}, u32[]{:S(2)}, u32[]{:S(2)}) %collective-permute-start.13) | collective-permute-done | bytes 65568 | tf_op jit(solution)/shard_map/ppermute | solution.py:249
  112.0 2.9 %collective-permute-start.14 = (bf16[128,256]{1,0:T(8,128)(2,1)S(1)}, bf16[128,256]{1,0:T(8,128)(2,1)S(1)}, u32[]{:S(2)}, u32[]{:S(2)}) collective-permute-start(bf16[128,256]{1,0:T(8,128)(2,1)S(1)} %get-tuple-element.68), channel_id=1, source_target_pairs={{0,48},{16,64},{32,80},{48,96},{64,112},{80,0},{96,16},{112,32},{1... | collective-permute-start | bytes 196616 | tf_op jit(solution)/shard_map/ppermute | solution.py:249
  114.9 3.2 %collective-permute-done.15.after = bf16[128,256]{1,0:T(8,128)(2,1)S(1)} collective-permute-done((bf16[128,256]{1,0:T(8,128)(2,1)S(1)}, bf16[128,256]{1,0:T(8,128)(2,1)S(1)}, u32[]{:S(2)}, u32[]{:S(2)}) %collective-permute-start.15) | collective-permute-done | bytes 65568 | tf_op jit(solution)/shard_map/ppermute | solution.py:249
  119.1 15.8 %all_to_all.27.u = bf16[16,136,256]{2,1,0:T(8,128)(2,1)S(1)} all-to-all(bf16[16,136,256]{2,1,0:T(8,128)(2,1)S(1)} %shard_map.86), channel_id=1, replica_groups=mesh['yh'=2,'z'=8,'c'=2,'x'=4,'yl'=2] {'x','yl','yh'}, dimensions={0} | all-to-all | bytes 2228224 | tf_op jit(solution)/shard_map/all_to_all | solution.py:281
  134.9 3.4 %shard_map.87 = (f32[256,256]{1,0:T(8,128)S(1)}, f32[264,256]{1,0:T(8,128)S(1)}, f32[8,128]{1,0:T(8,128)S(1)}) custom-call(s32[3]{0:T(128)S(1)} %pad_add_fusion.s, f32[4]{0:T(128)S(1)} %copy-done.4, bf16[4,256,2048]{2,1,0:T(8,128)(2,1)S(1)} %get-tuple-element.42.v1, bf16[4,256,2048]{2,1,0:T(8,128)(2,1)S(1)} %shard_map.74.v2, ...), custom_call_target="tpu_custom_call" | custom-call | flops 2684354560 | bytes 14233628 | tf_op jit(solution)/shard_map/pallas_call | solution.py:32
  138.4 5.9 %collective-permute-start.16 = (f32[264,256]{1,0:T(8,128)S(1)}, f32[264,256]{1,0:T(8,128)S(1)}, u32[]{:S(2)}, u32[]{:S(2)}) collective-permute-start(f32[264,256]{1,0:T(8,128)S(1)} %get-tuple-element.71), channel_id=1, source_target_pairs={{0,8},{8,0},{1,9},{9,1},{2,10},{10,2},{3,11},{11,3},{4,12},{12,4},... | collective-permute-start | bytes 811016 | tf_op jit(solution)/shard_map/ppermute | solution.py:244
  146.2 15.1 %all_to_all.28.pieces = bf16[16,16,256]{2,1,0:T(8,128)(2,1)S(1)} all-to-all(bf16[16,16,256]{2,1,0:T(8,128)(2,1)S(1)} %shard_map.88), channel_id=1, replica_groups=mesh['yh'=2,'z'=8,'c'=2,'x'=4,'yl'=2] {'yh','z'}, dimensions={0} | all-to-all | bytes 262144 | tf_op jit(solution)/shard_map/all_to_all | solution.py:341
  161.4 12.7 %all_to_all.29 = bf16[16,16,256]{2,1,0:T(8,128)(2,1)S(1)} all-to-all(bf16[16,16,256]{2,1,0:T(8,128)(2,1)S(1)} %shard_map.89), channel_id=1, replica_groups=mesh['yh'=2,'z'=8,'c'=2,'x'=4,'yl'=2] {'yh','z'}, dimensions={0} | all-to-all | bytes 262144 | tf_op jit(solution)/shard_map/all_to_all | solution.py:345
  174.1 2.5 %collective-permute-start.17 = (bf16[256,256]{1,0:T(8,128)(2,1)S(1)}, bf16[256,256]{1,0:T(8,128)(2,1)S(1)}, u32[]{:S(2)}, u32[]{:S(2)}) collective-permute-start(bf16[256,256]{1,0:T(8,128)(2,1)S(1)} %bitcast.6), channel_id=1, source_target_pairs={{0,8},{8,0},{1,9},{9,1},{2,10},{10,2},{3,11},{11,3},{4,12},{12,4},... | collective-permute-start | bytes 393224 | tf_op jit(solution)/shard_map/ppermute | solution.py:244
  177.6 1.5 shard_map.90
  (41 shorter events, 10.0 us)
Async XLA Ops:
  0.0 30.7 %collective-permute-start = (bf16[4,256,2048]{2,1,0:T(8,128)(2,1)}, bf16[4,256,2048]{2,1,0:T(8,128)(2,1)}, u32[]{:S(2)}, u32[]{:S(2)}) collective-permute-start(bf16[4,256,2048]{2,1,0:T(8,128)(2,1)} %v_h.1), channel_id=1, source_target_pairs={{0,8},{8,0},{1,9},{9,1},{2,10},{10,2},{3,11},{11,3},{4,12},{12,4},... | collective-permute-start | bytes 12582920 | tf_op jit(solution)/shard_map/ppermute | solution.py:244
  3.2 30.4 %collective-permute-start.1 = (bf16[4,512,512]{2,1,0:T(8,128)(2,1)}, bf16[4,512,512]{2,1,0:T(8,128)(2,1)S(1)}, u32[]{:S(2)}, u32[]{:S(2)}) collective-permute-start(bf16[4,512,512]{2,1,0:T(8,128)(2,1)} %o1.5), channel_id=1, source_target_pairs={{0,8},{8,0},{1,9},{9,1},{2,10},{10,2},{3,11},{11,3},{4,12},{12,4},... | collective-permute-start | bytes 6291464 | tf_op jit(solution)/shard_map/ppermute | solution.py:244
  6.6 22.2 %copy-start = (bf16[4,256,512]{2,1,0:T(8,128)(2,1)S(1)}, bf16[4,256,512]{2,1,0:T(8,128)(2,1)}, u32[]{:S(2)}) copy-start(bf16[4,256,512]{2,1,0:T(8,128)(2,1)} %ov.4) | copy-start | bytes 3145732
  28.8 8.4 %collective-permute-start.3 = (bf16[4,256,512]{2,1,0:T(8,128)(2,1)S(1)}, bf16[4,256,512]{2,1,0:T(8,128)(2,1)S(1)}, u32[]{:S(2)}, u32[]{:S(2)}) collective-permute-start(bf16[4,256,512]{2,1,0:T(8,128)(2,1)S(1)} %copy-done), channel_id=1, source_target_pairs={{0,8},{8,0},{1,9},{9,1},{2,10},{10,2},{3,11},{11,3},{4,12},{12,4},... | collective-permute-start | bytes 3145736 | tf_op jit(solution)/shard_map/ppermute | solution.py:244
  30.7 2.9 %copy-start.1 = (bf16[4,512,512]{2,1,0:T(8,128)(2,1)S(1)}, bf16[4,512,512]{2,1,0:T(8,128)(2,1)}, u32[]{:S(2)}) copy-start(bf16[4,512,512]{2,1,0:T(8,128)(2,1)} %o1.5) | copy-start | bytes 6291460
  30.7 2.9 %copy-start.4 = (f32[4]{0:T(128)S(1)}, f32[4]{0:T(128)}, u32[]{:S(2)}) copy-start(f32[4]{0:T(128)} %fit.2) | copy-start | bytes 52
  37.1 1.6 collective-permute-start.2
  39.6 33.4 %collective-permute-start.9 = (bf16[8,128,256]{2,1,0:T(8,128)(2,1)S(1)}, bf16[8,128,256]{2,1,0:T(8,128)(2,1)S(1)}, u32[]{:S(2)}, u32[]{:S(2)}) collective-permute-start(bf16[8,128,256]{2,1,0:T(8,128)(2,1)S(1)} %get-tuple-element.58), channel_id=1, source_target_pairs={{0,128},{128,0},{1,129},{129,1},{2,130},{130,2},{3,131},{131,3},{4... | collective-permute-start | bytes 1572872 | tf_op jit(solution)/shard_map/ppermute | solution.py:244
  40.3 15.6 %collective-permute-start.4 = (bf16[128,256]{1,0:T(8,128)(2,1)S(1)}, bf16[128,256]{1,0:T(8,128)(2,1)S(1)}, u32[]{:S(2)}, u32[]{:S(2)}) collective-permute-start(bf16[128,256]{1,0:T(8,128)(2,1)S(1)} %get-tuple-element.49), channel_id=1, source_target_pairs={{0,128},{128,0},{1,129},{129,1},{2,130},{130,2},{3,131},{131,3},{4... | collective-permute-start | bytes 196616 | tf_op jit(solution)/shard_map/ppermute | solution.py:244
  55.9 7.0 %collective-permute-start.5 = (bf16[128,256]{1,0:T(8,128)(2,1)S(1)}, bf16[128,256]{1,0:T(8,128)(2,1)S(1)}, u32[]{:S(2)}, u32[]{:S(2)}) collective-permute-start(bf16[128,256]{1,0:T(8,128)(2,1)S(1)} %get-tuple-element.51), channel_id=1, source_target_pairs={{0,112},{16,0},{32,16},{48,32},{64,48},{80,64},{96,80},{112,96},{1... | collective-permute-start | bytes 196616 | tf_op jit(solution)/shard_map/ppermute | solution.py:249
  61.6 4.3 %collective-permute-start.6 = (bf16[128,256]{1,0:T(8,128)(2,1)S(1)}, bf16[128,256]{1,0:T(8,128)(2,1)S(1)}, u32[]{:S(2)}, u32[]{:S(2)}) collective-permute-start(bf16[128,256]{1,0:T(8,128)(2,1)S(1)} %get-tuple-element.51), channel_id=1, source_target_pairs={{0,16},{16,32},{32,48},{48,64},{64,80},{80,96},{96,112},{112,0},{1... | collective-permute-start | bytes 196616 | tf_op jit(solution)/shard_map/ppermute | solution.py:249
  65.9 5.0 %collective-permute-start.8 = (bf16[128,256]{1,0:T(8,128)(2,1)S(1)}, bf16[128,256]{1,0:T(8,128)(2,1)S(1)}, u32[]{:S(2)}, u32[]{:S(2)}) collective-permute-start(bf16[128,256]{1,0:T(8,128)(2,1)S(1)} %get-tuple-element.55), channel_id=1, source_target_pairs={{0,80},{16,96},{32,112},{48,0},{64,16},{80,32},{96,48},{112,64},{1... | collective-permute-start | bytes 196616 | tf_op jit(solution)/shard_map/ppermute | solution.py:249
  66.4 6.6 %collective-permute-start.7 = (bf16[128,256]{1,0:T(8,128)(2,1)S(1)}, bf16[128,256]{1,0:T(8,128)(2,1)S(1)}, u32[]{:S(2)}, u32[]{:S(2)}) collective-permute-start(bf16[128,256]{1,0:T(8,128)(2,1)S(1)} %get-tuple-element.54), channel_id=1, source_target_pairs={{0,48},{16,64},{32,80},{48,96},{64,112},{80,0},{96,16},{112,32},{1... | collective-permute-start | bytes 196616 | tf_op jit(solution)/shard_map/ppermute | solution.py:249
  93.6 6.8 %collective-permute-start.10 = (f32[264,256]{1,0:T(8,128)S(1)}, f32[264,256]{1,0:T(8,128)S(1)}, u32[]{:S(2)}, u32[]{:S(2)}) collective-permute-start(f32[264,256]{1,0:T(8,128)S(1)} %get-tuple-element.60), channel_id=1, source_target_pairs={{0,8},{8,0},{1,9},{9,1},{2,10},{10,2},{3,11},{11,3},{4,12},{12,4},... | collective-permute-start | bytes 811016 | tf_op jit(solution)/shard_map/ppermute | solution.py:244
  101.2 4.7 %collective-permute-start.11 = (bf16[128,256]{1,0:T(8,128)(2,1)S(1)}, bf16[128,256]{1,0:T(8,128)(2,1)S(1)}, u32[]{:S(2)}, u32[]{:S(2)}) collective-permute-start(bf16[128,256]{1,0:T(8,128)(2,1)S(1)} %get-tuple-element.63), channel_id=1, source_target_pairs={{0,128},{128,0},{1,129},{129,1},{2,130},{130,2},{3,131},{131,3},{4... | collective-permute-start | bytes 196616 | tf_op jit(solution)/shard_map/ppermute | solution.py:244
  106.0 3.3 %collective-permute-start.12 = (bf16[128,256]{1,0:T(8,128)(2,1)S(1)}, bf16[128,256]{1,0:T(8,128)(2,1)S(1)}, u32[]{:S(2)}, u32[]{:S(2)}) collective-permute-start(bf16[128,256]{1,0:T(8,128)(2,1)S(1)} %get-tuple-element.65), channel_id=1, source_target_pairs={{0,112},{16,0},{32,16},{48,32},{64,48},{80,64},{96,80},{112,96},{1... | collective-permute-start | bytes 196616 | tf_op jit(solution)/shard_map/ppermute | solution.py:249
  107.2 4.3 %collective-permute-start.13 = (bf16[128,256]{1,0:T(8,128)(2,1)S(1)}, bf16[128,256]{1,0:T(8,128)(2,1)S(1)}, u32[]{:S(2)}, u32[]{:S(2)}) collective-permute-start(bf16[128,256]{1,0:T(8,128)(2,1)S(1)} %get-tuple-element.65), channel_id=1, source_target_pairs={{0,16},{16,32},{32,48},{48,64},{64,80},{80,96},{96,112},{112,0},{1... | collective-permute-start | bytes 196616 | tf_op jit(solution)/shard_map/ppermute | solution.py:249
  111.5 6.5 %collective-permute-start.15 = (bf16[128,256]{1,0:T(8,128)(2,1)S(1)}, bf16[128,256]{1,0:T(8,128)(2,1)S(1)}, u32[]{:S(2)}, u32[]{:S(2)}) collective-permute-start(bf16[128,256]{1,0:T(8,128)(2,1)S(1)} %get-tuple-element.69), channel_id=1, source_target_pairs={{0,80},{16,96},{32,112},{48,0},{64,16},{80,32},{96,48},{112,64},{1... | collective-permute-start | bytes 196616 | tf_op jit(solution)/shard_map/ppermute | solution.py:249
  112.0 6.3 %collective-permute-start.14 = (bf16[128,256]{1,0:T(8,128)(2,1)S(1)}, bf16[128,256]{1,0:T(8,128)(2,1)S(1)}, u32[]{:S(2)}, u32[]{:S(2)}) collective-permute-start(bf16[128,256]{1,0:T(8,128)(2,1)S(1)} %get-tuple-element.68), channel_id=1, source_target_pairs={{0,48},{16,64},{32,80},{48,96},{64,112},{80,0},{96,16},{112,32},{1... | collective-permute-start | bytes 196616 | tf_op jit(solution)/shard_map/ppermute | solution.py:249
  138.3 39.3 %copy-start.2 = (f32[256,512]{1,0:T(8,128)S(1)}, f32[256,512]{1,0:T(8,128)}, u32[]{:S(2)}) copy-start(f32[256,512]{1,0:T(8,128)} %rhs.1) | copy-start | bytes 1572868
  138.3 39.2 %copy-start.3 = (f32[512]{0:T(512)S(1)}, f32[512]{0:T(512)}, u32[]{:S(2)}) copy-start(f32[512]{0:T(512)} %param.13) | copy-start | bytes 6148
  138.4 39.2 %copy-start.5 = (f32[256]{0:T(256)S(1)}, f32[256]{0:T(256)}, u32[]{:S(2)}) copy-start(f32[256]{0:T(256)} %param.12) | copy-start | bytes 3076
  138.4 7.1 %collective-permute-start.16 = (f32[264,256]{1,0:T(8,128)S(1)}, f32[264,256]{1,0:T(8,128)S(1)}, u32[]{:S(2)}, u32[]{:S(2)}) collective-permute-start(f32[264,256]{1,0:T(8,128)S(1)} %get-tuple-element.71), channel_id=1, source_target_pairs={{0,8},{8,0},{1,9},{9,1},{2,10},{10,2},{3,11},{11,3},{4,12},{12,4},... | collective-permute-start | bytes 811016 | tf_op jit(solution)/shard_map/ppermute | solution.py:244
  174.1 3.5 %collective-permute-start.17 = (bf16[256,256]{1,0:T(8,128)(2,1)S(1)}, bf16[256,256]{1,0:T(8,128)(2,1)S(1)}, u32[]{:S(2)}, u32[]{:S(2)}) collective-permute-start(bf16[256,256]{1,0:T(8,128)(2,1)S(1)} %bitcast.6), channel_id=1, source_target_pairs={{0,8},{8,0},{1,9},{9,1},{2,10},{10,2},{3,11},{11,3},{4,12},{12,4},... | collective-permute-start | bytes 393224 | tf_op jit(solution)/shard_map/ppermute | solution.py:244
